TPU v7x, 32 devices: a whole 2x2x4 slice. The times are simulated.
32 devices in a mesh: pole: 4 (over x, core), row: 4 (over z), col: 2 (over y).
Axes of the slice: x: 2, y: 2, z: 4, core: 2. Of those that a mesh axis runs over, the one named last changes fastest.
Arguments:
- green: bfloat16 [4, 4096, 4096], P('pole', 'row', 'col'), may hold values from -6 to 6
- factor: bfloat16 [4, 4096, 1024], P('pole', 'row', 'col'), may hold values from -0.09375 to 0.09375
- diag_inverse: bfloat16 [4, 512, 1024], P('pole', 'row', 'col'), may hold values from -6 to 6
- pole_weight: float32 [4], P('pole'), may hold values from 0.25 to 1
- pattern: int32 [8, 2], replicated, may hold values 0 or 1
Outputs:
- off_density: float32 [4096, 1024], P(('row', 'pole'), 'col')
- diag_density: float32 [512, 1024], P(('pole', 'row'), 'col')
All inputs are finite; a program needn't handle non-finite values.
Results may differ from a plain program's by a relative error of at most 0.005.
Values may be sent and summed in bfloat16 or wider, within the bound.
No kernel may reach another device: no remote copies, remote signals or barrier semaphores. Data moves between devices by JAX's collectives and lax.ppermute only.
A program may use at most 64 MiB of HBM per device.

v0:
```python
import jax
import jax.numpy as jnp
from jax import lax
from jax.sharding import PartitionSpec as P

BLOCK = 512
ANC = 8


def body(green, factor, diag_inverse, pole_weight, pattern):
    poles_here = green.shape[0]
    local_rows = factor.shape[1]
    local_cols = factor.shape[2]
    level_count = pattern.shape[1]
    row_at = lax.axis_index("row")
    col_at = lax.axis_index("col")
    row_ids = (row_at * local_rows + jnp.arange(local_rows, dtype=jnp.int32)) // BLOCK
    col_ids = (col_at * local_cols + jnp.arange(local_cols, dtype=jnp.int32)) // BLOCK
    row_onehot = (row_ids[:, None] == jnp.arange(ANC, dtype=jnp.int32)[None, :]).astype(jnp.float32)
    col_onehot = (col_ids[:, None] == jnp.arange(level_count, dtype=jnp.int32)[None, :]).astype(
        jnp.float32
    )
    pattern_f = pattern.astype(jnp.float32)
    keep_mask = jnp.dot(jnp.dot(row_onehot, pattern_f), col_onehot.T)
    masked = factor * keep_mask.astype(jnp.bfloat16)[None]
    whole_rows = lax.all_gather(green, "col", axis=2, tiled=True)
    product = jnp.einsum(
        "pij,pjk->pik",
        whole_rows,
        lax.all_gather(masked, "row", axis=1, tiled=True),
        preferred_element_type=jnp.float32,
    )
    update = (product * keep_mask[None]).astype(jnp.bfloat16)
    weights = pole_weight[:, None, None]
    off_term = -jnp.sum(weights * update.astype(jnp.float32), axis=0)
    level_here = local_cols // BLOCK
    factor_split = masked.reshape(poles_here, local_rows, level_here, BLOCK)
    update_split = update.reshape(poles_here, local_rows, level_here, BLOCK)
    cross_term = jnp.einsum(
        "prka,prkb->pakb", factor_split, update_split, preferred_element_type=jnp.float32
    )
    cross_term = cross_term.reshape(poles_here, BLOCK, local_cols)
    diag_term = -jnp.sum(weights * cross_term, axis=0)
    dinv_count = diag_inverse.shape[1]
    dinv_rows = jnp.sum(weights * diag_inverse.astype(jnp.float32), axis=0)
    current = lax.dynamic_slice_in_dim(diag_term, row_at * dinv_count, dinv_count, 0)
    diag_term = lax.dynamic_update_slice_in_dim(
        diag_term, current + dinv_rows, row_at * dinv_count, 0
    )
    off_density, pole_part = (
        lax.psum_scatter(off_term, "pole", scatter_dimension=0, tiled=True),
        lax.psum_scatter(diag_term, "pole", scatter_dimension=0, tiled=True),
    )
    diag_density = lax.psum_scatter(pole_part, "row", scatter_dimension=0, tiled=True)
    return (off_density, diag_density)


def solution(mesh):
    in_specs = (
        P("pole", "row", "col"),
        P("pole", "row", "col"),
        P("pole", "row", "col"),
        P("pole"),
        P(),
    )
    out_specs = (P(("row", "pole"), "col"), P(("pole", "row"), "col"))
    return jax.shard_map(body, mesh=mesh, in_specs=in_specs, out_specs=out_specs, check_vma=False)
```

profile of v0, /device:TPU:0, one launch (start us, length us, event | category | flops | bytes accessed | tf_op | source)
XLA Modules:
  0.0 296.8 jit_solution(12370110417123104437)
XLA Ops:
  7.2 0.0 all-gather.3.cloned.1.call-start
  7.3 2.9 bitcast_multiply_fusion.1
  10.1 0.0 all-gather.3.cloned.1.call-update
  10.2 0.0 copy-start.2
  10.2 0.0 all-gather.5.cloned.1.call-start
  10.2 0.7 all-gather.5.cloned.1.call-update
  10.9 0.0 reduce-scatter.8.cloned.1.call-start
  11.6 0.0 copy-done.2
  11.6 0.1 copy.11
  11.8 82.0 %all-gather.3.cloned.1.call-done = bf16[1,4096,512]{2,1,0:T(8,128)(2,1)} async-done(((bf16[1,1024,512]{2,1,0:T(8,128)(2,1)}), bf16[1,4096,512]{2,1,0:T(8,128)(2,1)}) %all-gather.3.cloned.1.call-update) | async-done | bytes 4194320 | tf_op jit(solution)/shard_map/all_gather | solution.py:30
  93.8 104.0 %all-gather.5.cloned.1.call-done = bf16[1,1024,4096]{2,1,0:T(8,128)(2,1)} async-done(((bf16[1,1024,2048]{2,1,0:T(8,128)(2,1)}), bf16[1,1024,4096]{2,1,0:T(8,128)(2,1)}) %all-gather.5.cloned.1.call-update) | async-done | bytes 8388624 | tf_op jit(solution)/shard_map/all_gather | solution.py:26
  197.8 0.0 copy-start
  197.8 10.5 %multiply_negate_fusion = (f32[1024,512]{1,0:T(8,128)}, bf16[1024,512]{1,0:T(8,128)(2,1)S(1)}) fusion(f32[]{:T(128)} %bitcast.41, f32[1024,512]{1,0:T(8,128)S(1)} %get-tuple-element.7, bf16[1,4096,512]{2,1,0:T(8,128)(2,1)} %all-gather.3.cloned.1.call-done, bf16[1,1024,4096]{2,1,0:T(8,128)(2,1)} %all-gather.5.cloned.1.call-done), kind=kOutput, calls=%fused_computation.5 | convolution fusion | flops 4297588736 | bytes 17825796 | tf_op jit(solution)/shard_map/pij,pjk->pik/dot_general | solution.py:27
  208.3 0.0 copy-done
  208.3 0.7 fusion.8
  209.0 0.1 copy.16
  209.2 0.0 copy-start.1
  209.2 1.0 copy-done.1
  210.2 0.0 reduce-scatter.8.cloned.1.call-update
  210.2 0.0 reduce-scatter.10.cloned.1.call-start
  210.2 24.9 %reduce-scatter.8.cloned.1.call-done = f32[128,512]{0,1:T(8,128)} async-done(((f32[512,512]{0,1:T(8,128)}), f32[128,512]{0,1:T(8,128)}) %reduce-scatter.8.cloned.1.call-update) | async-done | bytes 262160 | tf_op jit(solution)/shard_map/reduce_scatter | solution.py:52
  235.2 1.8 copy.14
  236.9 0.0 reduce-scatter.10.cloned.1.call-update
  237.0 0.0 reduce-scatter.6.cloned.1.call-start
  237.0 0.5 reduce-scatter.6.cloned.1.call-update
  237.6 20.3 %reduce-scatter.10.cloned.1.call-done = f32[32,512]{1,0:T(8,128)} async-done(((f32[128,512]{1,0:T(8,128)}), f32[32,512]{1,0:T(8,128)}) %reduce-scatter.10.cloned.1.call-update) | async-done | bytes 65552
  257.9 32.4 %reduce-scatter.6.cloned.1.call-done = f32[256,512]{1,0:T(8,128)} async-done(((f32[1024,512]{1,0:T(8,128)}), f32[256,512]{1,0:T(8,128)}) %reduce-scatter.6.cloned.1.call-update) | async-done | bytes 524304 | tf_op jit(solution)/shard_map/reduce_scatter | solution.py:51
  (3 shorter events, 0.1 us)
Async XLA Ops:
  7.2 86.6 %all-gather.3.cloned.1.call-start = ((), (), s32[]{:S(2)}) async-start(), calls=%async_computation.3 | async-start | bytes 5242880 | tf_op jit(solution)/shard_map/all_gather | solution.py:30
  10.2 1.5 copy-start.2
  10.2 187.7 %all-gather.5.cloned.1.call-start = ((), (), s32[]{:S(2)}) async-start(), calls=%async_computation.4 | async-start | bytes 12582912 | tf_op jit(solution)/shard_map/all_gather | solution.py:26
  10.9 224.2 %reduce-scatter.8.cloned.1.call-start = ((), (), s32[]{:S(2)}) async-start(), calls=%async_computation.6 | async-start | bytes 1310720 | tf_op jit(solution)/shard_map/reduce_scatter | solution.py:52
  197.8 10.5 %copy-start = (bf16[1,1024,512]{2,1,0:T(8,128)(2,1)S(1)}, bf16[1,1024,512]{2,1,0:T(8,128)(2,1)}, u32[]{:S(2)}) copy-start(bf16[1,1024,512]{2,1,0:T(8,128)(2,1)} %get-tuple-element.6) | copy-start | bytes 3145732
  209.2 1.0 copy-start.1
  210.2 47.7 %reduce-scatter.10.cloned.1.call-start = ((), (), s32[]{:S(2)}) async-start(), calls=%async_computation.7 | async-start | bytes 327680
  237.0 53.3 %reduce-scatter.6.cloned.1.call-start = ((), (), s32[]{:S(2)}) async-start(), calls=%async_computation.5 | async-start | bytes 2621440 | tf_op jit(solution)/shard_map/reduce_scatter | solution.py:51
Sparse Core Ops, SparseCore 0:
  10.3 83.4 all-gather.2
  95.3 102.4 all-gather.4
  210.3 24.8 reduce-scatter.7
  237.8 19.9 reduce-scatter.9
  260.8 29.4 reduce-scatter.5
where the time goes:
time: 297 us
  waiting for transfers between devices  265 us (89%)
  between operations  14.5 us (5%)
  matrix products  14.1 us (5%)
    all_gather x1, waiting for transfers between devices, body(): whole_rows = lax.all_gather(green, 'col', axis=2, tiled=True)  104 us
    all_gather x1, waiting for transfers between devices, body(): lax.all_gather(masked, 'row', axis=1, tiled=True)  82 us
    reduce_scatter x1, waiting for transfers between devices, body(): lax.psum_scatter(off_term, 'pole', scatter_dimension=0, tiled=True)  32.4 us
    reduce_scatter x1, waiting for transfers between devices, body(): lax.psum_scatter(diag_term, 'pole', scatter_dimension=0, tiled=True)  24.9 us
    unnamed x6, waiting for transfers between devices  21.6 us
    dot_general x1, matrix products, body(): jnp.einsum('pij,pjk->pik', whole_rows, lax.all_gather(masked, 'row', axis...  10.5 us
  transfers between devices with their start and end apart: 5, of which 5 were waited for; matrix products, arithmetic and copies ran while one was open for 0% of the time, Pallas kernels for 0%

commit v1 on v0

v1 whole, which is shorter than its diff:
```python
import functools

import jax
import jax.numpy as jnp
from jax import lax
from jax.experimental import pallas as pl
from jax.experimental.pallas import tpu as pltpu
from jax.sharding import PartitionSpec as P


VMEM = pl.BlockSpec(memory_space=pltpu.VMEM)
SMEM = pl.BlockSpec(memory_space=pltpu.SMEM)
ANY = pl.BlockSpec(memory_space=pl.ANY)
F32 = jnp.float32
BF16 = jnp.bfloat16


class Sizes:
    def __init__(self, mesh, green, factor, diag_inverse, pattern):
        self.poles, self.rows, self.cols = (mesh.shape[a] for a in ("pole", "row", "col"))
        self.local_rows, self.k_local = green.shape[1], green.shape[2]
        self.width = factor.shape[2]
        self.anc, supers = pattern.shape
        self.block = self.local_rows * self.rows // self.anc
        self.per_row = self.local_rows // self.block
        self.half = self.k_local // self.block
        self.level = supers // self.cols
        self.count = diag_inverse.shape[1]
        self.cores = 2 if self.poles % 2 == 0 else 1
        self.outer = self.poles // self.cores


def swap_sum(part, axis, size, group, stride, held_as):
    at = lax.axis_index(axis)
    digit = (at // stride) % group
    total = lax.dynamic_index_in_dim(part, digit, 0, keepdims=False)
    for step in range(1, group):
        perm = []
        for i in range(size):
            d = (i // stride) % group
            perm.append((i, i + ((d + step) % group - d) * stride))
        to = (digit + step) % group
        send = lax.dynamic_index_in_dim(part, to, 0, keepdims=False).astype(held_as)
        total = total + lax.ppermute(send, axis, perm).astype(F32)
    return total


def generic(sz, green, factor, diag_inverse, pole_weight, pattern):
    block, per_row, cols = sz.block, sz.per_row, sz.width
    row_at = lax.axis_index("row")
    col_at = lax.axis_index("col")
    pattern_f = pattern.astype(F32)
    here = lax.dynamic_slice(pattern_f, (0, col_at * sz.level), (sz.anc, sz.level))
    keep = jnp.repeat(here, block, axis=1)
    own_keep = lax.dynamic_slice_in_dim(keep, row_at * per_row, per_row, 0)
    weight = pole_weight[0]
    gl = green[0]
    fac = factor[0].reshape(per_row, block, cols)
    got = {}
    for shift in range(1, sz.cols):
        perm = [(i, (i + shift) % sz.cols) for i in range(sz.cols)]
        for j in range(sz.half):
            got[shift, j] = lax.ppermute(gl[:, j * block:(j + 1) * block], "col", perm)
    right = [(i, i + 1) for i in range(sz.rows - 1)]
    left = [(i + 1, i) for i in range(sz.rows - 1)]
    blocks = {(0, e): fac[e] for e in range(per_row)}
    from_left, from_right = {}, {}
    for e in range(per_row):
        a = b = fac[e]
        for step in range(1, sz.rows):
            from_left[step, e] = a = lax.ppermute(a, "row", right)
            from_right[step, e] = b = lax.ppermute(b, "row", left)
    for step in range(1, sz.rows):
        for e in range(per_row):
            blocks[step, e] = jnp.where(row_at >= step, from_left[step, e], from_right[sz.rows - step, e])
    stacked = jnp.stack([blocks[s, e] for s in range(sz.rows) for e in range(per_row)])

    def factor_of(a):
        at = ((row_at - a // per_row) % sz.rows) * per_row + a % per_row
        kept = lax.dynamic_index_in_dim(keep, a, 0).astype(BF16)
        return lax.dynamic_index_in_dim(stacked, at, 0, keepdims=False) * kept

    product = jnp.zeros((sz.local_rows, cols), F32)
    for shift in range(sz.cols):
        for j in range(sz.half):
            src = (col_at - shift) % sz.cols
            g = gl[:, j * block:(j + 1) * block] if shift == 0 else got[shift, j]
            product += jnp.dot(g, factor_of(src * sz.half + j), preferred_element_type=F32)
    product = product.reshape(per_row, block, cols) * own_keep[:, None, :]
    update = product.astype(BF16).reshape(sz.local_rows, sz.level, block)
    masked = (fac * own_keep.astype(BF16)[:, None, :]).reshape(sz.local_rows, sz.level, block)
    cross = jnp.einsum("rka,rkb->akb", masked, update, preferred_element_type=F32).reshape(block, cols)
    diag = -weight * cross
    mine = lax.dynamic_slice_in_dim(diag, row_at * sz.count, sz.count, 0)
    mine = mine + weight * diag_inverse[0].astype(F32)
    diag = lax.dynamic_update_slice_in_dim(diag, mine, row_at * sz.count, 0)
    off = -weight * product.reshape(sz.local_rows, cols)
    res = []
    for x in (diag, off):
        r = x.shape[0] // sz.poles
        x = x.reshape(sz.outer, sz.cores, r, cols).transpose(1, 0, 2, 3)
        x = swap_sum(x, "pole", sz.poles, sz.cores, 1, BF16)
        res.append(swap_sum(x, "pole", sz.poles, sz.outer, sz.cores, BF16))
    diag, off = res
    return off, swap_sum(diag.reshape(sz.rows, -1, cols), "row", sz.rows, sz.rows, 1, BF16)


def swap_ranks(sz, pat, row, to):
    base = (1 - to) * sz.half
    need, dist = [], []
    for j in range(sz.half):
        need.append(pat[base + j, to])
        dist.append(jnp.abs((base + j) // sz.per_row - row))
    rank = []
    for j in range(sz.half):
        n = jnp.int32(0)
        for i in range(sz.half):
            if i != j:
                before = dist[i] <= dist[j] if i < j else dist[i] < dist[j]
                n = n + jnp.where(before, need[i], 0)
        rank.append(n)
    return need, rank


def pick_kernel(sz, slot, parts, pos, pat, green, out, buf, in_sem, out_sem):
    need, rank = swap_ranks(sz, pat, pos[1], 1 - pos[2])
    at = jnp.int32(0)
    for j in range(sz.half):
        at = jnp.where(jnp.logical_and(need[j] > 0, rank[j] == slot), j, at)
    at = pl.multiple_of(at * sz.block, sz.block)
    n = sz.local_rows // parts
    ins, outs = [], []
    for i in range(parts):
        ins.append(pltpu.make_async_copy(green.at[0, pl.ds(i * n, n), pl.ds(at, sz.block)], buf.at[i], in_sem.at[i]))
        outs.append(pltpu.make_async_copy(buf.at[i], out.at[pl.ds(i * n, n)], out_sem.at[i]))
        ins[i].start()
    for i in range(parts):
        ins[i].wait()
        outs[i].start()
    for i in range(parts):
        outs[i].wait()


def pick(sz, slot, pos, pattern, green):
    parts = 4
    return pl.pallas_call(
        functools.partial(pick_kernel, sz, slot, parts),
        out_shape=jax.ShapeDtypeStruct((sz.local_rows, sz.block), BF16),
        in_specs=[SMEM, SMEM, ANY],
        out_specs=ANY,
        scratch_shapes=[
            pltpu.VMEM((parts, sz.local_rows // parts, sz.block), BF16),
            pltpu.SemaphoreType.DMA((parts,)),
            pltpu.SemaphoreType.DMA((parts,)),
        ],
    )(pos, pattern, green)


def product_jobs(sz, pos, pat, ready, before, m_refs, g_local, g_slots, job, bufs, total):
    m_buf, g_buf, m_sem, g_sem = bufs
    row, col = pos[1], pos[2]
    _, rank = swap_ranks(sz, pat, row, col)

    def inside(bound, dist, e, slot):
        if bound is None:
            return jnp.bool_(False)
        d, last_e, s = bound
        near = jnp.logical_or(dist < d, jnp.logical_and(dist == d, e <= last_e))
        return jnp.logical_and(near, slot <= s)

    count = jnp.int32(0)
    for a in range(sz.anc):
        away = a // sz.per_row - row
        dist, e = jnp.abs(away), a % sz.per_row
        local = (a // sz.half) == col
        slot = jnp.where(local, -1, rank[a % sz.half])
        todo = jnp.logical_and(inside(ready, dist, e, slot), jnp.logical_not(inside(before, dist, e, slot)))
        todo = jnp.logical_and(todo, pat[a, col] > 0)

        @pl.when(todo)
        def _(a=a, count=count, slot=slot, away=away):
            job[0, count] = away * sz.per_row + a % sz.per_row
            job[1, count] = slot
            job[2, count] = a % sz.half

        count = count + jnp.where(todo, 1, 0)

    def fetch(n, into):
        for key, ref in m_refs.items():
            @pl.when(job[0, n] == key)
            def _(ref=ref):
                pltpu.make_async_copy(ref, m_buf.at[into], m_sem.at[into]).start()

        @pl.when(job[1, n] < 0)
        def _():
            at = pl.multiple_of(job[2, n] * sz.block, sz.block)
            pltpu.make_async_copy(g_local.at[0, :, pl.ds(at, sz.block)], g_buf.at[into], g_sem.at[into]).start()

        for s, ref in enumerate(g_slots):
            @pl.when(job[1, n] == s)
            def _(ref=ref):
                pltpu.make_async_copy(ref, g_buf.at[into], g_sem.at[into]).start()

    @pl.when(count > 0)
    def _():
        fetch(0, 0)

    def step(n, carry):
        now = lax.rem(n, 2)

        @pl.when(n + 1 < count)
        def _():
            fetch(n + 1, 1 - now)

        pltpu.make_async_copy(m_buf.at[now], m_buf.at[now], m_sem.at[now]).wait()
        pltpu.make_async_copy(g_buf.at[now], g_buf.at[now], g_sem.at[now]).wait()
        total[...] += jnp.dot(g_buf[now], m_buf[now], preferred_element_type=F32)
        return carry

    lax.fori_loop(0, count, step, 0)


def job_scratch(sz):
    return [
        pltpu.SMEM((3, sz.anc), jnp.int32),
        pltpu.VMEM((2, sz.block, sz.width), BF16),
        pltpu.VMEM((2, sz.local_rows, sz.block), BF16),
        pltpu.SemaphoreType.DMA((2,)),
        pltpu.SemaphoreType.DMA((2,)),
    ]


def early_kernel(sz, ready, before, keys, n_slots, first, pos, pat, g_local, *refs):
    refs = list(refs)
    m_refs = {k: refs.pop(0) for k in keys}
    g_slots = [refs.pop(0) for _ in range(n_slots)]
    total_in = None if first else refs.pop(0)
    out = refs.pop(0)
    job, m_buf, g_buf, m_sem, g_sem = refs
    if first:
        out[...] = jnp.zeros_like(out)
    else:
        out[...] = total_in[...]
    product_jobs(sz, pos, pat, ready, before, m_refs, g_local, g_slots, job, (m_buf, g_buf, m_sem, g_sem), out)


def early(sz, ready, before, pos, pattern, green, m, slots, total):
    keys = list(m)
    first = total is None
    args = [pos, pattern, green] + [m[k] for k in keys] + list(slots) + ([] if first else [total])
    return early_call(sz, ready, before, keys, slots, first, args)


def early_call(sz, ready, before, keys, slots, first, args):
    return pl.pallas_call(
        functools.partial(early_kernel, sz, ready, before, keys, len(slots), first),
        out_shape=jax.ShapeDtypeStruct((sz.local_rows, sz.width), F32),
        in_specs=[SMEM, SMEM] + [ANY] * (1 + len(keys) + len(slots)) + ([] if first else [VMEM]),
        out_specs=VMEM,
        scratch_shapes=job_scratch(sz),
        input_output_aliases={} if first else {len(args) - 1: 0},
    )(*args)


def pole_steps(sz):
    return [(dx, dc) for dx in range(sz.outer) for dc in range(sz.cores) if dx or dc]


def pole_perm(sz, step):
    dx, dc = step
    return [(x * sz.cores + c, (x + dx) % sz.outer * sz.cores + (c + dc) % sz.cores)
            for x in range(sz.outer) for c in range(sz.cores)]


def late_kernel(sz, ready, before, keys, n_slots, pos, pat, weight, g_local, *refs):
    refs = list(refs)
    m_refs = {k: refs.pop(0) for k in keys}
    g_slots = [refs.pop(0) for _ in range(n_slots)]
    total_in, factor, dinv = refs.pop(0), refs.pop(0), refs.pop(0)
    diag_out = [refs.pop(0) for _ in range(sz.poles)]
    off_out = [refs.pop(0) for _ in range(sz.poles)]
    total, diag = refs.pop(0), refs.pop(0)
    job, m_buf, g_buf, m_sem, g_sem = refs
    row, col = pos[1], pos[2]
    core, x_at = lax.rem(pos[0], sz.cores), pos[0] // sz.cores
    total[...] = total_in[...]
    product_jobs(sz, pos, pat, ready, before, m_refs, g_local, g_slots, job, (m_buf, g_buf, m_sem, g_sem), total)
    w = weight[0]
    diag[...] = jnp.zeros_like(diag)
    for e in range(sz.per_row):
        at = pl.ds(e * sz.block, sz.block)
        kept = pat[row * sz.per_row + e, col] > 0

        @pl.when(kept)
        def _(at=at):
            update = total[at, :]
            diag[...] -= w * lax.dot_general(
                factor[0, at, :], update.astype(BF16), (((0,), (0,)), ((), ())), preferred_element_type=F32)
            total[at, :] = -w * update

        @pl.when(jnp.logical_not(kept))
        def _(at=at):
            total[at, :] = jnp.zeros((sz.block, sz.width), F32)
    mine = pl.ds(pl.multiple_of(row * sz.count, sz.count), sz.count)
    diag[mine, :] += w * dinv[0].astype(F32)
    for src, keep, sends in ((diag, diag_out[0], diag_out[1:]), (total, off_out[0], off_out[1:])):
        n = src.shape[0] // sz.poles

        def part(x, c):
            return src[pl.ds(pl.multiple_of((x * sz.cores + c) * n, n), n), :]

        keep[...] = part(x_at, core)
        for (dx, dc), send in zip(pole_steps(sz), sends):
            send[...] = part(lax.rem(x_at + dx, sz.outer), lax.rem(core + dc, sz.cores)).astype(BF16)


def late(sz, ready, before, pos, pattern, weight, green, m, slots, total, factor, dinv):
    keys = list(m)
    args = [pos, pattern, weight, green] + [m[k] for k in keys] + list(slots) + [total, factor, dinv]
    shapes = []
    for n in (sz.block, sz.local_rows):
        for i in range(sz.poles):
            shapes.append(jax.ShapeDtypeStruct((n // sz.poles, sz.width), BF16 if i else F32))
    return pl.pallas_call(
        functools.partial(late_kernel, sz, ready, before, keys, len(slots)),
        out_shape=shapes,
        in_specs=[SMEM] * 3 + [ANY] * (1 + len(keys) + len(slots)) + [VMEM] * 3,
        out_specs=[VMEM] * (2 * sz.poles),
        scratch_shapes=[pltpu.VMEM((sz.local_rows, sz.width), F32), pltpu.VMEM((sz.block, sz.width), F32)]
        + job_scratch(sz),
        name="late",
    )(*args)


def fold_kernel(group, n_in, axis_pos, stride, pos, keep, *refs):
    ins, outs = refs[:n_in], refs[n_in:]
    own, sends = outs[0], outs[1:]
    n = own.shape[0]
    me = lax.rem(pos[axis_pos] // stride, group)

    def part(d):
        at = pl.ds(pl.multiple_of(d * n, n), n)
        v = keep[at, :]
        for r in ins:
            v = v + r[at, :].astype(F32)
        return v

    for s, send in enumerate(sends):
        send[...] = part(lax.rem(me + s + 1, group)).astype(BF16)
    own[...] = part(me)


def fold(group, axis_pos, stride, pos, keep, ins):
    n, width = keep.shape[0] // group, keep.shape[1]
    shapes = [jax.ShapeDtypeStruct((n, width), F32)] + [jax.ShapeDtypeStruct((n, width), BF16)] * (group - 1)
    return pl.pallas_call(
        functools.partial(fold_kernel, group, len(ins), axis_pos, stride),
        out_shape=shapes,
        in_specs=[SMEM] + [VMEM] * (1 + len(ins)),
        out_specs=[VMEM] * group,
    )(pos, keep, *ins)


def shifts(size, group, stride):
    perms = []
    for step in range(1, group):
        perm = []
        for i in range(size):
            d = (i // stride) % group
            perm.append((i, i + ((d + step) % group - d) * stride))
        perms.append(perm)
    return perms


def blocked(sz, green, factor, diag_inverse, pole_weight, pattern):
    block, per_row = sz.block, sz.per_row
    pos = jnp.stack([lax.axis_index(a) for a in ("pole", "row", "col")]).astype(jnp.int32)
    fac = [factor[0, e * block:(e + 1) * block] for e in range(per_row)]
    right = [(i, i + 1) for i in range(sz.rows - 1)]
    left = [(i + 1, i) for i in range(sz.rows - 1)]
    swap = [(0, 1), (1, 0)]

    fixed = max(sz.half - 1, 1)
    slots = []
    for s in range(fixed):
        sent = pick(sz, s, pos, pattern, green)
        slots.append(lax.ppermute(sent, "col", swap))

    m = {e: fac[e] for e in range(per_row)}
    for e in range(per_row):
        a = b = fac[e]
        for step in range(1, sz.rows):
            m[-step * per_row + e] = a = lax.ppermute(a, "row", right)
            m[step * per_row + e] = b = lax.ppermute(b, "row", left)

    def upto(dist, last_e):
        return {k: v for k, v in m.items() if abs(k // per_row) < dist or (abs(k // per_row) == dist and k % per_row <= last_e)}

    far = sz.rows - 1
    bounds = [(far - 2, per_row - 1, 0), (far - 1, per_row - 1, fixed - 2), (far, per_row - 2, fixed - 2)]

    def part(i, total):
        dist, last_e, s = bounds[i]
        return early(sz, bounds[i], bounds[i - 1] if i else None, pos, pattern, green,
                     upto(dist, last_e), slots[:s + 1], total)

    total = part(1, part(0, None))
    extra = []
    if sz.half > fixed:
        full = jnp.bool_(False)
        for c in range(sz.cols):
            other = (1 - c) * sz.half
            full = jnp.logical_or(full, jnp.all(pattern[other:other + sz.half, c] > 0))

        def more(g):
            return lax.ppermute(pick(sz, fixed, pos, pattern, g), "col", swap)

        full, total = lax.optimization_barrier((full, total))
        got = lax.cond(full, more, lambda g: jnp.zeros((sz.local_rows, block), BF16), green)
        got, total = lax.optimization_barrier((got, total))
        extra.append(got)
    total = part(2, total)
    out = late(sz, (far, per_row - 1, sz.half), bounds[2], pos, pattern, pole_weight, green, m,
               slots + extra, total, factor, diag_inverse)

    def swapped(keep, *sends):
        ins = []
        for v, step in zip(sends, pole_steps(sz)):
            ins.append(lax.ppermute(v, "pole", pole_perm(sz, step)))
        return keep, ins

    diag, diag_in = swapped(*out[:sz.poles])
    off, off_in = swapped(*out[sz.poles:])
    diag, *sends = fold(sz.rows, 1, 1, pos, diag, diag_in)
    diag_in = []
    for v, p in zip(sends, shifts(sz.rows, sz.rows, 1)):
        diag_in.append(lax.ppermute(v, "row", p))
    for v in off_in:
        off = off + v.astype(F32)
    for v in diag_in:
        diag = diag + v.astype(F32)
    return off, diag


def make_body(mesh):
    def body(green, factor, diag_inverse, pole_weight, pattern):
        sz = Sizes(mesh, green, factor, diag_inverse, pattern)
        fits = sz.cols == 2 and sz.level == 1 and sz.cores == 2 and sz.rows >= 3 and sz.per_row >= 2 and sz.half >= 3
        if not fits:
            return generic(sz, green, factor, diag_inverse, pole_weight, pattern)
        return blocked(sz, green, factor, diag_inverse, pole_weight, pattern)

    return body


def solution(mesh):
    in_specs = (
        P("pole", "row", "col"),
        P("pole", "row", "col"),
        P("pole", "row", "col"),
        P("pole"),
        P(),
    )
    out_specs = (P(("row", "pole"), "col"), P(("pole", "row"), "col"))
    return jax.shard_map(make_body(mesh), mesh=mesh, in_specs=in_specs, out_specs=out_specs, check_vma=False)
```

time: 297 us -> 144 us (0.48)
  waiting for transfers between devices: 265 us -> 50.3 us
  starting transfers between devices: 0.2 us -> 47.1 us
  Pallas kernels: 0 us -> 32.4 us
  matrix products: 14.1 us -> 0 us
  between operations: 14.5 us -> 2.86 us
  other arithmetic: 0.07 us -> 4.26 us
  local copies, waits for them, and re-layouts: 2.95 us -> 6.28 us
    all_gather x2 -> x0, waiting for transfers between devices: 186 us -> none  [the longest x1 104 us: body(): whole_rows = lax.all_gather(green, 'col', axis=2, tiled=True)]
    reduce_scatter x2 -> x0, waiting for transfers between devices: 57.3 us -> none  [the longest x1 32.4 us: body(): lax.psum_scatter(off_term, 'pole', scatter_dimension=0, tiled=True)]
    ppermute x0 -> x24, waiting for transfers between devices: none -> 50.3 us  [the longest x6 26.5 us: blocked(): m[step * per_row + e] = b = lax.ppermute(b, 'row', left)]
    ppermute x0 -> x24, starting transfers between devices: none -> 47.1 us  [the longest x6 28.4 us: blocked(): m[-step * per_row + e] = a = lax.ppermute(a, 'row', right)]
    pallas_call x0 -> x8, Pallas kernels: none -> 32.4 us  [the longest x3 15.6 us: early_call(): pl.pallas_call(functools.partial(early_kernel, sz, ready, before, keys, l...]
    unnamed x6 -> x0, waiting for transfers between devices: 21.6 us -> none
    dot_general x3 -> x0, matrix products: 14.1 us -> none  [the longest x1 10.5 us: body(): jnp.einsum('pij,pjk->pik', whole_rows, lax.all_gather(masked, 'row', axis...]
    add x0 -> x2, other arithmetic: none -> 3.45 us  [the longest x1 1.96 us: blocked(): off = off + v.astype(F32)]
  transfers between devices with their start and end apart: 5 -> 24, of which waited for: 5 -> 13; matrix products, arithmetic and copies ran while one was open for 0% -> 3% of each run, Pallas kernels for 0% -> 17%
where the time goes in v1:
time: 144 us; the launch traced here: 143 us
  waiting for transfers between devices  50.3 us (35%)
  starting transfers between devices  47.1 us (33%)
  Pallas kernels  32.4 us (22%)
  local copies, waits for them, and re-layouts  6.28 us (4%)
  other arithmetic  4.26 us (3%)
  between operations  2.86 us (2%)
    ppermute x6, starting transfers between devices, blocked(): m[-step * per_row + e] = a = lax.ppermute(a, 'row', right)  28.4 us
    ppermute x6, waiting for transfers between devices, blocked(): m[step * per_row + e] = b = lax.ppermute(b, 'row', left)  26.5 us
    ppermute x6, waiting for transfers between devices, swapped(): ins.append(lax.ppermute(v, 'pole', pole_perm(sz, step)))  16.4 us
    pallas_call x3, Pallas kernels, early_call(): pl.pallas_call(functools.partial(early_kernel, sz, ready, before, keys, l...  15.6 us
    pallas_call x3, Pallas kernels, pick(): pl.pallas_call(functools.partial(pick_kernel, sz, slot, parts), out_shape...  8.41 us
    ppermute x6, starting transfers between devices, blocked(): m[step * per_row + e] = b = lax.ppermute(b, 'row', left)  7.73 us
    pallas_call x1, Pallas kernels, late(): pl.pallas_call(functools.partial(late_kernel, sz, ready, before, keys, le...  6.52 us
    ppermute x6, waiting for transfers between devices, blocked(): m[-step * per_row + e] = a = lax.ppermute(a, 'row', right)  4.08 us
  transfers between devices with their start and end apart: 24, of which 13 were waited for; matrix products, arithmetic and copies ran while one was open for 3% of the time, Pallas kernels for 17%

profile of v1, /device:TPU:0, one launch (start us, length us, event | category | flops | bytes accessed | tf_op | source)
XLA Modules:
  0.0 143.2 jit_solution(6628129424546253736)
XLA Ops:
  0.6 1.3 slice_bitcast_fusion
  1.9 5.8 %collective-permute-start.1 = (bf16[512,512]{1,0:T(8,128)(2,1)S(1)}, bf16[512,512]{1,0:T(8,128)(2,1)}, u32[]{:S(2)}, u32[]{:S(2)}) collective-permute-start(bf16[512,512]{1,0:T(8,128)(2,1)S(1)} %get-tuple-element.52.refs_0_), channel_id=1, source_target_pairs={{0,2},{2,4},{4,6},{1,3},{3,5},{5,7},{8,10},{10,12},{12,14},{9,11},... | collective-permute-start | bytes 1572872 | tf_op jit(solution)/shard_map/ppermute | solution.py:393
  7.8 0.7 copy.16.pat
  8.5 2.8 %shard_map.68 = bf16[1024,512]{1,0:T(8,128)(2,1)} custom-call(s32[3]{0:T(128)S(1)} %pad_add_fusion.pos, s32[8,2]{1,0:T(8,128)} %copy.16.pat, bf16[1,1024,2048]{2,1,0:T(8,128)(2,1)} %g_local.7), custom_call_target="tpu_custom_call" | custom-call | tf_op jit(solution)/shard_map/pallas_call | solution.py:146
  11.3 1.6 %collective-permute-start.13 = (bf16[1024,512]{1,0:T(8,128)(2,1)}, bf16[1024,512]{1,0:T(8,128)(2,1)S(1)}, u32[]{:S(2)}, u32[]{:S(2)}) collective-permute-start(bf16[1024,512]{1,0:T(8,128)(2,1)} %shard_map.68), channel_id=1, source_target_pairs={{0,1},{1,0},{2,3},{3,2},{4,5},{5,4},{6,7},{7,6},{8,9},{9,8},{10,11... | collective-permute-start | bytes 3145736 | tf_op jit(solution)/shard_map/ppermute | solution.py:387
  12.9 2.8 %shard_map.69 = bf16[1024,512]{1,0:T(8,128)(2,1)} custom-call(s32[3]{0:T(128)S(1)} %pad_add_fusion.pos, s32[8,2]{1,0:T(8,128)} %copy.16.pat, bf16[1,1024,2048]{2,1,0:T(8,128)(2,1)} %g_local.7), custom_call_target="tpu_custom_call" | custom-call | tf_op jit(solution)/shard_map/pallas_call | solution.py:146
  15.7 0.6 collective-permute-start.14
  16.3 1.3 collective-permute-start.8
  17.6 1.3 collective-permute-start.2
  18.9 6.0 %collective-permute-start.7 = (bf16[512,512]{1,0:T(8,128)(2,1)S(1)}, bf16[512,512]{1,0:T(8,128)(2,1)}, u32[]{:S(2)}, u32[]{:S(2)}) collective-permute-start(bf16[512,512]{1,0:T(8,128)(2,1)S(1)} %get-tuple-element.51.refs_1_), channel_id=1, source_target_pairs={{0,2},{2,4},{4,6},{1,3},{3,5},{5,7},{8,10},{10,12},{12,14},{9,11},... | collective-permute-start | bytes 1572872 | tf_op jit(solution)/shard_map/ppermute | solution.py:393
  24.9 8.2 %collective-permute-done.8.refs_5_.refs_7_.refs_9_ = bf16[512,512]{1,0:T(8,128)(2,1)} collective-permute-done((bf16[512,512]{1,0:T(8,128)(2,1)S(1)}, bf16[512,512]{1,0:T(8,128)(2,1)}, u32[]{:S(2)}, u32[]{:S(2)}) %collective-permute-start.8) | collective-permute-done | bytes 524320 | tf_op jit(solution)/shard_map/ppermute | solution.py:394
  33.0 1.3 collective-permute-start.10
  34.3 9.9 %collective-permute-done.2.refs_3_ = bf16[512,512]{1,0:T(8,128)(2,1)} collective-permute-done((bf16[512,512]{1,0:T(8,128)(2,1)S(1)}, bf16[512,512]{1,0:T(8,128)(2,1)}, u32[]{:S(2)}, u32[]{:S(2)}) %collective-permute-start.2) | collective-permute-done | bytes 524320 | tf_op jit(solution)/shard_map/ppermute | solution.py:394
  44.3 2.7 %collective-permute-start.3 = (bf16[512,512]{1,0:T(8,128)(2,1)}, bf16[512,512]{1,0:T(8,128)(2,1)S(1)}, u32[]{:S(2)}, u32[]{:S(2)}) collective-permute-start(bf16[512,512]{1,0:T(8,128)(2,1)} %collective-permute-done.1.refs_2_), channel_id=1, source_target_pairs={{0,2},{2,4},{4,6},{1,3},{3,5},{5,7},{8,10},{10,12},{12,14},{9,11},... | collective-permute-start | bytes 1572872 | tf_op jit(solution)/shard_map/ppermute | solution.py:393
  47.0 1.3 collective-permute-start.4
  48.3 5.3 %collective-permute-start.9 = (bf16[512,512]{1,0:T(8,128)(2,1)}, bf16[512,512]{1,0:T(8,128)(2,1)}, u32[]{:S(2)}, u32[]{:S(2)}) collective-permute-start(bf16[512,512]{1,0:T(8,128)(2,1)} %collective-permute-done.7.refs_4_.refs_6_.refs_8_), channel_id=1, source_target_pairs={{0,2},{2,4},{4,6},{1,3},{3,5},{5,7},{8,10},{10,12},{12,14},{9,11},... | collective-permute-start | bytes 1572872 | tf_op jit(solution)/shard_map/ppermute | solution.py:393
  53.6 2.8 %shard_map.70 = bf16[1024,512]{1,0:T(8,128)(2,1)} custom-call(s32[3]{0:T(128)S(1)} %pad_add_fusion.pos, s32[8,2]{1,0:T(8,128)} %copy.16.pat, bf16[1,1024,2048]{2,1,0:T(8,128)(2,1)} %g_local.7), custom_call_target="tpu_custom_call" | custom-call | tf_op jit(solution)/shard_map/pallas_call | solution.py:146
  56.5 2.2 %collective-permute-done.14.refs_11_.refs_13_.refs_15_ = bf16[1024,512]{1,0:T(8,128)(2,1)S(1)} collective-permute-done((bf16[1024,512]{1,0:T(8,128)(2,1)}, bf16[1024,512]{1,0:T(8,128)(2,1)S(1)}, u32[]{:S(2)}, u32[]{:S(2)}) %collective-permute-start.14) | collective-permute-done | bytes 1048608 | tf_op jit(solution)/shard_map/ppermute | solution.py:387
  58.6 1.5 %collective-permute-start.15 = (bf16[1024,512]{1,0:T(8,128)(2,1)}, bf16[1024,512]{1,0:T(8,128)(2,1)S(1)}, u32[]{:S(2)}, u32[]{:S(2)}) collective-permute-start(bf16[1024,512]{1,0:T(8,128)(2,1)} %shard_map.70), channel_id=1, source_target_pairs={{0,1},{1,0},{2,3},{3,2},{4,5},{5,4},{6,7},{7,6},{8,9},{9,8},{10,11... | collective-permute-start | bytes 3145736 | tf_op jit(solution)/shard_map/ppermute | solution.py:387
  60.2 0.7 compare_reduce_fusion
  62.2 7.3 %shard_map.71.refs_12_ = f32[1024,512]{1,0:T(8,128)} custom-call(s32[3]{0:T(128)S(1)} %pad_add_fusion.pos, s32[8,2]{1,0:T(8,128)} %copy.16.pat, bf16[1,1024,2048]{2,1,0:T(8,128)(2,1)} %g_local.7, bf16[512,512]{1,0:T(8,128)(2,1)} %copy-done.2, bf16[512,512]{1,0:T(8,128)(2,1)} %copy-done.1, bf16[512,512]{1,0:T(8,128)(2,1)} %collective-permute-done.1.refs_2_, ...), custom_call_target="tpu_custom_call" | custom-call | tf_op jit(solution)/shard_map/pallas_call | solution.py:255
  69.5 0.8 copy-done.4
  70.5 5.2 %shard_map.72.refs_14_ = f32[1024,512]{1,0:T(8,128)} custom-call(s32[3]{0:T(128)S(1)} %pad_add_fusion.pos, s32[8,2]{1,0:T(8,128)} %copy.16.pat, bf16[1,1024,2048]{2,1,0:T(8,128)(2,1)} %g_local.7, bf16[512,512]{1,0:T(8,128)(2,1)} %copy-done.2, bf16[512,512]{1,0:T(8,128)(2,1)} %copy-done.1, ...), custom_call_target="tpu_custom_call", output_to_operand_aliasing={{}: (15, {})} | custom-call | tf_op jit(solution)/shard_map/pallas_call | solution.py:255
  75.7 4.0 %collective-permute-start.5 = (bf16[512,512]{1,0:T(8,128)(2,1)}, bf16[512,512]{1,0:T(8,128)(2,1)S(1)}, u32[]{:S(2)}, u32[]{:S(2)}) collective-permute-start(bf16[512,512]{1,0:T(8,128)(2,1)} %copy-done.4), channel_id=1, source_target_pairs={{0,2},{2,4},{4,6},{1,3},{3,5},{5,7},{8,10},{10,12},{12,14},{9,11},... | collective-permute-start | bytes 1572872 | tf_op jit(solution)/shard_map/ppermute | solution.py:393
  79.7 1.3 collective-permute-start.6
  81.0 1.1 conditional.1
  81.0 1.0 broadcast.7
  82.1 4.6 %collective-permute-start.11 = (bf16[512,512]{1,0:T(8,128)(2,1)}, bf16[512,512]{1,0:T(8,128)(2,1)S(1)}, u32[]{:S(2)}, u32[]{:S(2)}) collective-permute-start(bf16[512,512]{1,0:T(8,128)(2,1)} %collective-permute-done.9.refs_8_.refs_10_), channel_id=1, source_target_pairs={{0,2},{2,4},{4,6},{1,3},{3,5},{5,7},{8,10},{10,12},{12,14},{9,11},... | collective-permute-start | bytes 1572872 | tf_op jit(solution)/shard_map/ppermute | solution.py:393
  86.6 1.3 collective-permute-start.12
  88.6 3.7 %collective-permute-done.5.refs_6_ = bf16[512,512]{1,0:T(8,128)(2,1)S(1)} collective-permute-done((bf16[512,512]{1,0:T(8,128)(2,1)}, bf16[512,512]{1,0:T(8,128)(2,1)S(1)}, u32[]{:S(2)}, u32[]{:S(2)}) %collective-permute-start.5) | collective-permute-done | bytes 524320 | tf_op jit(solution)/shard_map/ppermute | solution.py:393
  92.3 4.3 %collective-permute-done.6.refs_7_ = bf16[512,512]{1,0:T(8,128)(2,1)S(1)} collective-permute-done((bf16[512,512]{1,0:T(8,128)(2,1)}, bf16[512,512]{1,0:T(8,128)(2,1)S(1)}, u32[]{:S(2)}, u32[]{:S(2)}) %collective-permute-start.6) | collective-permute-done | bytes 524320 | tf_op jit(solution)/shard_map/ppermute | solution.py:394
  96.6 0.8 copy-done.7
  97.4 3.1 %shard_map.73.refs_18_ = f32[1024,512]{1,0:T(8,128)} custom-call(s32[3]{0:T(128)S(1)} %pad_add_fusion.pos, s32[8,2]{1,0:T(8,128)} %copy.16.pat, bf16[1,1024,2048]{2,1,0:T(8,128)(2,1)} %g_local.7, bf16[512,512]{1,0:T(8,128)(2,1)} %copy-done.2, bf16[512,512]{1,0:T(8,128)(2,1)} %copy-done.1, ...), custom_call_target="tpu_custom_call", output_to_operand_aliasing={{}: (17, {})} | custom-call | tf_op jit(solution)/shard_map/pallas_call | solution.py:255
  101.0 4.0 %collective-permute-done.12.refs_13_ = bf16[512,512]{1,0:T(8,128)(2,1)S(1)} collective-permute-done((bf16[512,512]{1,0:T(8,128)(2,1)}, bf16[512,512]{1,0:T(8,128)(2,1)S(1)}, u32[]{:S(2)}, u32[]{:S(2)}) %collective-permute-start.12) | collective-permute-done | bytes 524320 | tf_op jit(solution)/shard_map/ppermute | solution.py:394
  105.0 0.8 copy-done.10
  105.8 6.5 %late.1 = (f32[128,512]{1,0:T(8,128)}, bf16[128,512]{1,0:T(8,128)(2,1)}, bf16[128,512]{1,0:T(8,128)(2,1)}, bf16[128,512]{1,0:T(8,128)(2,1)}, f32[256,512]{1,0:T(...) custom-call(s32[3]{0:T(128)S(1)} %pad_add_fusion.pos, s32[8,2]{1,0:T(8,128)} %copy.16.pat, ...), custom_call_target="tpu_custom_call" | custom-call | tf_op jit(solution)/shard_map/late/pallas_call | solution.py:324
  112.4 1.5 %collective-permute-start.20 = (bf16[128,512]{1,0:T(8,128)(2,1)}, bf16[128,512]{1,0:T(8,128)(2,1)S(1)}, u32[]{:S(2)}, u32[]{:S(2)}) collective-permute-start(bf16[128,512]{1,0:T(8,128)(2,1)} %get-tuple-element.40), channel_id=1, source_target_pairs={{0,16},{8,24},{16,0},{24,8},{1,17},{9,25},{17,1},{25,9},{2,18},{10... | collective-permute-start | bytes 393224 | tf_op jit(solution)/shard_map/ppermute | solution.py:429
  114.3 4.8 %collective-permute-done.20.refs_1_ = bf16[128,512]{1,0:T(8,128)(2,1)S(1)} collective-permute-done((bf16[128,512]{1,0:T(8,128)(2,1)}, bf16[128,512]{1,0:T(8,128)(2,1)S(1)}, u32[]{:S(2)}, u32[]{:S(2)}) %collective-permute-start.20) | collective-permute-done | bytes 131104 | tf_op jit(solution)/shard_map/ppermute | solution.py:429
  119.1 1.7 %collective-permute-done.21.refs_2_ = bf16[128,512]{1,0:T(8,128)(2,1)S(1)} collective-permute-done((bf16[128,512]{1,0:T(8,128)(2,1)}, bf16[128,512]{1,0:T(8,128)(2,1)S(1)}, u32[]{:S(2)}, u32[]{:S(2)}) %collective-permute-start.21) | collective-permute-done | bytes 131104 | tf_op jit(solution)/shard_map/ppermute | solution.py:429
  120.8 0.7 copy-done.13
  121.4 1.8 %shard_map.74 = (f32[32,512]{1,0:T(8,128)}, bf16[32,512]{1,0:T(8,128)(2,1)}, bf16[32,512]{1,0:T(8,128)(2,1)}, bf16[32,512]{1,0:T(8,128)(2,1)}) custom-call(s32[3]{0:T(128)S(1)} %pad_add_fusion.pos, f32[128,512]{1,0:T(8,128)} %get-tuple-element.38.keep, bf16[128,512]{1,0:T(8,128)(2,1)} %copy-done.11, bf16[128,512]{1,0:T(8,128)(2,1)} %copy-done.12, ...), custom_call_target="tpu_custom_call" | custom-call | tf_op jit(solution)/shard_map/pallas_call | solution.py:356
  123.7 3.4 %collective-permute-start.24 = (bf16[32,512]{1,0:T(8,128)(2,1)}, bf16[32,512]{1,0:T(8,128)(2,1)S(1)}, u32[]{:S(2)}, u32[]{:S(2)}) collective-permute-start(bf16[32,512]{1,0:T(8,128)(2,1)} %get-tuple-element.45), channel_id=1, source_target_pairs={{0,6},{2,0},{4,2},{6,4},{1,7},{3,1},{5,3},{7,5},{8,14},{10,8},{12,... | collective-permute-start | bytes 98312 | tf_op jit(solution)/shard_map/ppermute | solution.py:437
  127.1 1.5 %collective-permute-start.17 = (bf16[256,512]{1,0:T(8,128)(2,1)}, bf16[256,512]{1,0:T(8,128)(2,1)S(1)}, u32[]{:S(2)}, u32[]{:S(2)}) collective-permute-start(bf16[256,512]{1,0:T(8,128)(2,1)} %get-tuple-element.36), channel_id=1, source_target_pairs={{0,16},{8,24},{16,0},{24,8},{1,17},{9,25},{17,1},{25,9},{2,18},{10... | collective-permute-start | bytes 786440 | tf_op jit(solution)/shard_map/ppermute | solution.py:429
  128.6 1.0 collective-permute-done.22
  129.8 1.5 %convert_add_fusion.1 = f32[32,512]{1,0:T(8,128)} fusion(bf16[32,512]{1,0:T(8,128)(2,1)S(1)} %collective-permute-done.24, bf16[32,512]{1,0:T(8,128)(2,1)S(1)} %collective-permute-done.23, f32[32,512]{1,0:T(8,128)} %get-tuple-element.42, bf16[32,512]{1,0:T(8,128)(2,1)S(1)} %collective-permute-done.22), kind=kLoop, calls=%fused_computation.3 | loop fusion | flops 98304 | bytes 229376 | tf_op jit(solution)/shard_map/add | solution.py:441
  131.3 5.2 %collective-permute-done.17 = bf16[256,512]{1,0:T(8,128)(2,1)S(1)} collective-permute-done((bf16[256,512]{1,0:T(8,128)(2,1)}, bf16[256,512]{1,0:T(8,128)(2,1)S(1)}, u32[]{:S(2)}, u32[]{:S(2)}) %collective-permute-start.17) | collective-permute-done | bytes 262176 | tf_op jit(solution)/shard_map/ppermute | solution.py:429
  136.5 4.7 %collective-permute-done.18 = bf16[256,512]{1,0:T(8,128)(2,1)S(1)} collective-permute-done((bf16[256,512]{1,0:T(8,128)(2,1)}, bf16[256,512]{1,0:T(8,128)(2,1)S(1)}, u32[]{:S(2)}, u32[]{:S(2)}) %collective-permute-start.18) | collective-permute-done | bytes 262176 | tf_op jit(solution)/shard_map/ppermute | solution.py:429
  141.2 2.0 %convert_add_fusion = f32[256,512]{1,0:T(8,128)} fusion(bf16[256,512]{1,0:T(8,128)(2,1)S(1)} %collective-permute-done.18, bf16[256,512]{1,0:T(8,128)(2,1)S(1)} %collective-permute-done.17, f32[256,512]{1,0:T(8,128)} %get-tuple-element.34, bf16[256,512]{1,0:T(8,128)(2,1)S(1)} %collective-permute-done.16), kind=kLoop, calls=%fused_computation | loop fusion | flops 786432 | bytes 1835008 | tf_op jit(solution)/shard_map/add | solution.py:439
  (46 shorter events, 1.8 us)
Async XLA Ops:
  0.6 7.2 %copy-start.14 = (s32[8,2]{0,1:T(2,128)S(1)}, s32[8,2]{0,1:T(2,128)}, u32[]{:S(2)}) copy-start(s32[8,2]{0,1:T(2,128)} %param.11) | copy-start | bytes 196
  1.9 15.6 %copy-start.2 = (bf16[512,512]{1,0:T(8,128)(2,1)}, bf16[512,512]{1,0:T(8,128)(2,1)S(1)}, u32[]{:S(2)}) copy-start(bf16[512,512]{1,0:T(8,128)(2,1)S(1)} %get-tuple-element.52.refs_0_) | copy-start | bytes 1572868
  1.9 16.9 %copy-start.1 = (bf16[512,512]{1,0:T(8,128)(2,1)}, bf16[512,512]{1,0:T(8,128)(2,1)S(1)}, u32[]{:S(2)}) copy-start(bf16[512,512]{1,0:T(8,128)(2,1)S(1)} %get-tuple-element.51.refs_1_) | copy-start | bytes 1572868
  1.9 16.9 %collective-permute-start.1 = (bf16[512,512]{1,0:T(8,128)(2,1)S(1)}, bf16[512,512]{1,0:T(8,128)(2,1)}, u32[]{:S(2)}, u32[]{:S(2)}) collective-permute-start(bf16[512,512]{1,0:T(8,128)(2,1)S(1)} %get-tuple-element.52.refs_0_), channel_id=1, source_target_pairs={{0,2},{2,4},{4,6},{1,3},{3,5},{5,7},{8,10},{10,12},{12,14},{9,11},... | collective-permute-start | bytes 1572872 | tf_op jit(solution)/shard_map/ppermute | solution.py:393
  11.3 37.0 %collective-permute-start.13 = (bf16[1024,512]{1,0:T(8,128)(2,1)}, bf16[1024,512]{1,0:T(8,128)(2,1)S(1)}, u32[]{:S(2)}, u32[]{:S(2)}) collective-permute-start(bf16[1024,512]{1,0:T(8,128)(2,1)} %shard_map.68), channel_id=1, source_target_pairs={{0,1},{1,0},{2,3},{3,2},{4,5},{5,4},{6,7},{7,6},{8,9},{9,8},{10,11... | collective-permute-start | bytes 3145736 | tf_op jit(solution)/shard_map/ppermute | solution.py:387
  15.7 43.0 %collective-permute-start.14 = (bf16[1024,512]{1,0:T(8,128)(2,1)}, bf16[1024,512]{1,0:T(8,128)(2,1)S(1)}, u32[]{:S(2)}, u32[]{:S(2)}) collective-permute-start(bf16[1024,512]{1,0:T(8,128)(2,1)} %shard_map.69), channel_id=1, source_target_pairs={{0,1},{1,0},{2,3},{3,2},{4,5},{5,4},{6,7},{7,6},{8,9},{9,8},{10,11... | collective-permute-start | bytes 3145736 | tf_op jit(solution)/shard_map/ppermute | solution.py:387
  16.3 16.8 %collective-permute-start.8 = (bf16[512,512]{1,0:T(8,128)(2,1)S(1)}, bf16[512,512]{1,0:T(8,128)(2,1)}, u32[]{:S(2)}, u32[]{:S(2)}) collective-permute-start(bf16[512,512]{1,0:T(8,128)(2,1)S(1)} %get-tuple-element.51.refs_1_), channel_id=1, source_target_pairs={{2,0},{4,2},{6,4},{3,1},{5,3},{7,5},{10,8},{12,10},{14,12},{11,9},... | collective-permute-start | bytes 1572872 | tf_op jit(solution)/shard_map/ppermute | solution.py:394
  17.6 26.7 %collective-permute-start.2 = (bf16[512,512]{1,0:T(8,128)(2,1)S(1)}, bf16[512,512]{1,0:T(8,128)(2,1)}, u32[]{:S(2)}, u32[]{:S(2)}) collective-permute-start(bf16[512,512]{1,0:T(8,128)(2,1)S(1)} %get-tuple-element.52.refs_0_), channel_id=1, source_target_pairs={{2,0},{4,2},{6,4},{3,1},{5,3},{7,5},{10,8},{12,10},{14,12},{11,9},... | collective-permute-start | bytes 1572872 | tf_op jit(solution)/shard_map/ppermute | solution.py:394
  18.9 28.1 %collective-permute-start.7 = (bf16[512,512]{1,0:T(8,128)(2,1)S(1)}, bf16[512,512]{1,0:T(8,128)(2,1)}, u32[]{:S(2)}, u32[]{:S(2)}) collective-permute-start(bf16[512,512]{1,0:T(8,128)(2,1)S(1)} %get-tuple-element.51.refs_1_), channel_id=1, source_target_pairs={{0,2},{2,4},{4,6},{1,3},{3,5},{5,7},{8,10},{10,12},{12,14},{9,11},... | collective-permute-start | bytes 1572872 | tf_op jit(solution)/shard_map/ppermute | solution.py:393
  33.0 36.4 %collective-permute-start.10 = (bf16[512,512]{1,0:T(8,128)(2,1)}, bf16[512,512]{1,0:T(8,128)(2,1)}, u32[]{:S(2)}, u32[]{:S(2)}) collective-permute-start(bf16[512,512]{1,0:T(8,128)(2,1)} %collective-permute-done.8.refs_5_.refs_7_.refs_9_), channel_id=1, source_target_pairs={{2,0},{4,2},{6,4},{3,1},{5,3},{7,5},{10,8},{12,10},{14,12},{11,9},... | collective-permute-start | bytes 1572872 | tf_op jit(solution)/shard_map/ppermute | solution.py:394
  44.3 25.2 %collective-permute-start.3 = (bf16[512,512]{1,0:T(8,128)(2,1)}, bf16[512,512]{1,0:T(8,128)(2,1)S(1)}, u32[]{:S(2)}, u32[]{:S(2)}) collective-permute-start(bf16[512,512]{1,0:T(8,128)(2,1)} %collective-permute-done.1.refs_2_), channel_id=1, source_target_pairs={{0,2},{2,4},{4,6},{1,3},{3,5},{5,7},{8,10},{10,12},{12,14},{9,11},... | collective-permute-start | bytes 1572872 | tf_op jit(solution)/shard_map/ppermute | solution.py:393
  47.0 22.5 %collective-permute-start.4 = (bf16[512,512]{1,0:T(8,128)(2,1)}, bf16[512,512]{1,0:T(8,128)(2,1)S(1)}, u32[]{:S(2)}, u32[]{:S(2)}) collective-permute-start(bf16[512,512]{1,0:T(8,128)(2,1)} %collective-permute-done.2.refs_3_), channel_id=1, source_target_pairs={{2,0},{4,2},{6,4},{3,1},{5,3},{7,5},{10,8},{12,10},{14,12},{11,9},... | collective-permute-start | bytes 1572872 | tf_op jit(solution)/shard_map/ppermute | solution.py:394
  48.3 8.2 %copy-start = (bf16[1024,512]{1,0:T(8,128)(2,1)}, bf16[1024,512]{1,0:T(8,128)(2,1)S(1)}, u32[]{:S(2)}) copy-start(bf16[1024,512]{1,0:T(8,128)(2,1)S(1)} %collective-permute-done.13.refs_6_.refs_10_.refs_12_.refs_14_) | copy-start | bytes 3145732
  48.3 21.2 %collective-permute-start.9 = (bf16[512,512]{1,0:T(8,128)(2,1)}, bf16[512,512]{1,0:T(8,128)(2,1)}, u32[]{:S(2)}, u32[]{:S(2)}) collective-permute-start(bf16[512,512]{1,0:T(8,128)(2,1)} %collective-permute-done.7.refs_4_.refs_6_.refs_8_), channel_id=1, source_target_pairs={{0,2},{2,4},{4,6},{1,3},{3,5},{5,7},{8,10},{10,12},{12,14},{9,11},... | collective-permute-start | bytes 1572872 | tf_op jit(solution)/shard_map/ppermute | solution.py:393
  58.6 10.8 %copy-start.3 = (bf16[1024,512]{1,0:T(8,128)(2,1)}, bf16[1024,512]{1,0:T(8,128)(2,1)S(1)}, u32[]{:S(2)}) copy-start(bf16[1024,512]{1,0:T(8,128)(2,1)S(1)} %collective-permute-done.14.refs_11_.refs_13_.refs_15_) | copy-start | bytes 3145732
  58.6 41.9 %collective-permute-start.15 = (bf16[1024,512]{1,0:T(8,128)(2,1)}, bf16[1024,512]{1,0:T(8,128)(2,1)S(1)}, u32[]{:S(2)}, u32[]{:S(2)}) collective-permute-start(bf16[1024,512]{1,0:T(8,128)(2,1)} %shard_map.70), channel_id=1, source_target_pairs={{0,1},{1,0},{2,3},{3,2},{4,5},{5,4},{6,7},{7,6},{8,9},{9,8},{10,11... | collective-permute-start | bytes 3145736 | tf_op jit(solution)/shard_map/ppermute | solution.py:387
  69.5 0.8 copy-start.4
  69.5 1.0 copy-start.5
  75.7 16.6 %collective-permute-start.5 = (bf16[512,512]{1,0:T(8,128)(2,1)}, bf16[512,512]{1,0:T(8,128)(2,1)S(1)}, u32[]{:S(2)}, u32[]{:S(2)}) collective-permute-start(bf16[512,512]{1,0:T(8,128)(2,1)} %copy-done.4), channel_id=1, source_target_pairs={{0,2},{2,4},{4,6},{1,3},{3,5},{5,7},{8,10},{10,12},{12,14},{9,11},... | collective-permute-start | bytes 1572872 | tf_op jit(solution)/shard_map/ppermute | solution.py:393
  79.7 16.9 %collective-permute-start.6 = (bf16[512,512]{1,0:T(8,128)(2,1)}, bf16[512,512]{1,0:T(8,128)(2,1)S(1)}, u32[]{:S(2)}, u32[]{:S(2)}) collective-permute-start(bf16[512,512]{1,0:T(8,128)(2,1)} %copy-done.5), channel_id=1, source_target_pairs={{2,0},{4,2},{6,4},{3,1},{5,3},{7,5},{10,8},{12,10},{14,12},{11,9},... | collective-permute-start | bytes 1572872 | tf_op jit(solution)/shard_map/ppermute | solution.py:394
  82.1 18.9 %collective-permute-start.11 = (bf16[512,512]{1,0:T(8,128)(2,1)}, bf16[512,512]{1,0:T(8,128)(2,1)S(1)}, u32[]{:S(2)}, u32[]{:S(2)}) collective-permute-start(bf16[512,512]{1,0:T(8,128)(2,1)} %collective-permute-done.9.refs_8_.refs_10_), channel_id=1, source_target_pairs={{0,2},{2,4},{4,6},{1,3},{3,5},{5,7},{8,10},{10,12},{12,14},{9,11},... | collective-permute-start | bytes 1572872 | tf_op jit(solution)/shard_map/ppermute | solution.py:393
  86.6 18.4 %collective-permute-start.12 = (bf16[512,512]{1,0:T(8,128)(2,1)}, bf16[512,512]{1,0:T(8,128)(2,1)S(1)}, u32[]{:S(2)}, u32[]{:S(2)}) collective-permute-start(bf16[512,512]{1,0:T(8,128)(2,1)} %collective-permute-done.10.refs_9_.refs_11_), channel_id=1, source_target_pairs={{2,0},{4,2},{6,4},{3,1},{5,3},{7,5},{10,8},{12,10},{14,12},{11,9},... | collective-permute-start | bytes 1572872 | tf_op jit(solution)/shard_map/ppermute | solution.py:394
  92.3 4.3 %copy-start.6 = (bf16[512,512]{1,0:T(8,128)(2,1)}, bf16[512,512]{1,0:T(8,128)(2,1)S(1)}, u32[]{:S(2)}) copy-start(bf16[512,512]{1,0:T(8,128)(2,1)S(1)} %collective-permute-done.5.refs_6_) | copy-start | bytes 1572868
  96.6 0.8 copy-start.7
  100.6 4.4 %copy-start.8 = (bf16[1024,512]{1,0:T(8,128)(2,1)}, bf16[1024,512]{1,0:T(8,128)(2,1)S(1)}, u32[]{:S(2)}) copy-start(bf16[1024,512]{1,0:T(8,128)(2,1)S(1)} %collective-permute-done.15.refs_16_) | copy-start | bytes 3145732
  101.0 4.0 %copy-start.9 = (bf16[512,512]{1,0:T(8,128)(2,1)}, bf16[512,512]{1,0:T(8,128)(2,1)S(1)}, u32[]{:S(2)}) copy-start(bf16[512,512]{1,0:T(8,128)(2,1)S(1)} %collective-permute-done.11.refs_12_) | copy-start | bytes 1572868
  105.0 0.8 copy-start.10
  112.3 1.9 %collective-permute-start.19 = (bf16[128,512]{1,0:T(8,128)(2,1)}, bf16[128,512]{1,0:T(8,128)(2,1)S(1)}, u32[]{:S(2)}, u32[]{:S(2)}) collective-permute-start(bf16[128,512]{1,0:T(8,128)(2,1)} %get-tuple-element.39), channel_id=1, source_target_pairs={{0,8},{8,0},{16,24},{24,16},{1,9},{9,1},{17,25},{25,17},{2,10},{10... | collective-permute-start | bytes 393224 | tf_op jit(solution)/shard_map/ppermute | solution.py:429
  112.4 6.6 %collective-permute-start.20 = (bf16[128,512]{1,0:T(8,128)(2,1)}, bf16[128,512]{1,0:T(8,128)(2,1)S(1)}, u32[]{:S(2)}, u32[]{:S(2)}) collective-permute-start(bf16[128,512]{1,0:T(8,128)(2,1)} %get-tuple-element.40), channel_id=1, source_target_pairs={{0,16},{8,24},{16,0},{24,8},{1,17},{9,25},{17,1},{25,9},{2,18},{10... | collective-permute-start | bytes 393224 | tf_op jit(solution)/shard_map/ppermute | solution.py:429
  114.0 6.8 %collective-permute-start.21 = (bf16[128,512]{1,0:T(8,128)(2,1)}, bf16[128,512]{1,0:T(8,128)(2,1)S(1)}, u32[]{:S(2)}, u32[]{:S(2)}) collective-permute-start(bf16[128,512]{1,0:T(8,128)(2,1)} %get-tuple-element.41), channel_id=1, source_target_pairs={{0,24},{8,16},{16,8},{24,0},{1,25},{9,17},{17,9},{25,1},{2,26},{10... | collective-permute-start | bytes 393224 | tf_op jit(solution)/shard_map/ppermute | solution.py:429
  114.3 6.5 %copy-start.11 = (bf16[128,512]{1,0:T(8,128)(2,1)}, bf16[128,512]{1,0:T(8,128)(2,1)S(1)}, u32[]{:S(2)}) copy-start(bf16[128,512]{1,0:T(8,128)(2,1)S(1)} %collective-permute-done.19.refs_0_) | copy-start | bytes 393220
  119.1 1.7 %copy-start.12 = (bf16[128,512]{1,0:T(8,128)(2,1)}, bf16[128,512]{1,0:T(8,128)(2,1)S(1)}, u32[]{:S(2)}) copy-start(bf16[128,512]{1,0:T(8,128)(2,1)S(1)} %collective-permute-done.20.refs_1_) | copy-start | bytes 393220
  120.8 0.7 copy-start.13
  123.3 6.3 %collective-permute-start.22 = (bf16[32,512]{1,0:T(8,128)(2,1)}, bf16[32,512]{1,0:T(8,128)(2,1)S(1)}, u32[]{:S(2)}, u32[]{:S(2)}) collective-permute-start(bf16[32,512]{1,0:T(8,128)(2,1)} %get-tuple-element.43), channel_id=1, source_target_pairs={{0,2},{2,4},{4,6},{6,0},{1,3},{3,5},{5,7},{7,1},{8,10},{10,12},{12... | collective-permute-start | bytes 98312 | tf_op jit(solution)/shard_map/ppermute | solution.py:437
  123.3 6.3 %collective-permute-start.23 = (bf16[32,512]{1,0:T(8,128)(2,1)}, bf16[32,512]{1,0:T(8,128)(2,1)S(1)}, u32[]{:S(2)}, u32[]{:S(2)}) collective-permute-start(bf16[32,512]{1,0:T(8,128)(2,1)} %get-tuple-element.44), channel_id=1, source_target_pairs={{0,4},{2,6},{4,0},{6,2},{1,5},{3,7},{5,1},{7,3},{8,12},{10,14},{12... | collective-permute-start | bytes 98312 | tf_op jit(solution)/shard_map/ppermute | solution.py:437
  123.7 6.1 %collective-permute-start.24 = (bf16[32,512]{1,0:T(8,128)(2,1)}, bf16[32,512]{1,0:T(8,128)(2,1)S(1)}, u32[]{:S(2)}, u32[]{:S(2)}) collective-permute-start(bf16[32,512]{1,0:T(8,128)(2,1)} %get-tuple-element.45), channel_id=1, source_target_pairs={{0,6},{2,0},{4,2},{6,4},{1,7},{3,1},{5,3},{7,5},{8,14},{10,8},{12,... | collective-permute-start | bytes 98312 | tf_op jit(solution)/shard_map/ppermute | solution.py:437
  127.1 4.2 %collective-permute-start.16 = (bf16[256,512]{1,0:T(8,128)(2,1)}, bf16[256,512]{1,0:T(8,128)(2,1)S(1)}, u32[]{:S(2)}, u32[]{:S(2)}) collective-permute-start(bf16[256,512]{1,0:T(8,128)(2,1)} %get-tuple-element.35), channel_id=1, source_target_pairs={{0,8},{8,0},{16,24},{24,16},{1,9},{9,1},{17,25},{25,17},{2,10},{10... | collective-permute-start | bytes 786440 | tf_op jit(solution)/shard_map/ppermute | solution.py:429
  127.1 9.4 %collective-permute-start.17 = (bf16[256,512]{1,0:T(8,128)(2,1)}, bf16[256,512]{1,0:T(8,128)(2,1)S(1)}, u32[]{:S(2)}, u32[]{:S(2)}) collective-permute-start(bf16[256,512]{1,0:T(8,128)(2,1)} %get-tuple-element.36), channel_id=1, source_target_pairs={{0,16},{8,24},{16,0},{24,8},{1,17},{9,25},{17,1},{25,9},{2,18},{10... | collective-permute-start | bytes 786440 | tf_op jit(solution)/shard_map/ppermute | solution.py:429
  129.5 11.6 %collective-permute-start.18 = (bf16[256,512]{1,0:T(8,128)(2,1)}, bf16[256,512]{1,0:T(8,128)(2,1)S(1)}, u32[]{:S(2)}, u32[]{:S(2)}) collective-permute-start(bf16[256,512]{1,0:T(8,128)(2,1)} %get-tuple-element.37), channel_id=1, source_target_pairs={{0,24},{8,16},{16,8},{24,0},{1,25},{9,17},{17,9},{25,1},{2,26},{10... | collective-permute-start | bytes 786440 | tf_op jit(solution)/shard_map/ppermute | solution.py:429

commit v2 on v1

--- a/solution.py
+++ b/solution.py
@@ -10,7 +10,8 @@
 
 VMEM = pl.BlockSpec(memory_space=pltpu.VMEM)
 SMEM = pl.BlockSpec(memory_space=pltpu.SMEM)
-ANY = pl.BlockSpec(memory_space=pl.ANY)
+ANY = pl.BlockSpec(memory_space=pltpu.HBM)
+SMALL = pltpu.CompilerParams(vmem_limit_bytes=12 * 2**20)
 F32 = jnp.float32
 BF16 = jnp.bfloat16
 
@@ -109,7 +110,7 @@
     base = (1 - to) * sz.half
     need, dist = [], []
     for j in range(sz.half):
-        need.append(pat[base + j, to])
+        need.append(pat[to, base + j])
         dist.append(jnp.abs((base + j) // sz.per_row - row))
     rank = []
     for j in range(sz.half):
@@ -122,8 +123,8 @@
     return need, rank
 
 
-def pick_kernel(sz, slot, parts, pos, pat, green, out, buf, in_sem, out_sem):
-    need, rank = swap_ranks(sz, pat, pos[1], 1 - pos[2])
+def pick_kernel(sz, slot, parts, pat, green, out, buf, in_sem, out_sem):
+    need, rank = swap_ranks(sz, pat, lax.axis_index("row"), 1 - lax.axis_index("col"))
     at = jnp.int32(0)
     for j in range(sz.half):
         at = jnp.where(jnp.logical_and(need[j] > 0, rank[j] == slot), j, at)
@@ -141,24 +142,25 @@
         outs[i].wait()
 
 
-def pick(sz, slot, pos, pattern, green):
+def pick(sz, slot, pattern, green):
     parts = 4
     return pl.pallas_call(
         functools.partial(pick_kernel, sz, slot, parts),
         out_shape=jax.ShapeDtypeStruct((sz.local_rows, sz.block), BF16),
-        in_specs=[SMEM, SMEM, ANY],
+        in_specs=[SMEM, ANY],
         out_specs=ANY,
         scratch_shapes=[
             pltpu.VMEM((parts, sz.local_rows // parts, sz.block), BF16),
             pltpu.SemaphoreType.DMA((parts,)),
             pltpu.SemaphoreType.DMA((parts,)),
         ],
-    )(pos, pattern, green)
-
-
-def product_jobs(sz, pos, pat, ready, before, m_refs, g_local, g_slots, job, bufs, total):
+        compiler_params=SMALL,
+    )(pattern, *in_hbm([green]))
+
+
+def product_jobs(sz, pat, ready, before, m_refs, g_local, g_slots, job, bufs, total):
     m_buf, g_buf, m_sem, g_sem = bufs
-    row, col = pos[1], pos[2]
+    row, col = lax.axis_index("row"), lax.axis_index("col")
     _, rank = swap_ranks(sz, pat, row, col)
 
     def inside(bound, dist, e, slot):
@@ -175,7 +177,7 @@
         local = (a // sz.half) == col
         slot = jnp.where(local, -1, rank[a % sz.half])
         todo = jnp.logical_and(inside(ready, dist, e, slot), jnp.logical_not(inside(before, dist, e, slot)))
-        todo = jnp.logical_and(todo, pat[a, col] > 0)
+        todo = jnp.logical_and(todo, pat[col, a] > 0)
 
         @pl.when(todo)
         def _(a=a, count=count, slot=slot, away=away):
@@ -218,6 +220,10 @@
         return carry
 
     lax.fori_loop(0, count, step, 0)
+
+
+def in_hbm(arrays):
+    return [pltpu.with_memory_space_constraint(a, pltpu.HBM) for a in arrays]
 
 
 def job_scratch(sz):
@@ -230,7 +236,7 @@
     ]
 
 
-def early_kernel(sz, ready, before, keys, n_slots, first, pos, pat, g_local, *refs):
+def early_kernel(sz, ready, before, keys, n_slots, first, pat, g_local, *refs):
     refs = list(refs)
     m_refs = {k: refs.pop(0) for k in keys}
     g_slots = [refs.pop(0) for _ in range(n_slots)]
@@ -241,13 +247,13 @@
         out[...] = jnp.zeros_like(out)
     else:
         out[...] = total_in[...]
-    product_jobs(sz, pos, pat, ready, before, m_refs, g_local, g_slots, job, (m_buf, g_buf, m_sem, g_sem), out)
-
-
-def early(sz, ready, before, pos, pattern, green, m, slots, total):
+    product_jobs(sz, pat, ready, before, m_refs, g_local, g_slots, job, (m_buf, g_buf, m_sem, g_sem), out)
+
+
+def early(sz, ready, before, pattern, green, m, slots, total):
     keys = list(m)
     first = total is None
-    args = [pos, pattern, green] + [m[k] for k in keys] + list(slots) + ([] if first else [total])
+    args = [pattern] + in_hbm([green] + [m[k] for k in keys] + list(slots)) + ([] if first else [total])
     return early_call(sz, ready, before, keys, slots, first, args)
 
 
@@ -255,10 +261,11 @@
     return pl.pallas_call(
         functools.partial(early_kernel, sz, ready, before, keys, len(slots), first),
         out_shape=jax.ShapeDtypeStruct((sz.local_rows, sz.width), F32),
-        in_specs=[SMEM, SMEM] + [ANY] * (1 + len(keys) + len(slots)) + ([] if first else [VMEM]),
+        in_specs=[SMEM] + [ANY] * (1 + len(keys) + len(slots)) + ([] if first else [VMEM]),
         out_specs=VMEM,
         scratch_shapes=job_scratch(sz),
         input_output_aliases={} if first else {len(args) - 1: 0},
+        compiler_params=SMALL,
     )(*args)
 
 
@@ -272,24 +279,24 @@
             for x in range(sz.outer) for c in range(sz.cores)]
 
 
-def late_kernel(sz, ready, before, keys, n_slots, pos, pat, weight, g_local, *refs):
+def late_kernel(sz, ready, before, keys, n_slots, pat, weight, g_local, *refs):
     refs = list(refs)
     m_refs = {k: refs.pop(0) for k in keys}
     g_slots = [refs.pop(0) for _ in range(n_slots)]
     total_in, factor, dinv = refs.pop(0), refs.pop(0), refs.pop(0)
     diag_out = [refs.pop(0) for _ in range(sz.poles)]
-    off_out = [refs.pop(0) for _ in range(sz.poles)]
+    off_out = [refs.pop(0) for _ in range(sz.cores)]
     total, diag = refs.pop(0), refs.pop(0)
     job, m_buf, g_buf, m_sem, g_sem = refs
-    row, col = pos[1], pos[2]
-    core, x_at = lax.rem(pos[0], sz.cores), pos[0] // sz.cores
+    row, col, pole = (lax.axis_index(a) for a in ("row", "col", "pole"))
+    core, x_at = lax.rem(pole, sz.cores), pole // sz.cores
     total[...] = total_in[...]
-    product_jobs(sz, pos, pat, ready, before, m_refs, g_local, g_slots, job, (m_buf, g_buf, m_sem, g_sem), total)
+    product_jobs(sz, pat, ready, before, m_refs, g_local, g_slots, job, (m_buf, g_buf, m_sem, g_sem), total)
     w = weight[0]
     diag[...] = jnp.zeros_like(diag)
     for e in range(sz.per_row):
         at = pl.ds(e * sz.block, sz.block)
-        kept = pat[row * sz.per_row + e, col] > 0
+        kept = pat[col, row * sz.per_row + e] > 0
 
         @pl.when(kept)
         def _(at=at):
@@ -303,40 +310,39 @@
             total[at, :] = jnp.zeros((sz.block, sz.width), F32)
     mine = pl.ds(pl.multiple_of(row * sz.count, sz.count), sz.count)
     diag[mine, :] += w * dinv[0].astype(F32)
-    for src, keep, sends in ((diag, diag_out[0], diag_out[1:]), (total, off_out[0], off_out[1:])):
-        n = src.shape[0] // sz.poles
-
-        def part(x, c):
-            return src[pl.ds(pl.multiple_of((x * sz.cores + c) * n, n), n), :]
-
-        keep[...] = part(x_at, core)
-        for (dx, dc), send in zip(pole_steps(sz), sends):
-            send[...] = part(lax.rem(x_at + dx, sz.outer), lax.rem(core + dc, sz.cores)).astype(BF16)
-
-
-def late(sz, ready, before, pos, pattern, weight, green, m, slots, total, factor, dinv):
+    n = diag.shape[0] // sz.poles
+    for (dx, dc), out in zip([(0, 0)] + pole_steps(sz), diag_out):
+        q = lax.rem(x_at + dx, sz.outer) * sz.cores + lax.rem(core + dc, sz.cores)
+        out[...] = diag[pl.ds(pl.multiple_of(q * n, n), n), :].astype(out.dtype)
+    n = total.shape[0] // sz.poles
+    for dc, out in enumerate(off_out):
+        for x in range(sz.outer):
+            q = x * sz.cores + lax.rem(core + dc, sz.cores)
+            out[x * n:(x + 1) * n, :] = total[pl.ds(pl.multiple_of(q * n, n), n), :].astype(out.dtype)
+
+
+def late(sz, ready, before, pattern, weight, green, m, slots, total, factor, dinv):
     keys = list(m)
-    args = [pos, pattern, weight, green] + [m[k] for k in keys] + list(slots) + [total, factor, dinv]
-    shapes = []
-    for n in (sz.block, sz.local_rows):
-        for i in range(sz.poles):
-            shapes.append(jax.ShapeDtypeStruct((n // sz.poles, sz.width), BF16 if i else F32))
+    args = [pattern, weight] + in_hbm([green] + [m[k] for k in keys] + list(slots)) + [total, factor, dinv]
+    shapes = [jax.ShapeDtypeStruct((sz.block // sz.poles, sz.width), BF16 if i else F32) for i in range(sz.poles)]
+    shapes += [jax.ShapeDtypeStruct((sz.local_rows // sz.cores, sz.width), BF16 if i else F32) for i in range(sz.cores)]
     return pl.pallas_call(
         functools.partial(late_kernel, sz, ready, before, keys, len(slots)),
         out_shape=shapes,
-        in_specs=[SMEM] * 3 + [ANY] * (1 + len(keys) + len(slots)) + [VMEM] * 3,
-        out_specs=[VMEM] * (2 * sz.poles),
+        in_specs=[SMEM] * 2 + [ANY] * (1 + len(keys) + len(slots)) + [VMEM] * 3,
+        out_specs=[VMEM] * (sz.poles + sz.cores),
         scratch_shapes=[pltpu.VMEM((sz.local_rows, sz.width), F32), pltpu.VMEM((sz.block, sz.width), F32)]
         + job_scratch(sz),
+        compiler_params=SMALL,
         name="late",
     )(*args)
 
 
-def fold_kernel(group, n_in, axis_pos, stride, pos, keep, *refs):
+def fold_kernel(group, n_in, axis, stride, keep, *refs):
     ins, outs = refs[:n_in], refs[n_in:]
     own, sends = outs[0], outs[1:]
     n = own.shape[0]
-    me = lax.rem(pos[axis_pos] // stride, group)
+    me = lax.rem(lax.axis_index(axis) // stride, group)
 
     def part(d):
         at = pl.ds(pl.multiple_of(d * n, n), n)
@@ -350,15 +356,16 @@
     own[...] = part(me)
 
 
-def fold(group, axis_pos, stride, pos, keep, ins):
+def fold(group, axis, stride, keep, ins):
     n, width = keep.shape[0] // group, keep.shape[1]
     shapes = [jax.ShapeDtypeStruct((n, width), F32)] + [jax.ShapeDtypeStruct((n, width), BF16)] * (group - 1)
     return pl.pallas_call(
-        functools.partial(fold_kernel, group, len(ins), axis_pos, stride),
+        functools.partial(fold_kernel, group, len(ins), axis, stride),
         out_shape=shapes,
-        in_specs=[SMEM] + [VMEM] * (1 + len(ins)),
+        in_specs=[VMEM] * (1 + len(ins)),
         out_specs=[VMEM] * group,
-    )(pos, keep, *ins)
+        compiler_params=SMALL,
+    )(keep, *ins)
 
 
 def shifts(size, group, stride):
@@ -374,7 +381,7 @@
 
 def blocked(sz, green, factor, diag_inverse, pole_weight, pattern):
     block, per_row = sz.block, sz.per_row
-    pos = jnp.stack([lax.axis_index(a) for a in ("pole", "row", "col")]).astype(jnp.int32)
+    pattern = pattern.T
     fac = [factor[0, e * block:(e + 1) * block] for e in range(per_row)]
     right = [(i, i + 1) for i in range(sz.rows - 1)]
     left = [(i + 1, i) for i in range(sz.rows - 1)]
@@ -383,7 +390,7 @@
     fixed = max(sz.half - 1, 1)
     slots = []
     for s in range(fixed):
-        sent = pick(sz, s, pos, pattern, green)
+        sent = pick(sz, s, pattern, green)
         slots.append(lax.ppermute(sent, "col", swap))
 
     m = {e: fac[e] for e in range(per_row)}
@@ -401,7 +408,7 @@
 
     def part(i, total):
         dist, last_e, s = bounds[i]
-        return early(sz, bounds[i], bounds[i - 1] if i else None, pos, pattern, green,
+        return early(sz, bounds[i], bounds[i - 1] if i else None, pattern, green,
                      upto(dist, last_e), slots[:s + 1], total)
 
     total = part(1, part(0, None))
@@ -410,31 +417,33 @@
         full = jnp.bool_(False)
         for c in range(sz.cols):
             other = (1 - c) * sz.half
-            full = jnp.logical_or(full, jnp.all(pattern[other:other + sz.half, c] > 0))
+            full = jnp.logical_or(full, jnp.all(pattern[c, other:other + sz.half] > 0))
 
         def more(g):
-            return lax.ppermute(pick(sz, fixed, pos, pattern, g), "col", swap)
+            return lax.ppermute(pick(sz, fixed, pattern, g), "col", swap)
 
         full, total = lax.optimization_barrier((full, total))
         got = lax.cond(full, more, lambda g: jnp.zeros((sz.local_rows, block), BF16), green)
         got, total = lax.optimization_barrier((got, total))
         extra.append(got)
     total = part(2, total)
-    out = late(sz, (far, per_row - 1, sz.half), bounds[2], pos, pattern, pole_weight, green, m,
+    out = late(sz, (far, per_row - 1, sz.half), bounds[2], pattern, pole_weight, green, m,
                slots + extra, total, factor, diag_inverse)
 
-    def swapped(keep, *sends):
+    def swapped(axis, sends, perms):
         ins = []
-        for v, step in zip(sends, pole_steps(sz)):
-            ins.append(lax.ppermute(v, "pole", pole_perm(sz, step)))
-        return keep, ins
-
-    diag, diag_in = swapped(*out[:sz.poles])
-    off, off_in = swapped(*out[sz.poles:])
-    diag, *sends = fold(sz.rows, 1, 1, pos, diag, diag_in)
-    diag_in = []
-    for v, p in zip(sends, shifts(sz.rows, sz.rows, 1)):
-        diag_in.append(lax.ppermute(v, "row", p))
+        for v, perm in zip(sends, perms):
+            ins.append(lax.ppermute(v, axis, perm))
+        return ins
+
+    diag, *sends = out[:sz.poles]
+    diag_in = swapped("pole", sends, [pole_perm(sz, step) for step in pole_steps(sz)])
+    off, *sends = out[sz.poles:]
+    off_in = swapped("pole", sends, shifts(sz.poles, sz.cores, 1))
+    off, *sends = fold(sz.outer, "pole", sz.cores, off, off_in)
+    off_in = swapped("pole", sends, shifts(sz.poles, sz.outer, sz.cores))
+    diag, *sends = fold(sz.rows, "row", 1, diag, diag_in)
+    diag_in = swapped("row", sends, shifts(sz.rows, sz.rows, 1))
     for v in off_in:
         off = off + v.astype(F32)
     for v in diag_in:

time: 144 us -> 118 us (0.82)
  waiting for transfers between devices: 50.3 us -> 35.1 us
  Pallas kernels: 32.4 us -> 20.1 us
  starting transfers between devices: 47.1 us -> 54.2 us
  local copies, waits for them, and re-layouts: 6.28 us -> 3.17 us
  other arithmetic: 4.26 us -> 2.28 us
    ppermute x6, waiting for transfers between devices: 26.5 us -> 18.1 us  [blocked(): m[step * per_row + e] = b = lax.ppermute(b, 'row', left)]
    pallas_call x3, Pallas kernels: 15.6 us -> 9.54 us  [early_call(): pl.pallas_call(functools.partial(early_kernel, sz, ready, before, keys, l...]
    ppermute x9 -> x8, waiting for transfers between devices: 17.6 us -> 12.2 us  [swapped(): ins.append(lax.ppermute(v, axis, perm))]
    unnamed x31 -> x20, local copies, waits for them, and re-layouts: 3.95 us -> 0.85 us
    ppermute x6, starting transfers between devices: 28.4 us -> 31.3 us  [blocked(): m[-step * per_row + e] = a = lax.ppermute(a, 'row', right)]
    ppermute x9 -> x8, starting transfers between devices: 7.29 us -> 10.1 us  [swapped(): ins.append(lax.ppermute(v, axis, perm))]
    pallas_call x1, Pallas kernels: 6.52 us -> 4.02 us  [late(): pl.pallas_call(functools.partial(late_kernel, sz, ready, before, keys, le...]
    pallas_call x3, Pallas kernels: 8.41 us -> 6.37 us  [pick(): pl.pallas_call(functools.partial(pick_kernel, sz, slot, parts), out_shape...]
  transfers between devices with their start and end apart: 24 -> 23, of which waited for: 13 -> 13; matrix products, arithmetic and copies ran while one was open for 3% -> 2% of each run, Pallas kernels for 17% -> 14%
where the time goes in v2:
time: 118 us
  starting transfers between devices  54.2 us (46%)
  waiting for transfers between devices  35.1 us (30%)
  Pallas kernels  20.1 us (17%)
  local copies, waits for them, and re-layouts  3.17 us (3%)
  between operations  2.83 us (2%)
  other arithmetic  2.28 us (2%)
    ppermute x6, starting transfers between devices, blocked(): m[-step * per_row + e] = a = lax.ppermute(a, 'row', right)  31.3 us
    ppermute x6, waiting for transfers between devices, blocked(): m[step * per_row + e] = b = lax.ppermute(b, 'row', left)  18.1 us
    ppermute x8, waiting for transfers between devices, swapped(): ins.append(lax.ppermute(v, axis, perm))  12.2 us
    ppermute x8, starting transfers between devices, swapped(): ins.append(lax.ppermute(v, axis, perm))  10.1 us
    pallas_call x3, Pallas kernels, early_call(): pl.pallas_call(functools.partial(early_kernel, sz, ready, before, keys, l...  9.54 us
    ppermute x6, starting transfers between devices, blocked(): m[step * per_row + e] = b = lax.ppermute(b, 'row', left)  7.71 us
    pallas_call x3, Pallas kernels, pick(): pl.pallas_call(functools.partial(pick_kernel, sz, slot, parts), out_shape...  6.37 us
    ppermute x3, starting transfers between devices, blocked(): slots.append(lax.ppermute(sent, 'col', swap))  5.06 us
  transfers between devices with their start and end apart: 23, of which 13 were waited for; matrix products, arithmetic and copies ran while one was open for 2% of the time, Pallas kernels for 14%

profile of v2, /device:TPU:0, one launch (start us, length us, event | category | flops | bytes accessed | tf_op | source)
XLA Modules:
  0.0 117.6 jit_solution(9750138255608982587)
XLA Ops:
  0.6 1.3 %slice_bitcast_fusion = (bf16[512,512]{1,0:T(8,128)(2,1)S(1)}, bf16[512,512]{1,0:T(8,128)(2,1)S(1)}) fusion(bf16[1,1024,512]{2,1,0:T(8,128)(2,1)} %refs_19_.1), kind=kLoop, calls=%fused_computation.1 | loop fusion | bytes 2097152 | tf_op jit(solution)/shard_map/squeeze | solution.py:385
  1.9 1.3 %collective-permute-start.8 = (bf16[512,512]{1,0:T(8,128)(2,1)S(1)}, bf16[512,512]{1,0:T(8,128)(2,1)S(1)}, u32[]{:S(2)}, u32[]{:S(2)}) collective-permute-start(bf16[512,512]{1,0:T(8,128)(2,1)S(1)} %get-tuple-element.45.refs_1_), channel_id=1, source_target_pairs={{2,0},{4,2},{6,4},{3,1},{5,3},{7,5},{10,8},{12,10},{14,12},{11,9},... | collective-permute-start | bytes 1572872 | tf_op jit(solution)/shard_map/ppermute | solution.py:401
  3.2 6.4 %collective-permute-start.7 = (bf16[512,512]{1,0:T(8,128)(2,1)S(1)}, bf16[512,512]{1,0:T(8,128)(2,1)}, u32[]{:S(2)}, u32[]{:S(2)}) collective-permute-start(bf16[512,512]{1,0:T(8,128)(2,1)S(1)} %get-tuple-element.45.refs_1_), channel_id=1, source_target_pairs={{0,2},{2,4},{4,6},{1,3},{3,5},{5,7},{8,10},{10,12},{12,14},{9,11},... | collective-permute-start | bytes 1572872 | tf_op jit(solution)/shard_map/ppermute | solution.py:400
  9.6 1.9 %shard_map.68 = bf16[1024,512]{1,0:T(8,128)(2,1)S(1)} custom-call(s32[2,8]{1,0:T(2,128)S(1)} %bitcast.5, bf16[1,1024,2048]{2,1,0:T(8,128)(2,1)} %g_local.7), custom_call_target="tpu_custom_call" | custom-call | tf_op jit(solution)/shard_map/pallas_call | solution.py:147
  11.5 2.0 %collective-permute-start.13 = (bf16[1024,512]{1,0:T(8,128)(2,1)S(1)}, bf16[1024,512]{1,0:T(8,128)(2,1)S(1)}, u32[]{:S(2)}, u32[]{:S(2)}) collective-permute-start(bf16[1024,512]{1,0:T(8,128)(2,1)S(1)} %shard_map.68), channel_id=1, source_target_pairs={{0,1},{1,0},{2,3},{3,2},{4,5},{5,4},{6,7},{7,6},{8,9},{9,8},{10,11... | collective-permute-start | bytes 3145736 | tf_op jit(solution)/shard_map/ppermute | solution.py:394
  13.6 1.3 %collective-permute-start.2 = (bf16[512,512]{1,0:T(8,128)(2,1)S(1)}, bf16[512,512]{1,0:T(8,128)(2,1)}, u32[]{:S(2)}, u32[]{:S(2)}) collective-permute-start(bf16[512,512]{1,0:T(8,128)(2,1)S(1)} %get-tuple-element.46.refs_0_), channel_id=1, source_target_pairs={{2,0},{4,2},{6,4},{3,1},{5,3},{7,5},{10,8},{12,10},{14,12},{11,9},... | collective-permute-start | bytes 1572872 | tf_op jit(solution)/shard_map/ppermute | solution.py:401
  14.9 5.4 %collective-permute-start.1 = (bf16[512,512]{1,0:T(8,128)(2,1)S(1)}, bf16[512,512]{1,0:T(8,128)(2,1)}, u32[]{:S(2)}, u32[]{:S(2)}) collective-permute-start(bf16[512,512]{1,0:T(8,128)(2,1)S(1)} %get-tuple-element.46.refs_0_), channel_id=1, source_target_pairs={{0,2},{2,4},{4,6},{1,3},{3,5},{5,7},{8,10},{10,12},{12,14},{9,11},... | collective-permute-start | bytes 1572872 | tf_op jit(solution)/shard_map/ppermute | solution.py:400
  20.2 1.3 %collective-permute-start.10 = (bf16[512,512]{1,0:T(8,128)(2,1)S(1)}, bf16[512,512]{1,0:T(8,128)(2,1)S(1)}, u32[]{:S(2)}, u32[]{:S(2)}) collective-permute-start(bf16[512,512]{1,0:T(8,128)(2,1)S(1)} %collective-permute-done.8.refs_5_.refs_7_.refs_9_), channel_id=1, source_target_pairs={{2,0},{4,2},{6,4},{3,1},{5,3},{7,5},{10,8},{12,10},{14,12},{11,9},... | collective-permute-start | bytes 1572872 | tf_op jit(solution)/shard_map/ppermute | solution.py:401
  21.5 2.6 %shard_map.69 = bf16[1024,512]{1,0:T(8,128)(2,1)} custom-call(s32[2,8]{1,0:T(2,128)S(1)} %bitcast.6, bf16[1,1024,2048]{2,1,0:T(8,128)(2,1)} %g_local.7), custom_call_target="tpu_custom_call" | custom-call | tf_op jit(solution)/shard_map/pallas_call | solution.py:147
  24.2 1.4 %collective-permute-start.14 = (bf16[1024,512]{1,0:T(8,128)(2,1)}, bf16[1024,512]{1,0:T(8,128)(2,1)}, u32[]{:S(2)}, u32[]{:S(2)}) collective-permute-start(bf16[1024,512]{1,0:T(8,128)(2,1)} %shard_map.69), channel_id=1, source_target_pairs={{0,1},{1,0},{2,3},{3,2},{4,5},{5,4},{6,7},{7,6},{8,9},{9,8},{10,11... | collective-permute-start | bytes 3145736 | tf_op jit(solution)/shard_map/ppermute | solution.py:394
  25.6 5.4 %collective-permute-done.2.refs_3_ = bf16[512,512]{1,0:T(8,128)(2,1)} collective-permute-done((bf16[512,512]{1,0:T(8,128)(2,1)S(1)}, bf16[512,512]{1,0:T(8,128)(2,1)}, u32[]{:S(2)}, u32[]{:S(2)}) %collective-permute-start.2) | collective-permute-done | bytes 524320 | tf_op jit(solution)/shard_map/ppermute | solution.py:401
  31.0 4.7 %collective-permute-start.9 = (bf16[512,512]{1,0:T(8,128)(2,1)}, bf16[512,512]{1,0:T(8,128)(2,1)}, u32[]{:S(2)}, u32[]{:S(2)}) collective-permute-start(bf16[512,512]{1,0:T(8,128)(2,1)} %collective-permute-done.7.refs_4_.refs_6_.refs_8_), channel_id=1, source_target_pairs={{0,2},{2,4},{4,6},{1,3},{3,5},{5,7},{8,10},{10,12},{12,14},{9,11},... | collective-permute-start | bytes 1572872 | tf_op jit(solution)/shard_map/ppermute | solution.py:400
  35.8 1.3 %collective-permute-start.4 = (bf16[512,512]{1,0:T(8,128)(2,1)}, bf16[512,512]{1,0:T(8,128)(2,1)}, u32[]{:S(2)}, u32[]{:S(2)}) collective-permute-start(bf16[512,512]{1,0:T(8,128)(2,1)} %collective-permute-done.2.refs_3_), channel_id=1, source_target_pairs={{2,0},{4,2},{6,4},{3,1},{5,3},{7,5},{10,8},{12,10},{14,12},{11,9},... | collective-permute-start | bytes 1572872 | tf_op jit(solution)/shard_map/ppermute | solution.py:401
  37.0 5.1 %collective-permute-done.10.refs_9_.refs_11_ = bf16[512,512]{1,0:T(8,128)(2,1)S(1)} collective-permute-done((bf16[512,512]{1,0:T(8,128)(2,1)S(1)}, bf16[512,512]{1,0:T(8,128)(2,1)S(1)}, u32[]{:S(2)}, u32[]{:S(2)}) %collective-permute-start.10) | collective-permute-done | bytes 524320 | tf_op jit(solution)/shard_map/ppermute | solution.py:401
  42.1 4.7 %collective-permute-start.3 = (bf16[512,512]{1,0:T(8,128)(2,1)}, bf16[512,512]{1,0:T(8,128)(2,1)}, u32[]{:S(2)}, u32[]{:S(2)}) collective-permute-start(bf16[512,512]{1,0:T(8,128)(2,1)} %collective-permute-done.1.refs_2_), channel_id=1, source_target_pairs={{0,2},{2,4},{4,6},{1,3},{3,5},{5,7},{8,10},{10,12},{12,14},{9,11},... | collective-permute-start | bytes 1572872 | tf_op jit(solution)/shard_map/ppermute | solution.py:400
  46.8 1.9 %shard_map.70 = bf16[1024,512]{1,0:T(8,128)(2,1)S(1)} custom-call(s32[2,8]{1,0:T(2,128)S(1)} %bitcast.7, bf16[1,1024,2048]{2,1,0:T(8,128)(2,1)} %g_local.7), custom_call_target="tpu_custom_call" | custom-call | tf_op jit(solution)/shard_map/pallas_call | solution.py:147
  48.8 1.6 %collective-permute-start.15 = (bf16[1024,512]{1,0:T(8,128)(2,1)S(1)}, bf16[1024,512]{1,0:T(8,128)(2,1)}, u32[]{:S(2)}, u32[]{:S(2)}) collective-permute-start(bf16[1024,512]{1,0:T(8,128)(2,1)S(1)} %shard_map.70), channel_id=1, source_target_pairs={{0,1},{1,0},{2,3},{3,2},{4,5},{5,4},{6,7},{7,6},{8,9},{9,8},{10,11... | collective-permute-start | bytes 3145736 | tf_op jit(solution)/shard_map/ppermute | solution.py:394
  50.3 0.8 compare_reduce_fusion
  52.4 5.8 %shard_map.71.refs_12_ = f32[1024,512]{1,0:T(8,128)S(1)} custom-call(s32[2,8]{1,0:T(2,128)S(1)} %bitcast.9, bf16[1,1024,2048]{2,1,0:T(8,128)(2,1)} %g_local.7, bf16[512,512]{1,0:T(8,128)(2,1)} %copy-done.4, bf16[512,512]{1,0:T(8,128)(2,1)} %copy-done.3, bf16[512,512]{1,0:T(8,128)(2,1)} %collective-permute-done.1.refs_2_, ...), custom_call_target="tpu_custom_call" | custom-call | tf_op jit(solution)/shard_map/pallas_call | solution.py:261
  58.2 2.0 %collective-permute-done.14.refs_11_.refs_13_.refs_15_ = bf16[1024,512]{1,0:T(8,128)(2,1)} collective-permute-done((bf16[1024,512]{1,0:T(8,128)(2,1)}, bf16[1024,512]{1,0:T(8,128)(2,1)}, u32[]{:S(2)}, u32[]{:S(2)}) %collective-permute-start.14) | collective-permute-done | bytes 1048608 | tf_op jit(solution)/shard_map/ppermute | solution.py:394
  60.2 2.8 %shard_map.72.refs_14_ = f32[1024,512]{1,0:T(8,128)S(1)} custom-call(s32[2,8]{1,0:T(2,128)S(1)} %bitcast.10, bf16[1,1024,2048]{2,1,0:T(8,128)(2,1)} %g_local.7, bf16[512,512]{1,0:T(8,128)(2,1)} %copy-done.4, bf16[512,512]{1,0:T(8,128)(2,1)} %copy-done.3, bf16[512,512]{1,0:T(8,128)(2,1)} %collective-permute-done.1.refs_2_, ...), custom_call_target="tpu_custom_call", output_to_operand_aliasing={{}: (14, {})} | custom-call | tf_op jit(solution)/shard_map/pallas_call | solution.py:261
  63.0 1.3 %collective-permute-start.6 = (bf16[512,512]{1,0:T(8,128)(2,1)}, bf16[512,512]{1,0:T(8,128)(2,1)}, u32[]{:S(2)}, u32[]{:S(2)}) collective-permute-start(bf16[512,512]{1,0:T(8,128)(2,1)} %collective-permute-done.4.refs_5_), channel_id=1, source_target_pairs={{2,0},{4,2},{6,4},{3,1},{5,3},{7,5},{10,8},{12,10},{14,12},{11,9},... | collective-permute-start | bytes 1572872 | tf_op jit(solution)/shard_map/ppermute | solution.py:401
  64.3 5.3 %collective-permute-start.5 = (bf16[512,512]{1,0:T(8,128)(2,1)}, bf16[512,512]{1,0:T(8,128)(2,1)}, u32[]{:S(2)}, u32[]{:S(2)}) collective-permute-start(bf16[512,512]{1,0:T(8,128)(2,1)} %collective-permute-done.3.refs_4_), channel_id=1, source_target_pairs={{0,2},{2,4},{4,6},{1,3},{3,5},{5,7},{8,10},{10,12},{12,14},{9,11},... | collective-permute-start | bytes 1572872 | tf_op jit(solution)/shard_map/ppermute | solution.py:400
  69.6 1.0 conditional.1
  69.6 1.0 broadcast.7
  70.7 1.3 %collective-permute-start.12 = (bf16[512,512]{1,0:T(8,128)(2,1)}, bf16[512,512]{1,0:T(8,128)(2,1)S(1)}, u32[]{:S(2)}, u32[]{:S(2)}) collective-permute-start(bf16[512,512]{1,0:T(8,128)(2,1)} %copy-done.6), channel_id=1, source_target_pairs={{2,0},{4,2},{6,4},{3,1},{5,3},{7,5},{10,8},{12,10},{14,12},{11,9},... | collective-permute-start | bytes 1572872 | tf_op jit(solution)/shard_map/ppermute | solution.py:401
  72.0 4.7 %collective-permute-start.11 = (bf16[512,512]{1,0:T(8,128)(2,1)}, bf16[512,512]{1,0:T(8,128)(2,1)S(1)}, u32[]{:S(2)}, u32[]{:S(2)}) collective-permute-start(bf16[512,512]{1,0:T(8,128)(2,1)} %collective-permute-done.9.refs_8_.refs_10_), channel_id=1, source_target_pairs={{0,2},{2,4},{4,6},{1,3},{3,5},{5,7},{8,10},{10,12},{12,14},{9,11},... | collective-permute-start | bytes 1572872 | tf_op jit(solution)/shard_map/ppermute | solution.py:400
  77.4 2.6 %collective-permute-done.6.refs_7_ = bf16[512,512]{1,0:T(8,128)(2,1)} collective-permute-done((bf16[512,512]{1,0:T(8,128)(2,1)}, bf16[512,512]{1,0:T(8,128)(2,1)}, u32[]{:S(2)}, u32[]{:S(2)}) %collective-permute-start.6) | collective-permute-done | bytes 524320 | tf_op jit(solution)/shard_map/ppermute | solution.py:401
  80.0 1.5 %collective-permute-done.5.refs_6_ = bf16[512,512]{1,0:T(8,128)(2,1)} collective-permute-done((bf16[512,512]{1,0:T(8,128)(2,1)}, bf16[512,512]{1,0:T(8,128)(2,1)}, u32[]{:S(2)}, u32[]{:S(2)}) %collective-permute-start.5) | collective-permute-done | bytes 524320 | tf_op jit(solution)/shard_map/ppermute | solution.py:400
  81.5 0.9 shard_map.73.refs_18_
  82.4 5.0 %collective-permute-done.12.refs_13_ = bf16[512,512]{1,0:T(8,128)(2,1)S(1)} collective-permute-done((bf16[512,512]{1,0:T(8,128)(2,1)}, bf16[512,512]{1,0:T(8,128)(2,1)S(1)}, u32[]{:S(2)}, u32[]{:S(2)}) %collective-permute-start.12) | collective-permute-done | bytes 524320 | tf_op jit(solution)/shard_map/ppermute | solution.py:401
  87.5 1.3 %collective-permute-done.11.refs_12_ = bf16[512,512]{1,0:T(8,128)(2,1)S(1)} collective-permute-done((bf16[512,512]{1,0:T(8,128)(2,1)}, bf16[512,512]{1,0:T(8,128)(2,1)S(1)}, u32[]{:S(2)}, u32[]{:S(2)}) %collective-permute-start.11) | collective-permute-done | bytes 524320 | tf_op jit(solution)/shard_map/ppermute | solution.py:400
  88.8 0.8 copy-done.8
  89.6 4.0 %late.1 = (f32[128,512]{1,0:T(8,128)S(1)}, bf16[128,512]{1,0:T(8,128)(2,1)S(1)}, bf16[128,512]{1,0:T(8,128)(2,1)S(1)}, bf16[128,512]{1,0:T(8,128)(2,1)S(1)}, f32...) custom-call(s32[2,8]{1,0:T(2,128)S(1)} %bitcast.13, f32[1]{0:T(128)S(6)} %copy.13.weight, ...), custom_call_target="tpu_custom_call" | custom-call | tf_op jit(solution)/shard_map/late/pallas_call | solution.py:329
  93.7 0.5 collective-permute-start.18
  94.2 1.4 %collective-permute-start.19 = (bf16[128,512]{1,0:T(8,128)(2,1)S(1)}, bf16[128,512]{1,0:T(8,128)(2,1)S(1)}, u32[]{:S(2)}, u32[]{:S(2)}) collective-permute-start(bf16[128,512]{1,0:T(8,128)(2,1)S(1)} %get-tuple-element.37), channel_id=1, source_target_pairs={{0,16},{8,24},{16,0},{24,8},{1,17},{9,25},{17,1},{25,9},{2,18},{10... | collective-permute-start | bytes 393224 | tf_op jit(solution)/shard_map/ppermute | solution.py:436
  95.6 0.2 collective-permute-done.18.refs_0_
  95.8 4.8 %collective-permute-done.19.refs_1_ = bf16[128,512]{1,0:T(8,128)(2,1)S(1)} collective-permute-done((bf16[128,512]{1,0:T(8,128)(2,1)S(1)}, bf16[128,512]{1,0:T(8,128)(2,1)S(1)}, u32[]{:S(2)}, u32[]{:S(2)}) %collective-permute-start.19) | collective-permute-done | bytes 131104 | tf_op jit(solution)/shard_map/ppermute | solution.py:436
  100.5 1.0 collective-permute-done.20.refs_2_
  101.6 0.6 collective-permute-start.21
  102.3 6.0 %collective-permute-start.22 = (bf16[32,512]{1,0:T(8,128)(2,1)S(1)}, bf16[32,512]{1,0:T(8,128)(2,1)S(1)}, u32[]{:S(2)}, u32[]{:S(2)}) collective-permute-start(bf16[32,512]{1,0:T(8,128)(2,1)S(1)} %get-tuple-element.41), channel_id=1, source_target_pairs={{0,4},{2,6},{4,0},{6,2},{1,5},{3,7},{5,1},{7,3},{8,12},{10,14},{12... | collective-permute-start | bytes 98312 | tf_op jit(solution)/shard_map/ppermute | solution.py:436
  108.2 0.1 shard_map.74
  108.3 1.6 %collective-permute-start.17 = (bf16[256,512]{1,0:T(8,128)(2,1)S(1)}, bf16[256,512]{1,0:T(8,128)(2,1)S(1)}, u32[]{:S(2)}, u32[]{:S(2)}) collective-permute-start(bf16[256,512]{1,0:T(8,128)(2,1)S(1)} %get-tuple-element.34), channel_id=1, source_target_pairs={{0,16},{8,24},{16,0},{24,8},{1,17},{9,25},{17,1},{25,9},{2,18},{10... | collective-permute-start | bytes 786440 | tf_op jit(solution)/shard_map/ppermute | solution.py:436
  109.9 1.4 %collective-permute-done.22 = bf16[32,512]{1,0:T(8,128)(2,1)S(1)} collective-permute-done((bf16[32,512]{1,0:T(8,128)(2,1)S(1)}, bf16[32,512]{1,0:T(8,128)(2,1)S(1)}, u32[]{:S(2)}, u32[]{:S(2)}) %collective-permute-start.22) | collective-permute-done | bytes 32800 | tf_op jit(solution)/shard_map/ppermute | solution.py:436
  111.3 0.8 collective-permute-done.23
  112.1 0.6 convert_add_fusion.1
  112.8 4.0 %collective-permute-done.17 = bf16[256,512]{1,0:T(8,128)(2,1)S(1)} collective-permute-done((bf16[256,512]{1,0:T(8,128)(2,1)S(1)}, bf16[256,512]{1,0:T(8,128)(2,1)S(1)}, u32[]{:S(2)}, u32[]{:S(2)}) %collective-permute-start.17) | collective-permute-done | bytes 262176 | tf_op jit(solution)/shard_map/ppermute | solution.py:436
  116.8 0.9 convert_add_fusion
  (33 shorter events, 0.3 us)
Async XLA Ops:
  0.6 9.0 %copy-start.9 = (s32[8,2]{0,1:T(2,128)S(1)}, s32[8,2]{0,1:T(2,128)}, u32[]{:S(2)}) copy-start(s32[8,2]{0,1:T(2,128)} %param.11) | copy-start | bytes 196
  1.9 9.6 %copy-start.3 = (bf16[512,512]{1,0:T(8,128)(2,1)}, bf16[512,512]{1,0:T(8,128)(2,1)S(1)}, u32[]{:S(2)}) copy-start(bf16[512,512]{1,0:T(8,128)(2,1)S(1)} %get-tuple-element.45.refs_1_) | copy-start | bytes 1572868
  1.9 12.9 %copy-start.4 = (bf16[512,512]{1,0:T(8,128)(2,1)}, bf16[512,512]{1,0:T(8,128)(2,1)S(1)}, u32[]{:S(2)}) copy-start(bf16[512,512]{1,0:T(8,128)(2,1)S(1)} %get-tuple-element.46.refs_0_) | copy-start | bytes 1572868
  1.9 18.3 %collective-permute-start.8 = (bf16[512,512]{1,0:T(8,128)(2,1)S(1)}, bf16[512,512]{1,0:T(8,128)(2,1)S(1)}, u32[]{:S(2)}, u32[]{:S(2)}) collective-permute-start(bf16[512,512]{1,0:T(8,128)(2,1)S(1)} %get-tuple-element.45.refs_1_), channel_id=1, source_target_pairs={{2,0},{4,2},{6,4},{3,1},{5,3},{7,5},{10,8},{12,10},{14,12},{11,9},... | collective-permute-start | bytes 1572872 | tf_op jit(solution)/shard_map/ppermute | solution.py:401
  3.2 20.9 %collective-permute-start.7 = (bf16[512,512]{1,0:T(8,128)(2,1)S(1)}, bf16[512,512]{1,0:T(8,128)(2,1)}, u32[]{:S(2)}, u32[]{:S(2)}) collective-permute-start(bf16[512,512]{1,0:T(8,128)(2,1)S(1)} %get-tuple-element.45.refs_1_), channel_id=1, source_target_pairs={{0,2},{2,4},{4,6},{1,3},{3,5},{5,7},{8,10},{10,12},{12,14},{9,11},... | collective-permute-start | bytes 1572872 | tf_op jit(solution)/shard_map/ppermute | solution.py:400
  11.5 37.2 %collective-permute-start.13 = (bf16[1024,512]{1,0:T(8,128)(2,1)S(1)}, bf16[1024,512]{1,0:T(8,128)(2,1)S(1)}, u32[]{:S(2)}, u32[]{:S(2)}) collective-permute-start(bf16[1024,512]{1,0:T(8,128)(2,1)S(1)} %shard_map.68), channel_id=1, source_target_pairs={{0,1},{1,0},{2,3},{3,2},{4,5},{5,4},{6,7},{7,6},{8,9},{9,8},{10,11... | collective-permute-start | bytes 3145736 | tf_op jit(solution)/shard_map/ppermute | solution.py:394
  13.6 17.4 %collective-permute-start.2 = (bf16[512,512]{1,0:T(8,128)(2,1)S(1)}, bf16[512,512]{1,0:T(8,128)(2,1)}, u32[]{:S(2)}, u32[]{:S(2)}) collective-permute-start(bf16[512,512]{1,0:T(8,128)(2,1)S(1)} %get-tuple-element.46.refs_0_), channel_id=1, source_target_pairs={{2,0},{4,2},{6,4},{3,1},{5,3},{7,5},{10,8},{12,10},{14,12},{11,9},... | collective-permute-start | bytes 1572872 | tf_op jit(solution)/shard_map/ppermute | solution.py:401
  14.9 20.9 %collective-permute-start.1 = (bf16[512,512]{1,0:T(8,128)(2,1)S(1)}, bf16[512,512]{1,0:T(8,128)(2,1)}, u32[]{:S(2)}, u32[]{:S(2)}) collective-permute-start(bf16[512,512]{1,0:T(8,128)(2,1)S(1)} %get-tuple-element.46.refs_0_), channel_id=1, source_target_pairs={{0,2},{2,4},{4,6},{1,3},{3,5},{5,7},{8,10},{10,12},{12,14},{9,11},... | collective-permute-start | bytes 1572872 | tf_op jit(solution)/shard_map/ppermute | solution.py:400
  20.2 3.9 %copy-start.5 = (bf16[512,512]{1,0:T(8,128)(2,1)}, bf16[512,512]{1,0:T(8,128)(2,1)S(1)}, u32[]{:S(2)}) copy-start(bf16[512,512]{1,0:T(8,128)(2,1)S(1)} %collective-permute-done.8.refs_5_.refs_7_.refs_9_) | copy-start | bytes 1572868
  20.2 21.9 %collective-permute-start.10 = (bf16[512,512]{1,0:T(8,128)(2,1)S(1)}, bf16[512,512]{1,0:T(8,128)(2,1)S(1)}, u32[]{:S(2)}, u32[]{:S(2)}) collective-permute-start(bf16[512,512]{1,0:T(8,128)(2,1)S(1)} %collective-permute-done.8.refs_5_.refs_7_.refs_9_), channel_id=1, source_target_pairs={{2,0},{4,2},{6,4},{3,1},{5,3},{7,5},{10,8},{12,10},{14,12},{11,9},... | collective-permute-start | bytes 1572872 | tf_op jit(solution)/shard_map/ppermute | solution.py:401
  24.2 36.1 %collective-permute-start.14 = (bf16[1024,512]{1,0:T(8,128)(2,1)}, bf16[1024,512]{1,0:T(8,128)(2,1)}, u32[]{:S(2)}, u32[]{:S(2)}) collective-permute-start(bf16[1024,512]{1,0:T(8,128)(2,1)} %shard_map.69), channel_id=1, source_target_pairs={{0,1},{1,0},{2,3},{3,2},{4,5},{5,4},{6,7},{7,6},{8,9},{9,8},{10,11... | collective-permute-start | bytes 3145736 | tf_op jit(solution)/shard_map/ppermute | solution.py:394
  31.0 27.2 %collective-permute-start.9 = (bf16[512,512]{1,0:T(8,128)(2,1)}, bf16[512,512]{1,0:T(8,128)(2,1)}, u32[]{:S(2)}, u32[]{:S(2)}) collective-permute-start(bf16[512,512]{1,0:T(8,128)(2,1)} %collective-permute-done.7.refs_4_.refs_6_.refs_8_), channel_id=1, source_target_pairs={{0,2},{2,4},{4,6},{1,3},{3,5},{5,7},{8,10},{10,12},{12,14},{9,11},... | collective-permute-start | bytes 1572872 | tf_op jit(solution)/shard_map/ppermute | solution.py:400
  35.8 22.4 %collective-permute-start.4 = (bf16[512,512]{1,0:T(8,128)(2,1)}, bf16[512,512]{1,0:T(8,128)(2,1)}, u32[]{:S(2)}, u32[]{:S(2)}) collective-permute-start(bf16[512,512]{1,0:T(8,128)(2,1)} %collective-permute-done.2.refs_3_), channel_id=1, source_target_pairs={{2,0},{4,2},{6,4},{3,1},{5,3},{7,5},{10,8},{12,10},{14,12},{11,9},... | collective-permute-start | bytes 1572872 | tf_op jit(solution)/shard_map/ppermute | solution.py:401
  42.1 6.6 %copy-start.6 = (bf16[512,512]{1,0:T(8,128)(2,1)}, bf16[512,512]{1,0:T(8,128)(2,1)S(1)}, u32[]{:S(2)}) copy-start(bf16[512,512]{1,0:T(8,128)(2,1)S(1)} %collective-permute-done.10.refs_9_.refs_11_) | copy-start | bytes 1572868
  42.1 16.1 %collective-permute-start.3 = (bf16[512,512]{1,0:T(8,128)(2,1)}, bf16[512,512]{1,0:T(8,128)(2,1)}, u32[]{:S(2)}, u32[]{:S(2)}) collective-permute-start(bf16[512,512]{1,0:T(8,128)(2,1)} %collective-permute-done.1.refs_2_), channel_id=1, source_target_pairs={{0,2},{2,4},{4,6},{1,3},{3,5},{5,7},{8,10},{10,12},{12,14},{9,11},... | collective-permute-start | bytes 1572872 | tf_op jit(solution)/shard_map/ppermute | solution.py:400
  48.7 1.6 %copy-start.2 = (bf16[1024,512]{1,0:T(8,128)(2,1)}, bf16[1024,512]{1,0:T(8,128)(2,1)S(1)}, u32[]{:S(2)}) copy-start(bf16[1024,512]{1,0:T(8,128)(2,1)S(1)} %collective-permute-done.13.refs_6_.refs_10_.refs_12_.refs_14_) | copy-start | bytes 3145732
  48.8 33.7 %collective-permute-start.15 = (bf16[1024,512]{1,0:T(8,128)(2,1)S(1)}, bf16[1024,512]{1,0:T(8,128)(2,1)}, u32[]{:S(2)}, u32[]{:S(2)}) collective-permute-start(bf16[1024,512]{1,0:T(8,128)(2,1)S(1)} %shard_map.70), channel_id=1, source_target_pairs={{0,1},{1,0},{2,3},{3,2},{4,5},{5,4},{6,7},{7,6},{8,9},{9,8},{10,11... | collective-permute-start | bytes 3145736 | tf_op jit(solution)/shard_map/ppermute | solution.py:394
  63.0 17.0 %collective-permute-start.6 = (bf16[512,512]{1,0:T(8,128)(2,1)}, bf16[512,512]{1,0:T(8,128)(2,1)}, u32[]{:S(2)}, u32[]{:S(2)}) collective-permute-start(bf16[512,512]{1,0:T(8,128)(2,1)} %collective-permute-done.4.refs_5_), channel_id=1, source_target_pairs={{2,0},{4,2},{6,4},{3,1},{5,3},{7,5},{10,8},{12,10},{14,12},{11,9},... | collective-permute-start | bytes 1572872 | tf_op jit(solution)/shard_map/ppermute | solution.py:401
  64.3 17.2 %collective-permute-start.5 = (bf16[512,512]{1,0:T(8,128)(2,1)}, bf16[512,512]{1,0:T(8,128)(2,1)}, u32[]{:S(2)}, u32[]{:S(2)}) collective-permute-start(bf16[512,512]{1,0:T(8,128)(2,1)} %collective-permute-done.3.refs_4_), channel_id=1, source_target_pairs={{0,2},{2,4},{4,6},{1,3},{3,5},{5,7},{8,10},{10,12},{12,14},{9,11},... | collective-permute-start | bytes 1572872 | tf_op jit(solution)/shard_map/ppermute | solution.py:400
  70.7 16.8 %collective-permute-start.12 = (bf16[512,512]{1,0:T(8,128)(2,1)}, bf16[512,512]{1,0:T(8,128)(2,1)S(1)}, u32[]{:S(2)}, u32[]{:S(2)}) collective-permute-start(bf16[512,512]{1,0:T(8,128)(2,1)} %copy-done.6), channel_id=1, source_target_pairs={{2,0},{4,2},{6,4},{3,1},{5,3},{7,5},{10,8},{12,10},{14,12},{11,9},... | collective-permute-start | bytes 1572872 | tf_op jit(solution)/shard_map/ppermute | solution.py:401
  72.0 16.8 %collective-permute-start.11 = (bf16[512,512]{1,0:T(8,128)(2,1)}, bf16[512,512]{1,0:T(8,128)(2,1)S(1)}, u32[]{:S(2)}, u32[]{:S(2)}) collective-permute-start(bf16[512,512]{1,0:T(8,128)(2,1)} %collective-permute-done.9.refs_8_.refs_10_), channel_id=1, source_target_pairs={{0,2},{2,4},{4,6},{1,3},{3,5},{5,7},{8,10},{10,12},{12,14},{9,11},... | collective-permute-start | bytes 1572872 | tf_op jit(solution)/shard_map/ppermute | solution.py:400
  77.4 12.2 %copy-start = (bf16[1,1024,512]{2,1,0:T(8,128)(2,1)S(1)}, bf16[1,1024,512]{2,1,0:T(8,128)(2,1)}, u32[]{:S(2)}) copy-start(bf16[1,1024,512]{2,1,0:T(8,128)(2,1)} %refs_19_.1) | copy-start | bytes 3145732
  77.4 12.2 %copy-start.1 = (bf16[1,128,512]{2,1,0:T(8,128)(2,1)S(1)}, bf16[1,128,512]{2,1,0:T(8,128)(2,1)}, u32[]{:S(2)}) copy-start(bf16[1,128,512]{2,1,0:T(8,128)(2,1)} %refs_20_.1) | copy-start | bytes 393220
  87.5 1.3 %copy-start.7 = (bf16[512,512]{1,0:T(8,128)(2,1)}, bf16[512,512]{1,0:T(8,128)(2,1)S(1)}, u32[]{:S(2)}) copy-start(bf16[512,512]{1,0:T(8,128)(2,1)S(1)} %collective-permute-done.12.refs_13_) | copy-start | bytes 1572868
  88.8 0.8 copy-start.8
  93.6 14.6 %collective-permute-start.16 = (bf16[512,512]{1,0:T(8,128)(2,1)S(1)}, bf16[512,512]{1,0:T(8,128)(2,1)S(1)}, u32[]{:S(2)}, u32[]{:S(2)}) collective-permute-start(bf16[512,512]{1,0:T(8,128)(2,1)S(1)} %get-tuple-element.32), channel_id=1, source_target_pairs={{0,8},{8,0},{16,24},{24,16},{1,9},{9,1},{17,25},{25,17},{2,10},{10... | collective-permute-start | bytes 1572872 | tf_op jit(solution)/shard_map/ppermute | solution.py:436
  93.7 2.1 %collective-permute-start.18 = (bf16[128,512]{1,0:T(8,128)(2,1)S(1)}, bf16[128,512]{1,0:T(8,128)(2,1)S(1)}, u32[]{:S(2)}, u32[]{:S(2)}) collective-permute-start(bf16[128,512]{1,0:T(8,128)(2,1)S(1)} %get-tuple-element.36), channel_id=1, source_target_pairs={{0,8},{8,0},{16,24},{24,16},{1,9},{9,1},{17,25},{25,17},{2,10},{10... | collective-permute-start | bytes 393224 | tf_op jit(solution)/shard_map/ppermute | solution.py:436
  94.2 6.4 %collective-permute-start.19 = (bf16[128,512]{1,0:T(8,128)(2,1)S(1)}, bf16[128,512]{1,0:T(8,128)(2,1)S(1)}, u32[]{:S(2)}, u32[]{:S(2)}) collective-permute-start(bf16[128,512]{1,0:T(8,128)(2,1)S(1)} %get-tuple-element.37), channel_id=1, source_target_pairs={{0,16},{8,24},{16,0},{24,8},{1,17},{9,25},{17,1},{25,9},{2,18},{10... | collective-permute-start | bytes 393224 | tf_op jit(solution)/shard_map/ppermute | solution.py:436
  95.5 6.0 %collective-permute-start.20 = (bf16[128,512]{1,0:T(8,128)(2,1)S(1)}, bf16[128,512]{1,0:T(8,128)(2,1)S(1)}, u32[]{:S(2)}, u32[]{:S(2)}) collective-permute-start(bf16[128,512]{1,0:T(8,128)(2,1)S(1)} %get-tuple-element.38), channel_id=1, source_target_pairs={{0,24},{8,16},{16,8},{24,0},{1,25},{9,17},{17,9},{25,1},{2,26},{10... | collective-permute-start | bytes 393224 | tf_op jit(solution)/shard_map/ppermute | solution.py:436
  101.6 8.3 %collective-permute-start.21 = (bf16[32,512]{1,0:T(8,128)(2,1)S(1)}, bf16[32,512]{1,0:T(8,128)(2,1)S(1)}, u32[]{:S(2)}, u32[]{:S(2)}) collective-permute-start(bf16[32,512]{1,0:T(8,128)(2,1)S(1)} %get-tuple-element.40), channel_id=1, source_target_pairs={{0,2},{2,4},{4,6},{6,0},{1,3},{3,5},{5,7},{7,1},{8,10},{10,12},{12... | collective-permute-start | bytes 98312 | tf_op jit(solution)/shard_map/ppermute | solution.py:436
  102.3 9.1 %collective-permute-start.22 = (bf16[32,512]{1,0:T(8,128)(2,1)S(1)}, bf16[32,512]{1,0:T(8,128)(2,1)S(1)}, u32[]{:S(2)}, u32[]{:S(2)}) collective-permute-start(bf16[32,512]{1,0:T(8,128)(2,1)S(1)} %get-tuple-element.41), channel_id=1, source_target_pairs={{0,4},{2,6},{4,0},{6,2},{1,5},{3,7},{5,1},{7,3},{8,12},{10,14},{12... | collective-permute-start | bytes 98312 | tf_op jit(solution)/shard_map/ppermute | solution.py:436
  108.2 3.9 %collective-permute-start.23 = (bf16[32,512]{1,0:T(8,128)(2,1)S(1)}, bf16[32,512]{1,0:T(8,128)(2,1)S(1)}, u32[]{:S(2)}, u32[]{:S(2)}) collective-permute-start(bf16[32,512]{1,0:T(8,128)(2,1)S(1)} %get-tuple-element.42), channel_id=1, source_target_pairs={{0,6},{2,0},{4,2},{6,4},{1,7},{3,1},{5,3},{7,5},{8,14},{10,8},{12,... | collective-permute-start | bytes 98312 | tf_op jit(solution)/shard_map/ppermute | solution.py:436
  108.3 8.4 %collective-permute-start.17 = (bf16[256,512]{1,0:T(8,128)(2,1)S(1)}, bf16[256,512]{1,0:T(8,128)(2,1)S(1)}, u32[]{:S(2)}, u32[]{:S(2)}) collective-permute-start(bf16[256,512]{1,0:T(8,128)(2,1)S(1)} %get-tuple-element.34), channel_id=1, source_target_pairs={{0,16},{8,24},{16,0},{24,8},{1,17},{9,25},{17,1},{25,9},{2,18},{10... | collective-permute-start | bytes 786440 | tf_op jit(solution)/shard_map/ppermute | solution.py:436

commit v3 on v2

--- a/solution.py
+++ b/solution.py
@@ -117,7 +117,7 @@
         n = jnp.int32(0)
         for i in range(sz.half):
             if i != j:
-                before = dist[i] <= dist[j] if i < j else dist[i] < dist[j]
+                before = dist[i] > dist[j] if i < j else dist[i] >= dist[j]
                 n = n + jnp.where(before, need[i], 0)
         rank.append(n)
     return need, rank
@@ -279,62 +279,144 @@
             for x in range(sz.outer) for c in range(sz.cores)]
 
 
-def late_kernel(sz, ready, before, keys, n_slots, pat, weight, g_local, *refs):
+def far_block(sz, row):
+    far = jnp.where(row < sz.rows // 2, sz.rows - 1, 0)
+    return far * sz.per_row + sz.per_row - 1
+
+
+def inner_kernel(sz, pat, green, slot, factor, out, g_buf, sem):
+    row, col = lax.axis_index("row"), lax.axis_index("col")
+    a = far_block(sz, row)
+
+    @pl.when(a // sz.half == col)
+    def _():
+        at = pl.multiple_of(lax.rem(a, sz.half) * sz.block, sz.block)
+        pltpu.make_async_copy(green.at[0, :, pl.ds(at, sz.block)], g_buf, sem).start()
+
+    @pl.when(a // sz.half != col)
+    def _():
+        pltpu.make_async_copy(slot, g_buf, sem).start()
+
+    pltpu.make_async_copy(g_buf, g_buf, sem).wait()
+    total = jnp.zeros((sz.width, sz.block), F32)
+    for e in range(sz.per_row):
+        at = pl.ds(e * sz.block, sz.block)
+        kept = pat[col, row * sz.per_row + e] > 0
+        part = lax.dot_general(factor[0, at, :], g_buf[at, :], (((0,), (0,)), ((), ())), preferred_element_type=F32)
+        total = total + jnp.where(kept, part, 0.0)
+    out[...] = total.astype(BF16)
+
+
+def inner(sz, pattern, green, slot, factor):
+    return pl.pallas_call(
+        functools.partial(inner_kernel, sz),
+        out_shape=jax.ShapeDtypeStruct((sz.width, sz.block), BF16),
+        in_specs=[SMEM, ANY, ANY, VMEM],
+        out_specs=VMEM,
+        scratch_shapes=[pltpu.VMEM((sz.local_rows, sz.block), BF16), pltpu.SemaphoreType.DMA],
+        compiler_params=SMALL,
+        name="inner",
+    )(pattern, *in_hbm([green, slot]), factor)
+
+
+def late_diag_kernel(sz, ready, before, keys, n_slots, pat, weight, g_local, *refs):
     refs = list(refs)
     m_refs = {k: refs.pop(0) for k in keys}
     g_slots = [refs.pop(0) for _ in range(n_slots)]
-    total_in, factor, dinv = refs.pop(0), refs.pop(0), refs.pop(0)
-    diag_out = [refs.pop(0) for _ in range(sz.poles)]
-    off_out = [refs.pop(0) for _ in range(sz.cores)]
+    total_in, factor, dinv, far_term = (refs.pop(0) for _ in range(4))
+    outs = [refs.pop(0) for _ in range(sz.poles)]
     total, diag = refs.pop(0), refs.pop(0)
     job, m_buf, g_buf, m_sem, g_sem = refs
     row, col, pole = (lax.axis_index(a) for a in ("row", "col", "pole"))
     core, x_at = lax.rem(pole, sz.cores), pole // sz.cores
+
+    away = sz.rows - 2
+    for at_row, sign in ((1, 1), (sz.rows - 2, -1)):
+        key = sign * away * sz.per_row + sz.per_row - 1
+
+        @pl.when(row == at_row)
+        def _(key=key):
+            copy = pltpu.make_async_copy(m_refs[key], m_buf.at[0], m_sem.at[0])
+            copy.start()
+            copy.wait()
+
+    inward = jnp.logical_or(row == 1, row == sz.rows - 2)
+    a = far_block(sz, row)
+    w = weight[0]
+    diag[...] = jnp.zeros_like(diag)
+
+    @pl.when(jnp.logical_and(inward, pat[col, a] > 0))
+    def _():
+        diag[...] -= w * jnp.dot(far_term[...], m_buf[0], preferred_element_type=F32)
+
+    total[...] = total_in[...]
+    product_jobs(sz, pat, ready, before, m_refs, g_local, g_slots, job, (m_buf, g_buf, m_sem, g_sem), total)
+    for e in range(sz.per_row):
+        at = pl.ds(e * sz.block, sz.block)
+
+        @pl.when(pat[col, row * sz.per_row + e] > 0)
+        def _(at=at):
+            diag[...] -= w * lax.dot_general(
+                factor[0, at, :], total[at, :].astype(BF16), (((0,), (0,)), ((), ())), preferred_element_type=F32)
+
+    mine = pl.ds(pl.multiple_of(row * sz.count, sz.count), sz.count)
+    diag[mine, :] += w * dinv[0].astype(F32)
+    n = diag.shape[0] // sz.poles
+    for (dx, dc), out in zip([(0, 0)] + pole_steps(sz), outs):
+        q = lax.rem(x_at + dx, sz.outer) * sz.cores + lax.rem(core + dc, sz.cores)
+        out[...] = diag[pl.ds(pl.multiple_of(q * n, n), n), :].astype(out.dtype)
+
+
+def late_diag(sz, ready, before, pattern, weight, green, m, slots, total, factor, dinv, far_term):
+    keys = list(m)
+    args = [pattern, weight] + in_hbm([green] + [m[k] for k in keys] + list(slots)) + [total, factor, dinv, far_term]
+    shapes = [jax.ShapeDtypeStruct((sz.block // sz.poles, sz.width), BF16 if i else F32) for i in range(sz.poles)]
+    shapes.append(jax.ShapeDtypeStruct((sz.local_rows, sz.width), F32))
+    return pl.pallas_call(
+        functools.partial(late_diag_kernel, sz, ready, before, keys, len(slots)),
+        out_shape=shapes,
+        in_specs=[SMEM] * 2 + [ANY] * (1 + len(keys) + len(slots)) + [VMEM] * 4,
+        out_specs=[VMEM] * (sz.poles + 1),
+        scratch_shapes=[pltpu.VMEM((sz.block, sz.width), F32)] + job_scratch(sz),
+        compiler_params=SMALL,
+        name="late_diag",
+    )(*args)
+
+
+def late_off_kernel(sz, ready, before, keys, n_slots, pat, weight, g_local, *refs):
+    refs = list(refs)
+    m_refs = {k: refs.pop(0) for k in keys}
+    g_slots = [refs.pop(0) for _ in range(n_slots)]
+    total_in = refs.pop(0)
+    outs = [refs.pop(0) for _ in range(sz.cores)]
+    total = refs.pop(0)
+    job, m_buf, g_buf, m_sem, g_sem = refs
+    row, col = lax.axis_index("row"), lax.axis_index("col")
+    core = lax.rem(lax.axis_index("pole"), sz.cores)
     total[...] = total_in[...]
     product_jobs(sz, pat, ready, before, m_refs, g_local, g_slots, job, (m_buf, g_buf, m_sem, g_sem), total)
     w = weight[0]
-    diag[...] = jnp.zeros_like(diag)
-    for e in range(sz.per_row):
-        at = pl.ds(e * sz.block, sz.block)
-        kept = pat[col, row * sz.per_row + e] > 0
-
-        @pl.when(kept)
-        def _(at=at):
-            update = total[at, :]
-            diag[...] -= w * lax.dot_general(
-                factor[0, at, :], update.astype(BF16), (((0,), (0,)), ((), ())), preferred_element_type=F32)
-            total[at, :] = -w * update
-
-        @pl.when(jnp.logical_not(kept))
-        def _(at=at):
-            total[at, :] = jnp.zeros((sz.block, sz.width), F32)
-    mine = pl.ds(pl.multiple_of(row * sz.count, sz.count), sz.count)
-    diag[mine, :] += w * dinv[0].astype(F32)
-    n = diag.shape[0] // sz.poles
-    for (dx, dc), out in zip([(0, 0)] + pole_steps(sz), diag_out):
-        q = lax.rem(x_at + dx, sz.outer) * sz.cores + lax.rem(core + dc, sz.cores)
-        out[...] = diag[pl.ds(pl.multiple_of(q * n, n), n), :].astype(out.dtype)
     n = total.shape[0] // sz.poles
-    for dc, out in enumerate(off_out):
+    for dc, out in enumerate(outs):
         for x in range(sz.outer):
             q = x * sz.cores + lax.rem(core + dc, sz.cores)
-            out[x * n:(x + 1) * n, :] = total[pl.ds(pl.multiple_of(q * n, n), n), :].astype(out.dtype)
-
-
-def late(sz, ready, before, pattern, weight, green, m, slots, total, factor, dinv):
+            kept = pat[col, row * sz.per_row + (q * n) // sz.block] > 0
+            v = total[pl.ds(pl.multiple_of(q * n, n), n), :]
+            out[x * n:(x + 1) * n, :] = jnp.where(kept, -w * v, 0.0).astype(out.dtype)
+
+
+def late_off(sz, ready, before, pattern, weight, green, m, slots, total):
     keys = list(m)
-    args = [pattern, weight] + in_hbm([green] + [m[k] for k in keys] + list(slots)) + [total, factor, dinv]
-    shapes = [jax.ShapeDtypeStruct((sz.block // sz.poles, sz.width), BF16 if i else F32) for i in range(sz.poles)]
-    shapes += [jax.ShapeDtypeStruct((sz.local_rows // sz.cores, sz.width), BF16 if i else F32) for i in range(sz.cores)]
+    args = [pattern, weight] + in_hbm([green] + [m[k] for k in keys] + list(slots)) + [total]
+    shapes = [jax.ShapeDtypeStruct((sz.local_rows // sz.cores, sz.width), BF16 if i else F32) for i in range(sz.cores)]
     return pl.pallas_call(
-        functools.partial(late_kernel, sz, ready, before, keys, len(slots)),
+        functools.partial(late_off_kernel, sz, ready, before, keys, len(slots)),
         out_shape=shapes,
-        in_specs=[SMEM] * 2 + [ANY] * (1 + len(keys) + len(slots)) + [VMEM] * 3,
-        out_specs=[VMEM] * (sz.poles + sz.cores),
-        scratch_shapes=[pltpu.VMEM((sz.local_rows, sz.width), F32), pltpu.VMEM((sz.block, sz.width), F32)]
-        + job_scratch(sz),
+        in_specs=[SMEM] * 2 + [ANY] * (1 + len(keys) + len(slots)) + [VMEM],
+        out_specs=[VMEM] * sz.cores,
+        scratch_shapes=[pltpu.VMEM((sz.local_rows, sz.width), F32)] + job_scratch(sz),
         compiler_params=SMALL,
-        name="late",
+        name="late_off",
     )(*args)
 
 
@@ -383,8 +465,6 @@
     block, per_row = sz.block, sz.per_row
     pattern = pattern.T
     fac = [factor[0, e * block:(e + 1) * block] for e in range(per_row)]
-    right = [(i, i + 1) for i in range(sz.rows - 1)]
-    left = [(i + 1, i) for i in range(sz.rows - 1)]
     swap = [(0, 1), (1, 0)]
 
     fixed = max(sz.half - 1, 1)
@@ -397,21 +477,23 @@
     for e in range(per_row):
         a = b = fac[e]
         for step in range(1, sz.rows):
-            m[-step * per_row + e] = a = lax.ppermute(a, "row", right)
-            m[step * per_row + e] = b = lax.ppermute(b, "row", left)
+            m[-step * per_row + e] = a = lax.ppermute(a, "row", [(i, i + 1) for i in range(step - 1, sz.rows - 1)])
+            m[step * per_row + e] = b = lax.ppermute(b, "row", [(i + 1, i) for i in range(sz.rows - step)])
 
     def upto(dist, last_e):
         return {k: v for k, v in m.items() if abs(k // per_row) < dist or (abs(k // per_row) == dist and k % per_row <= last_e)}
 
     far = sz.rows - 1
-    bounds = [(far - 2, per_row - 1, 0), (far - 1, per_row - 1, fixed - 2), (far, per_row - 2, fixed - 2)]
+    bounds = [(far - 1, per_row - 1, fixed - 2), (far, per_row - 2, fixed - 2)]
+    far_term = inner(sz, pattern, green, slots[0], factor)
+    far_term = lax.ppermute(far_term, "row", [(0, 1), (far, far - 1)])
 
     def part(i, total):
         dist, last_e, s = bounds[i]
         return early(sz, bounds[i], bounds[i - 1] if i else None, pattern, green,
                      upto(dist, last_e), slots[:s + 1], total)
 
-    total = part(1, part(0, None))
+    total = part(0, None)
     extra = []
     if sz.half > fixed:
         full = jnp.bool_(False)
@@ -426,9 +508,13 @@
         got = lax.cond(full, more, lambda g: jnp.zeros((sz.local_rows, block), BF16), green)
         got, total = lax.optimization_barrier((got, total))
         extra.append(got)
-    total = part(2, total)
-    out = late(sz, (far, per_row - 1, sz.half), bounds[2], pattern, pole_weight, green, m,
-               slots + extra, total, factor, diag_inverse)
+    total = part(1, total)
+    near = (far, per_row - 2, sz.half)
+    *out, total = late_diag(sz, near, bounds[1], pattern, pole_weight, green, upto(far, per_row - 2),
+                            slots + extra, total, factor, diag_inverse, far_term)
+    last = (far, per_row - 1, sz.half)
+    only = {k: v for k, v in m.items() if abs(k // per_row) == far and k % per_row == per_row - 1}
+    off_out = late_off(sz, last, near, pattern, pole_weight, green, only, slots + extra, total)
 
     def swapped(axis, sends, perms):
         ins = []
@@ -436,9 +522,9 @@
             ins.append(lax.ppermute(v, axis, perm))
         return ins
 
-    diag, *sends = out[:sz.poles]
+    diag, *sends = out
     diag_in = swapped("pole", sends, [pole_perm(sz, step) for step in pole_steps(sz)])
-    off, *sends = out[sz.poles:]
+    off, *sends = off_out
     off_in = swapped("pole", sends, shifts(sz.poles, sz.cores, 1))
     off, *sends = fold(sz.outer, "pole", sz.cores, off, off_in)
     off_in = swapped("pole", sends, shifts(sz.poles, sz.outer, sz.cores))
@@ -454,7 +540,7 @@
 def make_body(mesh):
     def body(green, factor, diag_inverse, pole_weight, pattern):
         sz = Sizes(mesh, green, factor, diag_inverse, pattern)
-        fits = sz.cols == 2 and sz.level == 1 and sz.cores == 2 and sz.rows >= 3 and sz.per_row >= 2 and sz.half >= 3
+        fits = sz.cols == 2 and sz.level == 1 and sz.cores == 2 and sz.rows >= 4 and sz.block % (sz.local_rows // sz.poles) == 0 and sz.per_row >= 2 and sz.half >= 3
         if not fits:
             return generic(sz, green, factor, diag_inverse, pole_weight, pattern)
         return blocked(sz, green, factor, diag_inverse, pole_weight, pattern)

time: 118 us -> 122 us (1.034)
  starting transfers between devices: 54.2 us -> 38.9 us
  waiting for transfers between devices: 35.1 us -> 49.2 us
  Pallas kernels: 20.1 us -> 23.1 us
  local copies, waits for them, and re-layouts: 3.17 us -> 4.95 us
    ppermute x12 -> x13, starting transfers between devices: 39 us -> 27.8 us  [the longest x6 13.9 us: blocked(): lax.ppermute(a, 'row', [(i, i + 1) for i in range(step - 1, sz.rows - 1)])]
    ppermute x3, waiting for transfers between devices: 1.99 us -> 10.5 us  [blocked(): slots.append(lax.ppermute(sent, 'col', swap))]
    ppermute x12 -> x13, waiting for transfers between devices: 20.9 us -> 26.6 us  [the longest x6 22.3 us: blocked(): lax.ppermute(b, 'row', [(i + 1, i) for i in range(sz.rows - step)])]
    pallas_call x1 -> x3, Pallas kernels: 4.02 us -> 8.59 us  [the longest x1 3.33 us: inner(): pl.pallas_call(functools.partial(inner_kernel, sz), out_shape=jax.ShapeDt...]
    ppermute x8, starting transfers between devices: 10.1 us -> 7.51 us  [swapped(): ins.append(lax.ppermute(v, axis, perm))]
    unnamed x20 -> x28, local copies, waits for them, and re-layouts: 0.85 us -> 2.59 us
    pallas_call x3 -> x2, Pallas kernels: 9.54 us -> 7.95 us  [early_call(): pl.pallas_call(functools.partial(early_kernel, sz, ready, before, keys, l...]
    ppermute x3, starting transfers between devices: 5.06 us -> 3.68 us  [blocked(): slots.append(lax.ppermute(sent, 'col', swap))]
  transfers between devices with their start and end apart: 23 -> 24, of which waited for: 13 -> 12; matrix products, arithmetic and copies ran while one was open for 2% -> 2% of each run, Pallas kernels for 14% -> 17%
where the time goes in v3:
time: 122 us; the launch traced here: 121 us
  waiting for transfers between devices  49.2 us (40%)
  starting transfers between devices  38.9 us (32%)
  Pallas kernels  23.1 us (19%)
  local copies, waits for them, and re-layouts  4.95 us (4%)
  between operations  2.96 us (2%)
  other arithmetic  2.22 us (2%)
    ppermute x6, waiting for transfers between devices, blocked(): lax.ppermute(b, 'row', [(i + 1, i) for i in range(sz.rows - step)])  22.3 us
    ppermute x6, starting transfers between devices, blocked(): lax.ppermute(a, 'row', [(i, i + 1) for i in range(step - 1, sz.rows - 1)])  13.9 us
    ppermute x8, waiting for transfers between devices, swapped(): ins.append(lax.ppermute(v, axis, perm))  12.1 us
    ppermute x3, waiting for transfers between devices, blocked(): slots.append(lax.ppermute(sent, 'col', swap))  10.5 us
    pallas_call x2, Pallas kernels, early_call(): pl.pallas_call(functools.partial(early_kernel, sz, ready, before, keys, l...  7.95 us
    ppermute x6, starting transfers between devices, blocked(): lax.ppermute(b, 'row', [(i + 1, i) for i in range(sz.rows - step)])  7.73 us
    ppermute x8, starting transfers between devices, swapped(): ins.append(lax.ppermute(v, axis, perm))  7.51 us
    pallas_call x3, Pallas kernels, pick(): pl.pallas_call(functools.partial(pick_kernel, sz, slot, parts), out_shape...  6.4 us
  transfers between devices with their start and end apart: 24, of which 12 were waited for; matrix products, arithmetic and copies ran while one was open for 2% of the time, Pallas kernels for 17%

profile of v3, /device:TPU:0, one launch (start us, length us, event | category | flops | bytes accessed | tf_op | source)
XLA Modules:
  0.0 121.4 jit_solution(10113549288258775389)
XLA Ops:
  0.6 1.3 %slice_bitcast_fusion = (bf16[512,512]{1,0:T(8,128)(2,1)S(1)}, bf16[512,512]{1,0:T(8,128)(2,1)S(1)}) fusion(bf16[1,1024,512]{2,1,0:T(8,128)(2,1)} %refs_17_.1), kind=kLoop, calls=%fused_computation.1 | loop fusion | bytes 2097152 | tf_op jit(solution)/shard_map/squeeze | solution.py:467
  1.9 5.0 %collective-permute-start.10 = (bf16[512,512]{1,0:T(8,128)(2,1)S(1)}, bf16[512,512]{1,0:T(8,128)(2,1)S(1)}, u32[]{:S(2)}, u32[]{:S(2)}) collective-permute-start(bf16[512,512]{1,0:T(8,128)(2,1)S(1)} %get-tuple-element.47.refs_0_), channel_id=1, source_target_pairs={{0,2},{2,4},{4,6},{1,3},{3,5},{5,7},{8,10},{10,12},{12,14},{9,11},... | collective-permute-start | bytes 1572872 | tf_op jit(solution)/shard_map/ppermute | solution.py:480
  6.9 1.9 %shard_map.68 = bf16[1024,512]{1,0:T(8,128)(2,1)S(1)} custom-call(s32[2,8]{1,0:T(2,128)S(1)} %bitcast.5, bf16[1,1024,2048]{2,1,0:T(8,128)(2,1)} %g_local.7), custom_call_target="tpu_custom_call" | custom-call | tf_op jit(solution)/shard_map/pallas_call | solution.py:147
  8.8 1.6 %collective-permute-start.7 = (bf16[1024,512]{1,0:T(8,128)(2,1)S(1)}, bf16[1024,512]{1,0:T(8,128)(2,1)S(1)}, u32[]{:S(2)}, u32[]{:S(2)}) collective-permute-start(bf16[1024,512]{1,0:T(8,128)(2,1)S(1)} %shard_map.68), channel_id=1, source_target_pairs={{0,1},{1,0},{2,3},{3,2},{4,5},{5,4},{6,7},{7,6},{8,9},{9,8},{10,11... | collective-permute-start | bytes 3145736 | tf_op jit(solution)/shard_map/ppermute | solution.py:474
  10.4 1.9 %shard_map.69 = bf16[1024,512]{1,0:T(8,128)(2,1)S(1)} custom-call(s32[2,8]{1,0:T(2,128)S(1)} %bitcast.6, bf16[1,1024,2048]{2,1,0:T(8,128)(2,1)} %g_local.7), custom_call_target="tpu_custom_call" | custom-call | tf_op jit(solution)/shard_map/pallas_call | solution.py:147
  12.3 0.6 collective-permute-start.8
  12.9 1.3 %collective-permute-start.11 = (bf16[512,512]{1,0:T(8,128)(2,1)S(1)}, bf16[512,512]{1,0:T(8,128)(2,1)S(1)}, u32[]{:S(2)}, u32[]{:S(2)}) collective-permute-start(bf16[512,512]{1,0:T(8,128)(2,1)S(1)} %get-tuple-element.47.refs_0_), channel_id=1, source_target_pairs={{2,0},{4,2},{6,4},{3,1},{5,3},{7,5},{10,8},{12,10},{14,12},{11,9},... | collective-permute-start | bytes 1572872 | tf_op jit(solution)/shard_map/ppermute | solution.py:481
  14.2 4.6 %collective-permute-start.1 = (bf16[512,512]{1,0:T(8,128)(2,1)S(1)}, bf16[512,512]{1,0:T(8,128)(2,1)S(1)}, u32[]{:S(2)}, u32[]{:S(2)}) collective-permute-start(bf16[512,512]{1,0:T(8,128)(2,1)S(1)} %get-tuple-element.48.refs_1_), channel_id=1, source_target_pairs={{0,2},{2,4},{4,6},{1,3},{3,5},{5,7},{8,10},{10,12},{12,14},{9,11},... | collective-permute-start | bytes 1572872 | tf_op jit(solution)/shard_map/ppermute | solution.py:480
  18.8 1.3 %collective-permute-start.4 = (bf16[512,512]{1,0:T(8,128)(2,1)S(1)}, bf16[512,512]{1,0:T(8,128)(2,1)S(1)}, u32[]{:S(2)}, u32[]{:S(2)}) collective-permute-start(bf16[512,512]{1,0:T(8,128)(2,1)S(1)} %get-tuple-element.48.refs_1_), channel_id=1, source_target_pairs={{2,0},{4,2},{6,4},{3,1},{5,3},{7,5},{10,8},{12,10},{14,12},{11,9},... | collective-permute-start | bytes 1572872 | tf_op jit(solution)/shard_map/ppermute | solution.py:481
  20.1 9.5 %collective-permute-done.11.refs_3_ = bf16[512,512]{1,0:T(8,128)(2,1)S(1)} collective-permute-done((bf16[512,512]{1,0:T(8,128)(2,1)S(1)}, bf16[512,512]{1,0:T(8,128)(2,1)S(1)}, u32[]{:S(2)}, u32[]{:S(2)}) %collective-permute-start.11) | collective-permute-done | bytes 524320 | tf_op jit(solution)/shard_map/ppermute | solution.py:481
  29.6 1.5 %collective-permute-start.12 = (bf16[512,512]{1,0:T(8,128)(2,1)S(1)}, bf16[512,512]{1,0:T(8,128)(2,1)}, u32[]{:S(2)}, u32[]{:S(2)}) collective-permute-start(bf16[512,512]{1,0:T(8,128)(2,1)S(1)} %collective-permute-done.10.refs_2_), channel_id=1, source_target_pairs={{2,4},{4,6},{3,5},{5,7},{10,12},{12,14},{11,13},{13,15},{18,20},{2... | collective-permute-start | bytes 1572872 | tf_op jit(solution)/shard_map/ppermute | solution.py:480
  31.1 1.3 %collective-permute-start.13 = (bf16[512,512]{1,0:T(8,128)(2,1)S(1)}, bf16[512,512]{1,0:T(8,128)(2,1)}, u32[]{:S(2)}, u32[]{:S(2)}) collective-permute-start(bf16[512,512]{1,0:T(8,128)(2,1)S(1)} %collective-permute-done.11.refs_3_), channel_id=1, source_target_pairs={{2,0},{4,2},{3,1},{5,3},{10,8},{12,10},{11,9},{13,11},{18,16},{20,... | collective-permute-start | bytes 1572872 | tf_op jit(solution)/shard_map/ppermute | solution.py:481
  32.4 8.4 %collective-permute-done.4.refs_7_.refs_9_ = bf16[512,512]{1,0:T(8,128)(2,1)S(1)} collective-permute-done((bf16[512,512]{1,0:T(8,128)(2,1)S(1)}, bf16[512,512]{1,0:T(8,128)(2,1)S(1)}, u32[]{:S(2)}, u32[]{:S(2)}) %collective-permute-start.4) | collective-permute-done | bytes 524320 | tf_op jit(solution)/shard_map/ppermute | solution.py:481
  40.8 0.7 collective-permute-start.2
  41.5 1.3 %collective-permute-start.5 = (bf16[512,512]{1,0:T(8,128)(2,1)S(1)}, bf16[512,512]{1,0:T(8,128)(2,1)}, u32[]{:S(2)}, u32[]{:S(2)}) collective-permute-start(bf16[512,512]{1,0:T(8,128)(2,1)S(1)} %collective-permute-done.4.refs_7_.refs_9_), channel_id=1, source_target_pairs={{2,0},{4,2},{3,1},{5,3},{10,8},{12,10},{11,9},{13,11},{18,16},{20,... | collective-permute-start | bytes 1572872 | tf_op jit(solution)/shard_map/ppermute | solution.py:481
  42.8 2.6 %shard_map.70 = bf16[1024,512]{1,0:T(8,128)(2,1)} custom-call(s32[2,8]{1,0:T(2,128)S(1)} %bitcast.7, bf16[1,1024,2048]{2,1,0:T(8,128)(2,1)} %g_local.7), custom_call_target="tpu_custom_call" | custom-call | tf_op jit(solution)/shard_map/pallas_call | solution.py:147
  45.5 10.5 %collective-permute-done.8.refs_11_.refs_13_.refs_3_ = bf16[1024,512]{1,0:T(8,128)(2,1)S(1)} collective-permute-done((bf16[1024,512]{1,0:T(8,128)(2,1)S(1)}, bf16[1024,512]{1,0:T(8,128)(2,1)S(1)}, u32[]{:S(2)}, u32[]{:S(2)}) %collective-permute-start.8) | collective-permute-done | bytes 1048608 | tf_op jit(solution)/shard_map/ppermute | solution.py:474
  56.0 1.0 copy-done.3
  57.0 1.5 %collective-permute-start.9 = (bf16[1024,512]{1,0:T(8,128)(2,1)}, bf16[1024,512]{1,0:T(8,128)(2,1)}, u32[]{:S(2)}, u32[]{:S(2)}) collective-permute-start(bf16[1024,512]{1,0:T(8,128)(2,1)} %shard_map.70), channel_id=1, source_target_pairs={{0,1},{1,0},{2,3},{3,2},{4,5},{5,4},{6,7},{7,6},{8,9},{9,8},{10,11... | collective-permute-start | bytes 3145736 | tf_op jit(solution)/shard_map/ppermute | solution.py:474
  58.5 1.5 %collective-permute-start.14 = (bf16[512,512]{1,0:T(8,128)(2,1)}, bf16[512,512]{1,0:T(8,128)(2,1)}, u32[]{:S(2)}, u32[]{:S(2)}) collective-permute-start(bf16[512,512]{1,0:T(8,128)(2,1)} %collective-permute-done.12.refs_4_), channel_id=1, source_target_pairs={{4,6},{5,7},{12,14},{13,15},{20,22},{21,23},{28,30},{29,31}} | collective-permute-start | bytes 1572872 | tf_op jit(solution)/shard_map/ppermute | solution.py:480
  60.0 0.7 compare_reduce_fusion
  62.0 0.8 copy-done.10
  62.8 7.0 %shard_map.71.refs_14_ = f32[1024,512]{1,0:T(8,128)S(1)} custom-call(s32[2,8]{1,0:T(2,128)S(1)} %bitcast.9, bf16[1,1024,2048]{2,1,0:T(8,128)(2,1)} %g_local.7, bf16[512,512]{1,0:T(8,128)(2,1)} %copy-done.4, bf16[512,512]{1,0:T(8,128)(2,1)} %copy-done.5, bf16[512,512]{1,0:T(8,128)(2,1)} %copy-done.6, bf16[512,512]{1,0:T(8,128)(2,1)} %copy-done.7, ...), custom_call_target="tpu_custom_call" | custom-call | tf_op jit(solution)/shard_map/pallas_call | solution.py:261
  69.8 1.3 %collective-permute-start.15 = (bf16[512,512]{1,0:T(8,128)(2,1)}, bf16[512,512]{1,0:T(8,128)(2,1)}, u32[]{:S(2)}, u32[]{:S(2)}) collective-permute-start(bf16[512,512]{1,0:T(8,128)(2,1)} %collective-permute-done.13.refs_5_), channel_id=1, source_target_pairs={{2,0},{3,1},{10,8},{11,9},{18,16},{19,17},{26,24},{27,25}} | collective-permute-start | bytes 1572872 | tf_op jit(solution)/shard_map/ppermute | solution.py:481
  71.1 3.3 %inner.1 = bf16[512,512]{1,0:T(8,128)(2,1)} custom-call(s32[2,8]{1,0:T(2,128)S(1)} %bitcast.10, bf16[1,1024,2048]{2,1,0:T(8,128)(2,1)} %g_local.7, bf16[1024,512]{1,0:T(8,128)(2,1)} %copy-done.2, bf16[1,1024,512]{2,1,0:T(8,128)(2,1)S(1)} %copy-done), custom_call_target="tpu_custom_call" | custom-call | tf_op jit(solution)/shard_map/inner/pallas_call | solution.py:311
  74.5 6.1 %collective-permute-start.16 = (bf16[512,512]{1,0:T(8,128)(2,1)}, bf16[512,512]{1,0:T(8,128)(2,1)}, u32[]{:S(2)}, u32[]{:S(2)}) collective-permute-start(bf16[512,512]{1,0:T(8,128)(2,1)} %inner.1), channel_id=1, source_target_pairs={{0,2},{6,4},{1,3},{7,5},{8,10},{14,12},{9,11},{15,13},{16,18},{22,... | collective-permute-start | bytes 1572872 | tf_op jit(solution)/shard_map/ppermute | solution.py:489
  80.6 1.1 conditional.1
  80.6 1.1 broadcast.7
  81.7 0.7 collective-permute-start.3
  82.4 1.3 %collective-permute-start.6 = (bf16[512,512]{1,0:T(8,128)(2,1)}, bf16[512,512]{1,0:T(8,128)(2,1)S(1)}, u32[]{:S(2)}, u32[]{:S(2)}) collective-permute-start(bf16[512,512]{1,0:T(8,128)(2,1)} %collective-permute-done.5.refs_9_.refs_11_), channel_id=1, source_target_pairs={{2,0},{3,1},{10,8},{11,9},{18,16},{19,17},{26,24},{27,25}} | collective-permute-start | bytes 1572872 | tf_op jit(solution)/shard_map/ppermute | solution.py:481
  84.5 0.9 shard_map.72.refs_16_
  85.5 4.3 %collective-permute-done.16.refs_19_ = bf16[512,512]{1,0:T(8,128)(2,1)} collective-permute-done((bf16[512,512]{1,0:T(8,128)(2,1)}, bf16[512,512]{1,0:T(8,128)(2,1)}, u32[]{:S(2)}, u32[]{:S(2)}) %collective-permute-start.16) | collective-permute-done | bytes 524320 | tf_op jit(solution)/shard_map/ppermute | solution.py:489
  89.8 2.4 %late_diag.1 = (f32[128,512]{1,0:T(8,128)S(1)}, bf16[128,512]{1,0:T(8,128)(2,1)S(1)}, bf16[128,512]{1,0:T(8,128)(2,1)S(1)}, bf16[128,512]{1,0:T(8,128)(2,1)S(1)}, f32[1024,512]{1,0:T(8,128)S(1)}) custom-call(s32[2,8]{1,0:T(2,128)S(1)} %bitcast.13, f32[1]{0:T(128)S(6)} %copy.11.weight, bf16[1,1024,2048]{2,1,0:T(8,128)(2,1)} %g_local.7, ...), custom_call_target="tpu_custom_call" | custom-call | tf_op jit(solution)/shard_map/late_diag/pallas_call | solution.py:375
  92.2 4.2 %collective-permute-done.6.refs_1_ = bf16[512,512]{1,0:T(8,128)(2,1)S(1)} collective-permute-done((bf16[512,512]{1,0:T(8,128)(2,1)}, bf16[512,512]{1,0:T(8,128)(2,1)S(1)}, u32[]{:S(2)}, u32[]{:S(2)}) %collective-permute-start.6) | collective-permute-done | bytes 524320 | tf_op jit(solution)/shard_map/ppermute | solution.py:481
  96.4 0.8 copy-done.12
  97.2 2.9 %late_off.1 = (f32[512,512]{1,0:T(8,128)S(1)}, bf16[512,512]{1,0:T(8,128)(2,1)S(1)}) custom-call(s32[2,8]{1,0:T(2,128)S(1)} %bitcast.14, f32[1]{0:T(128)S(6)} %copy.11.weight, bf16[1,1024,2048]{2,1,0:T(8,128)(2,1)} %g_local.7, bf16[512,512]{1,0:T(8,128)(2,1)} %copy-done.11, bf16[512,512]{1,0:T(8,128)(2,1)} %copy-done.12, bf16[1024,512]{1,0:T(8,128)(2,1)} %copy-done.2, ...), custom_call_target="tpu_custom_call" | custom-call | tf_op jit(solution)/shard_map/late_off/pallas_call | solution.py:412
  100.2 0.5 collective-permute-start.19
  100.7 1.5 %collective-permute-start.20 = (bf16[128,512]{1,0:T(8,128)(2,1)S(1)}, bf16[128,512]{1,0:T(8,128)(2,1)S(1)}, u32[]{:S(2)}, u32[]{:S(2)}) collective-permute-start(bf16[128,512]{1,0:T(8,128)(2,1)S(1)} %get-tuple-element.39), channel_id=1, source_target_pairs={{0,16},{8,24},{16,0},{24,8},{1,17},{9,25},{17,1},{25,9},{2,18},{10... | collective-permute-start | bytes 393224 | tf_op jit(solution)/shard_map/ppermute | solution.py:522
  102.2 4.8 %collective-permute-done.20.refs_1_ = bf16[128,512]{1,0:T(8,128)(2,1)S(1)} collective-permute-done((bf16[128,512]{1,0:T(8,128)(2,1)S(1)}, bf16[128,512]{1,0:T(8,128)(2,1)S(1)}, u32[]{:S(2)}, u32[]{:S(2)}) %collective-permute-start.20) | collective-permute-done | bytes 131104 | tf_op jit(solution)/shard_map/ppermute | solution.py:522
  107.0 1.0 collective-permute-done.21.refs_2_
  108.2 2.7 %collective-permute-start.23 = (bf16[32,512]{1,0:T(8,128)(2,1)S(1)}, bf16[32,512]{1,0:T(8,128)(2,1)S(1)}, u32[]{:S(2)}, u32[]{:S(2)}) collective-permute-start(bf16[32,512]{1,0:T(8,128)(2,1)S(1)} %get-tuple-element.43), channel_id=1, source_target_pairs={{0,4},{2,6},{4,0},{6,2},{1,5},{3,7},{5,1},{7,3},{8,12},{10,14},{12... | collective-permute-start | bytes 98312 | tf_op jit(solution)/shard_map/ppermute | solution.py:522
  110.9 1.1 collective-permute-start.24
  112.1 1.6 %collective-permute-start.18 = (bf16[256,512]{1,0:T(8,128)(2,1)S(1)}, bf16[256,512]{1,0:T(8,128)(2,1)S(1)}, u32[]{:S(2)}, u32[]{:S(2)}) collective-permute-start(bf16[256,512]{1,0:T(8,128)(2,1)S(1)} %get-tuple-element.36), channel_id=1, source_target_pairs={{0,16},{8,24},{16,0},{24,8},{1,17},{9,25},{17,1},{25,9},{2,18},{10... | collective-permute-start | bytes 786440 | tf_op jit(solution)/shard_map/ppermute | solution.py:522
  113.7 0.6 collective-permute-done.22
  114.2 0.5 collective-permute-done.24
  114.8 0.6 convert_add_fusion.1
  115.4 5.1 %collective-permute-done.18 = bf16[256,512]{1,0:T(8,128)(2,1)S(1)} collective-permute-done((bf16[256,512]{1,0:T(8,128)(2,1)S(1)}, bf16[256,512]{1,0:T(8,128)(2,1)S(1)}, u32[]{:S(2)}, u32[]{:S(2)}) %collective-permute-start.18) | collective-permute-done | bytes 262176 | tf_op jit(solution)/shard_map/ppermute | solution.py:522
  120.5 0.9 convert_add_fusion
  (44 shorter events, 0.6 us)
Async XLA Ops:
  0.6 6.3 %copy-start.13 = (s32[8,2]{0,1:T(2,128)S(1)}, s32[8,2]{0,1:T(2,128)}, u32[]{:S(2)}) copy-start(s32[8,2]{0,1:T(2,128)} %param.11) | copy-start | bytes 196
  1.9 11.0 %copy-start.4 = (bf16[512,512]{1,0:T(8,128)(2,1)}, bf16[512,512]{1,0:T(8,128)(2,1)S(1)}, u32[]{:S(2)}) copy-start(bf16[512,512]{1,0:T(8,128)(2,1)S(1)} %get-tuple-element.47.refs_0_) | copy-start | bytes 1572868
  1.9 16.9 %copy-start.5 = (bf16[512,512]{1,0:T(8,128)(2,1)}, bf16[512,512]{1,0:T(8,128)(2,1)S(1)}, u32[]{:S(2)}) copy-start(bf16[512,512]{1,0:T(8,128)(2,1)S(1)} %get-tuple-element.48.refs_1_) | copy-start | bytes 1572868
  1.9 16.8 %collective-permute-start.10 = (bf16[512,512]{1,0:T(8,128)(2,1)S(1)}, bf16[512,512]{1,0:T(8,128)(2,1)S(1)}, u32[]{:S(2)}, u32[]{:S(2)}) collective-permute-start(bf16[512,512]{1,0:T(8,128)(2,1)S(1)} %get-tuple-element.47.refs_0_), channel_id=1, source_target_pairs={{0,2},{2,4},{4,6},{1,3},{3,5},{5,7},{8,10},{10,12},{12,14},{9,11},... | collective-permute-start | bytes 1572872 | tf_op jit(solution)/shard_map/ppermute | solution.py:480
  8.8 32.7 %collective-permute-start.7 = (bf16[1024,512]{1,0:T(8,128)(2,1)S(1)}, bf16[1024,512]{1,0:T(8,128)(2,1)S(1)}, u32[]{:S(2)}, u32[]{:S(2)}) collective-permute-start(bf16[1024,512]{1,0:T(8,128)(2,1)S(1)} %shard_map.68), channel_id=1, source_target_pairs={{0,1},{1,0},{2,3},{3,2},{4,5},{5,4},{6,7},{7,6},{8,9},{9,8},{10,11... | collective-permute-start | bytes 3145736 | tf_op jit(solution)/shard_map/ppermute | solution.py:474
  12.3 43.7 %collective-permute-start.8 = (bf16[1024,512]{1,0:T(8,128)(2,1)S(1)}, bf16[1024,512]{1,0:T(8,128)(2,1)S(1)}, u32[]{:S(2)}, u32[]{:S(2)}) collective-permute-start(bf16[1024,512]{1,0:T(8,128)(2,1)S(1)} %shard_map.69), channel_id=1, source_target_pairs={{0,1},{1,0},{2,3},{3,2},{4,5},{5,4},{6,7},{7,6},{8,9},{9,8},{10,11... | collective-permute-start | bytes 3145736 | tf_op jit(solution)/shard_map/ppermute | solution.py:474
  12.9 16.7 %collective-permute-start.11 = (bf16[512,512]{1,0:T(8,128)(2,1)S(1)}, bf16[512,512]{1,0:T(8,128)(2,1)S(1)}, u32[]{:S(2)}, u32[]{:S(2)}) collective-permute-start(bf16[512,512]{1,0:T(8,128)(2,1)S(1)} %get-tuple-element.47.refs_0_), channel_id=1, source_target_pairs={{2,0},{4,2},{6,4},{3,1},{5,3},{7,5},{10,8},{12,10},{14,12},{11,9},... | collective-permute-start | bytes 1572872 | tf_op jit(solution)/shard_map/ppermute | solution.py:481
  14.2 16.9 %collective-permute-start.1 = (bf16[512,512]{1,0:T(8,128)(2,1)S(1)}, bf16[512,512]{1,0:T(8,128)(2,1)S(1)}, u32[]{:S(2)}, u32[]{:S(2)}) collective-permute-start(bf16[512,512]{1,0:T(8,128)(2,1)S(1)} %get-tuple-element.48.refs_1_), channel_id=1, source_target_pairs={{0,2},{2,4},{4,6},{1,3},{3,5},{5,7},{8,10},{10,12},{12,14},{9,11},... | collective-permute-start | bytes 1572872 | tf_op jit(solution)/shard_map/ppermute | solution.py:480
  18.8 26.7 %copy-start.6 = (bf16[512,512]{1,0:T(8,128)(2,1)}, bf16[512,512]{1,0:T(8,128)(2,1)S(1)}, u32[]{:S(2)}) copy-start(bf16[512,512]{1,0:T(8,128)(2,1)S(1)} %collective-permute-done.10.refs_2_) | copy-start | bytes 1572868
  18.8 22.0 %collective-permute-start.4 = (bf16[512,512]{1,0:T(8,128)(2,1)S(1)}, bf16[512,512]{1,0:T(8,128)(2,1)S(1)}, u32[]{:S(2)}, u32[]{:S(2)}) collective-permute-start(bf16[512,512]{1,0:T(8,128)(2,1)S(1)} %get-tuple-element.48.refs_1_), channel_id=1, source_target_pairs={{2,0},{4,2},{6,4},{3,1},{5,3},{7,5},{10,8},{12,10},{14,12},{11,9},... | collective-permute-start | bytes 1572872 | tf_op jit(solution)/shard_map/ppermute | solution.py:481
  29.6 15.9 %copy-start.7 = (bf16[512,512]{1,0:T(8,128)(2,1)}, bf16[512,512]{1,0:T(8,128)(2,1)S(1)}, u32[]{:S(2)}) copy-start(bf16[512,512]{1,0:T(8,128)(2,1)S(1)} %collective-permute-done.11.refs_3_) | copy-start | bytes 1572868
  29.6 28.9 %collective-permute-start.12 = (bf16[512,512]{1,0:T(8,128)(2,1)S(1)}, bf16[512,512]{1,0:T(8,128)(2,1)}, u32[]{:S(2)}, u32[]{:S(2)}) collective-permute-start(bf16[512,512]{1,0:T(8,128)(2,1)S(1)} %collective-permute-done.10.refs_2_), channel_id=1, source_target_pairs={{2,4},{4,6},{3,5},{5,7},{10,12},{12,14},{11,13},{13,15},{18,20},{2... | collective-permute-start | bytes 1572872 | tf_op jit(solution)/shard_map/ppermute | solution.py:480
  31.1 14.4 %copy-start.8 = (bf16[512,512]{1,0:T(8,128)(2,1)}, bf16[512,512]{1,0:T(8,128)(2,1)S(1)}, u32[]{:S(2)}) copy-start(bf16[512,512]{1,0:T(8,128)(2,1)S(1)} %collective-permute-done.1.refs_6_.refs_8_) | copy-start | bytes 1572868
  31.1 30.9 %collective-permute-start.13 = (bf16[512,512]{1,0:T(8,128)(2,1)S(1)}, bf16[512,512]{1,0:T(8,128)(2,1)}, u32[]{:S(2)}, u32[]{:S(2)}) collective-permute-start(bf16[512,512]{1,0:T(8,128)(2,1)S(1)} %collective-permute-done.11.refs_3_), channel_id=1, source_target_pairs={{2,0},{4,2},{3,1},{5,3},{10,8},{12,10},{11,9},{13,11},{18,16},{20,... | collective-permute-start | bytes 1572872 | tf_op jit(solution)/shard_map/ppermute | solution.py:481
  40.8 4.7 %copy-start.9 = (bf16[512,512]{1,0:T(8,128)(2,1)}, bf16[512,512]{1,0:T(8,128)(2,1)S(1)}, u32[]{:S(2)}) copy-start(bf16[512,512]{1,0:T(8,128)(2,1)S(1)} %collective-permute-done.4.refs_7_.refs_9_) | copy-start | bytes 1572868
  40.8 21.2 %collective-permute-start.2 = (bf16[512,512]{1,0:T(8,128)(2,1)S(1)}, bf16[512,512]{1,0:T(8,128)(2,1)S(1)}, u32[]{:S(2)}, u32[]{:S(2)}) collective-permute-start(bf16[512,512]{1,0:T(8,128)(2,1)S(1)} %collective-permute-done.1.refs_6_.refs_8_), channel_id=1, source_target_pairs={{2,4},{4,6},{3,5},{5,7},{10,12},{12,14},{11,13},{13,15},{18,20},{2... | collective-permute-start | bytes 1572872 | tf_op jit(solution)/shard_map/ppermute | solution.py:480
  41.5 4.0 %copy-start.2 = (bf16[1024,512]{1,0:T(8,128)(2,1)}, bf16[1024,512]{1,0:T(8,128)(2,1)S(1)}, u32[]{:S(2)}) copy-start(bf16[1024,512]{1,0:T(8,128)(2,1)S(1)} %collective-permute-done.7.refs_10_.refs_12_.slot.refs_2_) | copy-start | bytes 3145732
  41.5 21.3 %collective-permute-start.5 = (bf16[512,512]{1,0:T(8,128)(2,1)S(1)}, bf16[512,512]{1,0:T(8,128)(2,1)}, u32[]{:S(2)}, u32[]{:S(2)}) collective-permute-start(bf16[512,512]{1,0:T(8,128)(2,1)S(1)} %collective-permute-done.4.refs_7_.refs_9_), channel_id=1, source_target_pairs={{2,0},{4,2},{3,1},{5,3},{10,8},{12,10},{11,9},{13,11},{18,16},{20,... | collective-permute-start | bytes 1572872 | tf_op jit(solution)/shard_map/ppermute | solution.py:481
  56.0 1.0 copy-start.3
  57.0 28.5 %collective-permute-start.9 = (bf16[1024,512]{1,0:T(8,128)(2,1)}, bf16[1024,512]{1,0:T(8,128)(2,1)}, u32[]{:S(2)}, u32[]{:S(2)}) collective-permute-start(bf16[1024,512]{1,0:T(8,128)(2,1)} %shard_map.70), channel_id=1, source_target_pairs={{0,1},{1,0},{2,3},{3,2},{4,5},{5,4},{6,7},{7,6},{8,9},{9,8},{10,11... | collective-permute-start | bytes 3145736 | tf_op jit(solution)/shard_map/ppermute | solution.py:474
  58.5 23.9 %collective-permute-start.14 = (bf16[512,512]{1,0:T(8,128)(2,1)}, bf16[512,512]{1,0:T(8,128)(2,1)}, u32[]{:S(2)}, u32[]{:S(2)}) collective-permute-start(bf16[512,512]{1,0:T(8,128)(2,1)} %collective-permute-done.12.refs_4_), channel_id=1, source_target_pairs={{4,6},{5,7},{12,14},{13,15},{20,22},{21,23},{28,30},{29,31}} | collective-permute-start | bytes 1572872 | tf_op jit(solution)/shard_map/ppermute | solution.py:480
  62.0 9.1 %copy-start = (bf16[1,1024,512]{2,1,0:T(8,128)(2,1)S(1)}, bf16[1,1024,512]{2,1,0:T(8,128)(2,1)}, u32[]{:S(2)}) copy-start(bf16[1,1024,512]{2,1,0:T(8,128)(2,1)} %refs_17_.1) | copy-start | bytes 3145732
  62.0 0.8 copy-start.10
  69.8 14.7 %collective-permute-start.15 = (bf16[512,512]{1,0:T(8,128)(2,1)}, bf16[512,512]{1,0:T(8,128)(2,1)}, u32[]{:S(2)}, u32[]{:S(2)}) collective-permute-start(bf16[512,512]{1,0:T(8,128)(2,1)} %collective-permute-done.13.refs_5_), channel_id=1, source_target_pairs={{2,0},{3,1},{10,8},{11,9},{18,16},{19,17},{26,24},{27,25}} | collective-permute-start | bytes 1572872 | tf_op jit(solution)/shard_map/ppermute | solution.py:481
  74.5 15.3 %collective-permute-start.16 = (bf16[512,512]{1,0:T(8,128)(2,1)}, bf16[512,512]{1,0:T(8,128)(2,1)}, u32[]{:S(2)}, u32[]{:S(2)}) collective-permute-start(bf16[512,512]{1,0:T(8,128)(2,1)} %inner.1), channel_id=1, source_target_pairs={{0,2},{6,4},{1,3},{7,5},{8,10},{14,12},{9,11},{15,13},{16,18},{22,... | collective-permute-start | bytes 1572872 | tf_op jit(solution)/shard_map/ppermute | solution.py:489
  81.7 10.5 %collective-permute-start.3 = (bf16[512,512]{1,0:T(8,128)(2,1)}, bf16[512,512]{1,0:T(8,128)(2,1)S(1)}, u32[]{:S(2)}, u32[]{:S(2)}) collective-permute-start(bf16[512,512]{1,0:T(8,128)(2,1)} %copy-done.10), channel_id=1, source_target_pairs={{4,6},{5,7},{12,14},{13,15},{20,22},{21,23},{28,30},{29,31}} | collective-permute-start | bytes 1572872 | tf_op jit(solution)/shard_map/ppermute | solution.py:480
  82.4 14.0 %collective-permute-start.6 = (bf16[512,512]{1,0:T(8,128)(2,1)}, bf16[512,512]{1,0:T(8,128)(2,1)S(1)}, u32[]{:S(2)}, u32[]{:S(2)}) collective-permute-start(bf16[512,512]{1,0:T(8,128)(2,1)} %collective-permute-done.5.refs_9_.refs_11_), channel_id=1, source_target_pairs={{2,0},{3,1},{10,8},{11,9},{18,16},{19,17},{26,24},{27,25}} | collective-permute-start | bytes 1572872 | tf_op jit(solution)/shard_map/ppermute | solution.py:481
  84.3 5.5 %copy-start.1 = (bf16[1,128,512]{2,1,0:T(8,128)(2,1)S(1)}, bf16[1,128,512]{2,1,0:T(8,128)(2,1)}, u32[]{:S(2)}) copy-start(bf16[1,128,512]{2,1,0:T(8,128)(2,1)} %refs_18_.1) | copy-start | bytes 393220
  92.2 4.2 %copy-start.11 = (bf16[512,512]{1,0:T(8,128)(2,1)}, bf16[512,512]{1,0:T(8,128)(2,1)S(1)}, u32[]{:S(2)}) copy-start(bf16[512,512]{1,0:T(8,128)(2,1)S(1)} %collective-permute-done.3.refs_0_) | copy-start | bytes 1572868
  96.4 0.8 copy-start.12
  100.1 11.9 %collective-permute-start.17 = (bf16[512,512]{1,0:T(8,128)(2,1)S(1)}, bf16[512,512]{1,0:T(8,128)(2,1)S(1)}, u32[]{:S(2)}, u32[]{:S(2)}) collective-permute-start(bf16[512,512]{1,0:T(8,128)(2,1)S(1)} %get-tuple-element.34), channel_id=1, source_target_pairs={{0,8},{8,0},{16,24},{24,16},{1,9},{9,1},{17,25},{25,17},{2,10},{10... | collective-permute-start | bytes 1572872 | tf_op jit(solution)/shard_map/ppermute | solution.py:522
  100.2 2.1 %collective-permute-start.19 = (bf16[128,512]{1,0:T(8,128)(2,1)S(1)}, bf16[128,512]{1,0:T(8,128)(2,1)S(1)}, u32[]{:S(2)}, u32[]{:S(2)}) collective-permute-start(bf16[128,512]{1,0:T(8,128)(2,1)S(1)} %get-tuple-element.38), channel_id=1, source_target_pairs={{0,8},{8,0},{16,24},{24,16},{1,9},{9,1},{17,25},{25,17},{2,10},{10... | collective-permute-start | bytes 393224 | tf_op jit(solution)/shard_map/ppermute | solution.py:522
  100.7 6.4 %collective-permute-start.20 = (bf16[128,512]{1,0:T(8,128)(2,1)S(1)}, bf16[128,512]{1,0:T(8,128)(2,1)S(1)}, u32[]{:S(2)}, u32[]{:S(2)}) collective-permute-start(bf16[128,512]{1,0:T(8,128)(2,1)S(1)} %get-tuple-element.39), channel_id=1, source_target_pairs={{0,16},{8,24},{16,0},{24,8},{1,17},{9,25},{17,1},{25,9},{2,18},{10... | collective-permute-start | bytes 393224 | tf_op jit(solution)/shard_map/ppermute | solution.py:522
  102.2 5.9 %collective-permute-start.21 = (bf16[128,512]{1,0:T(8,128)(2,1)S(1)}, bf16[128,512]{1,0:T(8,128)(2,1)S(1)}, u32[]{:S(2)}, u32[]{:S(2)}) collective-permute-start(bf16[128,512]{1,0:T(8,128)(2,1)S(1)} %get-tuple-element.40), channel_id=1, source_target_pairs={{0,24},{8,16},{16,8},{24,0},{1,25},{9,17},{17,9},{25,1},{2,26},{10... | collective-permute-start | bytes 393224 | tf_op jit(solution)/shard_map/ppermute | solution.py:522
  108.1 6.1 %collective-permute-start.22 = (bf16[32,512]{1,0:T(8,128)(2,1)S(1)}, bf16[32,512]{1,0:T(8,128)(2,1)S(1)}, u32[]{:S(2)}, u32[]{:S(2)}) collective-permute-start(bf16[32,512]{1,0:T(8,128)(2,1)S(1)} %get-tuple-element.42), channel_id=1, source_target_pairs={{0,2},{2,4},{4,6},{6,0},{1,3},{3,5},{5,7},{7,1},{8,10},{10,12},{12... | collective-permute-start | bytes 98312 | tf_op jit(solution)/shard_map/ppermute | solution.py:522
  108.2 6.0 %collective-permute-start.23 = (bf16[32,512]{1,0:T(8,128)(2,1)S(1)}, bf16[32,512]{1,0:T(8,128)(2,1)S(1)}, u32[]{:S(2)}, u32[]{:S(2)}) collective-permute-start(bf16[32,512]{1,0:T(8,128)(2,1)S(1)} %get-tuple-element.43), channel_id=1, source_target_pairs={{0,4},{2,6},{4,0},{6,2},{1,5},{3,7},{5,1},{7,3},{8,12},{10,14},{12... | collective-permute-start | bytes 98312 | tf_op jit(solution)/shard_map/ppermute | solution.py:522
  110.9 3.9 %collective-permute-start.24 = (bf16[32,512]{1,0:T(8,128)(2,1)S(1)}, bf16[32,512]{1,0:T(8,128)(2,1)S(1)}, u32[]{:S(2)}, u32[]{:S(2)}) collective-permute-start(bf16[32,512]{1,0:T(8,128)(2,1)S(1)} %get-tuple-element.44), channel_id=1, source_target_pairs={{0,6},{2,0},{4,2},{6,4},{1,7},{3,1},{5,3},{7,5},{8,14},{10,8},{12,... | collective-permute-start | bytes 98312 | tf_op jit(solution)/shard_map/ppermute | solution.py:522
  112.1 8.4 %collective-permute-start.18 = (bf16[256,512]{1,0:T(8,128)(2,1)S(1)}, bf16[256,512]{1,0:T(8,128)(2,1)S(1)}, u32[]{:S(2)}, u32[]{:S(2)}) collective-permute-start(bf16[256,512]{1,0:T(8,128)(2,1)S(1)} %get-tuple-element.36), channel_id=1, source_target_pairs={{0,16},{8,24},{16,0},{24,8},{1,17},{9,25},{17,1},{25,9},{2,18},{10... | collective-permute-start | bytes 786440 | tf_op jit(solution)/shard_map/ppermute | solution.py:522

commit v4 on v3

--- a/solution.py
+++ b/solution.py
@@ -269,16 +269,6 @@
     )(*args)
 
 
-def pole_steps(sz):
-    return [(dx, dc) for dx in range(sz.outer) for dc in range(sz.cores) if dx or dc]
-
-
-def pole_perm(sz, step):
-    dx, dc = step
-    return [(x * sz.cores + c, (x + dx) % sz.outer * sz.cores + (c + dc) % sz.cores)
-            for x in range(sz.outer) for c in range(sz.cores)]
-
-
 def far_block(sz, row):
     far = jnp.where(row < sz.rows // 2, sz.rows - 1, 0)
     return far * sz.per_row + sz.per_row - 1
@@ -324,11 +314,11 @@
     m_refs = {k: refs.pop(0) for k in keys}
     g_slots = [refs.pop(0) for _ in range(n_slots)]
     total_in, factor, dinv, far_term = (refs.pop(0) for _ in range(4))
-    outs = [refs.pop(0) for _ in range(sz.poles)]
+    outs = [refs.pop(0) for _ in range(sz.cores)]
     total, diag = refs.pop(0), refs.pop(0)
     job, m_buf, g_buf, m_sem, g_sem = refs
-    row, col, pole = (lax.axis_index(a) for a in ("row", "col", "pole"))
-    core, x_at = lax.rem(pole, sz.cores), pole // sz.cores
+    row, col = lax.axis_index("row"), lax.axis_index("col")
+    core = lax.rem(lax.axis_index("pole"), sz.cores)
 
     away = sz.rows - 2
     for at_row, sign in ((1, 1), (sz.rows - 2, -1)):
@@ -362,21 +352,24 @@
     mine = pl.ds(pl.multiple_of(row * sz.count, sz.count), sz.count)
     diag[mine, :] += w * dinv[0].astype(F32)
     n = diag.shape[0] // sz.poles
-    for (dx, dc), out in zip([(0, 0)] + pole_steps(sz), outs):
-        q = lax.rem(x_at + dx, sz.outer) * sz.cores + lax.rem(core + dc, sz.cores)
-        out[...] = diag[pl.ds(pl.multiple_of(q * n, n), n), :].astype(out.dtype)
-
-
-def late_diag(sz, ready, before, pattern, weight, green, m, slots, total, factor, dinv, far_term):
+    for dc, out in enumerate(outs):
+        for x in range(sz.outer):
+            q = x * sz.cores + lax.rem(core + dc, sz.cores)
+            out[x * n:(x + 1) * n, :] = diag[pl.ds(pl.multiple_of(q * n, n), n), :].astype(out.dtype)
+
+
+def late_diag(sz, ready, before, pattern, weight, green, m, slots, landed, total, factor, dinv, far_term):
     keys = list(m)
-    args = [pattern, weight] + in_hbm([green] + [m[k] for k in keys] + list(slots)) + [total, factor, dinv, far_term]
-    shapes = [jax.ShapeDtypeStruct((sz.block // sz.poles, sz.width), BF16 if i else F32) for i in range(sz.poles)]
+    args = [pattern, weight] + in_hbm([green] + [m[k] for k in keys])
+    args += [v if s == landed else in_hbm([v])[0] for s, v in enumerate(slots)] + [total, factor, dinv, far_term]
+    shapes = [jax.ShapeDtypeStruct((sz.block // sz.cores, sz.width), BF16 if i else F32) for i in range(sz.cores)]
     shapes.append(jax.ShapeDtypeStruct((sz.local_rows, sz.width), F32))
     return pl.pallas_call(
         functools.partial(late_diag_kernel, sz, ready, before, keys, len(slots)),
         out_shape=shapes,
-        in_specs=[SMEM] * 2 + [ANY] * (1 + len(keys) + len(slots)) + [VMEM] * 4,
-        out_specs=[VMEM] * (sz.poles + 1),
+        in_specs=[SMEM] * 2 + [ANY] * (1 + len(keys))
+        + [VMEM if s == landed else ANY for s in range(len(slots))] + [VMEM] * 4,
+        out_specs=[VMEM] * (sz.cores + 1),
         scratch_shapes=[pltpu.VMEM((sz.block, sz.width), F32)] + job_scratch(sz),
         compiler_params=SMALL,
         name="late_diag",
@@ -484,7 +477,7 @@
         return {k: v for k, v in m.items() if abs(k // per_row) < dist or (abs(k // per_row) == dist and k % per_row <= last_e)}
 
     far = sz.rows - 1
-    bounds = [(far - 1, per_row - 1, fixed - 2), (far, per_row - 2, fixed - 2)]
+    bounds = [(far - 2, per_row - 1, 0), (far - 1, per_row - 1, fixed - 2), (far, per_row - 2, fixed - 2)]
     far_term = inner(sz, pattern, green, slots[0], factor)
     far_term = lax.ppermute(far_term, "row", [(0, 1), (far, far - 1)])
 
@@ -493,7 +486,7 @@
         return early(sz, bounds[i], bounds[i - 1] if i else None, pattern, green,
                      upto(dist, last_e), slots[:s + 1], total)
 
-    total = part(0, None)
+    total = part(1, part(0, None))
     extra = []
     if sz.half > fixed:
         full = jnp.bool_(False)
@@ -508,10 +501,10 @@
         got = lax.cond(full, more, lambda g: jnp.zeros((sz.local_rows, block), BF16), green)
         got, total = lax.optimization_barrier((got, total))
         extra.append(got)
-    total = part(1, total)
+    total = part(2, total)
     near = (far, per_row - 2, sz.half)
-    *out, total = late_diag(sz, near, bounds[1], pattern, pole_weight, green, upto(far, per_row - 2),
-                            slots + extra, total, factor, diag_inverse, far_term)
+    *out, total = late_diag(sz, near, bounds[2], pattern, pole_weight, green, upto(far, per_row - 2),
+                            slots + extra, fixed - 1, total, factor, diag_inverse, far_term)
     last = (far, per_row - 1, sz.half)
     only = {k: v for k, v in m.items() if abs(k // per_row) == far and k % per_row == per_row - 1}
     off_out = late_off(sz, last, near, pattern, pole_weight, green, only, slots + extra, total)
@@ -523,7 +516,9 @@
         return ins
 
     diag, *sends = out
-    diag_in = swapped("pole", sends, [pole_perm(sz, step) for step in pole_steps(sz)])
+    diag_in = swapped("pole", sends, shifts(sz.poles, sz.cores, 1))
+    diag, *sends = fold(sz.outer, "pole", sz.cores, diag, diag_in)
+    diag_in = swapped("pole", sends, shifts(sz.poles, sz.outer, sz.cores))
     off, *sends = off_out
     off_in = swapped("pole", sends, shifts(sz.poles, sz.cores, 1))
     off, *sends = fold(sz.outer, "pole", sz.cores, off, off_in)

time: 122 us -> 115 us (0.943)
  waiting for transfers between devices: 49.2 us -> 43.7 us
  Pallas kernels: 23.1 us -> 26.1 us
  local copies, waits for them, and re-layouts: 4.95 us -> 1.97 us
    ppermute x6, waiting for transfers between devices: 0.02 us -> 12.9 us  [blocked(): lax.ppermute(a, 'row', [(i, i + 1) for i in range(step - 1, sz.rows - 1)])]
    ppermute x3, waiting for transfers between devices: 10.5 us -> 0.01 us  [blocked(): slots.append(lax.ppermute(sent, 'col', swap))]
    ppermute x6, waiting for transfers between devices: 22.3 us -> 16.6 us  [blocked(): lax.ppermute(b, 'row', [(i + 1, i) for i in range(sz.rows - step)])]
    ppermute x6, starting transfers between devices: 13.9 us -> 12 us  [blocked(): lax.ppermute(a, 'row', [(i, i + 1) for i in range(step - 1, sz.rows - 1)])]
    unnamed x28 -> x20, local copies, waits for them, and re-layouts: 2.59 us -> 0.85 us
    pallas_call x2 -> x3, Pallas kernels: 7.95 us -> 9.57 us  [early_call(): pl.pallas_call(functools.partial(early_kernel, sz, ready, before, keys, l...]
    ppermute x8 -> x7, waiting for transfers between devices: 12.1 us -> 10.6 us  [swapped(): ins.append(lax.ppermute(v, axis, perm))]
    ppermute x8 -> x7, starting transfers between devices: 7.51 us -> 7.54 us  [swapped(): ins.append(lax.ppermute(v, axis, perm))]
  transfers between devices with their start and end apart: 24 -> 23, of which waited for: 12 -> 11; matrix products, arithmetic and copies ran while one was open for 2% -> 2% of each run, Pallas kernels for 17% -> 18%
where the time goes in v4:
time: 115 us; the launch traced here: 114 us
  waiting for transfers between devices  43.7 us (38%)
  starting transfers between devices  37.7 us (33%)
  Pallas kernels  26.1 us (23%)
  between operations  2.83 us (2%)
  other arithmetic  2.22 us (2%)
  local copies, waits for them, and re-layouts  1.97 us (2%)
    ppermute x6, waiting for transfers between devices, blocked(): lax.ppermute(b, 'row', [(i + 1, i) for i in range(sz.rows - step)])  16.6 us
    ppermute x6, waiting for transfers between devices, blocked(): lax.ppermute(a, 'row', [(i, i + 1) for i in range(step - 1, sz.rows - 1)])  12.9 us
    ppermute x6, starting transfers between devices, blocked(): lax.ppermute(a, 'row', [(i, i + 1) for i in range(step - 1, sz.rows - 1)])  12 us
    ppermute x7, waiting for transfers between devices, swapped(): ins.append(lax.ppermute(v, axis, perm))  10.6 us
    pallas_call x3, Pallas kernels, early_call(): pl.pallas_call(functools.partial(early_kernel, sz, ready, before, keys, l...  9.57 us
    ppermute x6, starting transfers between devices, blocked(): lax.ppermute(b, 'row', [(i + 1, i) for i in range(sz.rows - step)])  7.73 us
    ppermute x7, starting transfers between devices, swapped(): ins.append(lax.ppermute(v, axis, perm))  7.54 us
    pallas_call x3, Pallas kernels, pick(): pl.pallas_call(functools.partial(pick_kernel, sz, slot, parts), out_shape...  7.41 us
  transfers between devices with their start and end apart: 23, of which 11 were waited for; matrix products, arithmetic and copies ran while one was open for 2% of the time, Pallas kernels for 18%

profile of v4, /device:TPU:0, one launch (start us, length us, event | category | flops | bytes accessed | tf_op | source)
XLA Modules:
  0.0 114.4 jit_solution(3699186608280256142)
XLA Ops:
  0.6 2.2 %shard_map.68 = bf16[1024,512]{1,0:T(8,128)(2,1)S(1)} custom-call(s32[2,8]{1,0:T(2,128)} %bitcast.5, bf16[1,1024,2048]{2,1,0:T(8,128)(2,1)} %g_local.9), custom_call_target="tpu_custom_call" | custom-call | tf_op jit(solution)/shard_map/pallas_call | solution.py:147
  2.8 3.1 %collective-permute-start.7 = (bf16[1024,512]{1,0:T(8,128)(2,1)S(1)}, bf16[1024,512]{1,0:T(8,128)(2,1)S(1)}, u32[]{:S(2)}, u32[]{:S(2)}) collective-permute-start(bf16[1024,512]{1,0:T(8,128)(2,1)S(1)} %shard_map.68), channel_id=1, source_target_pairs={{0,1},{1,0},{2,3},{3,2},{4,5},{5,4},{6,7},{7,6},{8,9},{9,8},{10,11... | collective-permute-start | bytes 3145736 | tf_op jit(solution)/shard_map/ppermute | solution.py:467
  6.0 4.3 %collective-permute-start.1 = (bf16[512,512]{1,0:T(8,128)(2,1)S(1)}, bf16[512,512]{1,0:T(8,128)(2,1)}, u32[]{:S(2)}, u32[]{:S(2)}) collective-permute-start(bf16[512,512]{1,0:T(8,128)(2,1)S(1)} %get-tuple-element.48.refs_1_), channel_id=1, source_target_pairs={{0,2},{2,4},{4,6},{1,3},{3,5},{5,7},{8,10},{10,12},{12,14},{9,11},... | collective-permute-start | bytes 1572872 | tf_op jit(solution)/shard_map/ppermute | solution.py:473
  10.3 2.7 %collective-permute-start.10 = (bf16[512,512]{1,0:T(8,128)(2,1)S(1)}, bf16[512,512]{1,0:T(8,128)(2,1)S(1)}, u32[]{:S(2)}, u32[]{:S(2)}) collective-permute-start(bf16[512,512]{1,0:T(8,128)(2,1)S(1)} %get-tuple-element.47.refs_0_), channel_id=1, source_target_pairs={{0,2},{2,4},{4,6},{1,3},{3,5},{5,7},{8,10},{10,12},{12,14},{9,11},... | collective-permute-start | bytes 1572872 | tf_op jit(solution)/shard_map/ppermute | solution.py:473
  13.0 1.3 %collective-permute-start.11 = (bf16[512,512]{1,0:T(8,128)(2,1)S(1)}, bf16[512,512]{1,0:T(8,128)(2,1)S(1)}, u32[]{:S(2)}, u32[]{:S(2)}) collective-permute-start(bf16[512,512]{1,0:T(8,128)(2,1)S(1)} %get-tuple-element.47.refs_0_), channel_id=1, source_target_pairs={{2,0},{4,2},{6,4},{3,1},{5,3},{7,5},{10,8},{12,10},{14,12},{11,9},... | collective-permute-start | bytes 1572872 | tf_op jit(solution)/shard_map/ppermute | solution.py:474
  14.3 1.3 %collective-permute-start.4 = (bf16[512,512]{1,0:T(8,128)(2,1)S(1)}, bf16[512,512]{1,0:T(8,128)(2,1)}, u32[]{:S(2)}, u32[]{:S(2)}) collective-permute-start(bf16[512,512]{1,0:T(8,128)(2,1)S(1)} %get-tuple-element.48.refs_1_), channel_id=1, source_target_pairs={{2,0},{4,2},{6,4},{3,1},{5,3},{7,5},{10,8},{12,10},{14,12},{11,9},... | collective-permute-start | bytes 1572872 | tf_op jit(solution)/shard_map/ppermute | solution.py:474
  15.6 2.6 %shard_map.69 = bf16[1024,512]{1,0:T(8,128)(2,1)} custom-call(s32[2,8]{1,0:T(2,128)S(1)} %bitcast.6, bf16[1,1024,2048]{2,1,0:T(8,128)(2,1)} %g_local.9), custom_call_target="tpu_custom_call" | custom-call | tf_op jit(solution)/shard_map/pallas_call | solution.py:147
  18.2 3.5 %collective-permute-done.1.refs_4_.refs_6_.refs_8_ = bf16[512,512]{1,0:T(8,128)(2,1)} collective-permute-done((bf16[512,512]{1,0:T(8,128)(2,1)S(1)}, bf16[512,512]{1,0:T(8,128)(2,1)}, u32[]{:S(2)}, u32[]{:S(2)}) %collective-permute-start.1) | collective-permute-done | bytes 524320 | tf_op jit(solution)/shard_map/ppermute | solution.py:473
  21.8 0.5 collective-permute-start.8
  22.3 9.3 %collective-permute-done.10.refs_2_ = bf16[512,512]{1,0:T(8,128)(2,1)S(1)} collective-permute-done((bf16[512,512]{1,0:T(8,128)(2,1)S(1)}, bf16[512,512]{1,0:T(8,128)(2,1)S(1)}, u32[]{:S(2)}, u32[]{:S(2)}) %collective-permute-start.10) | collective-permute-done | bytes 524320 | tf_op jit(solution)/shard_map/ppermute | solution.py:473
  31.6 1.4 %collective-permute-start.12 = (bf16[512,512]{1,0:T(8,128)(2,1)S(1)}, bf16[512,512]{1,0:T(8,128)(2,1)}, u32[]{:S(2)}, u32[]{:S(2)}) collective-permute-start(bf16[512,512]{1,0:T(8,128)(2,1)S(1)} %collective-permute-done.10.refs_2_), channel_id=1, source_target_pairs={{2,4},{4,6},{3,5},{5,7},{10,12},{12,14},{11,13},{13,15},{18,20},{2... | collective-permute-start | bytes 1572872 | tf_op jit(solution)/shard_map/ppermute | solution.py:473
  33.0 1.3 %collective-permute-start.13 = (bf16[512,512]{1,0:T(8,128)(2,1)S(1)}, bf16[512,512]{1,0:T(8,128)(2,1)}, u32[]{:S(2)}, u32[]{:S(2)}) collective-permute-start(bf16[512,512]{1,0:T(8,128)(2,1)S(1)} %collective-permute-done.11.refs_3_), channel_id=1, source_target_pairs={{2,0},{4,2},{3,1},{5,3},{10,8},{12,10},{11,9},{13,11},{18,16},{20,... | collective-permute-start | bytes 1572872 | tf_op jit(solution)/shard_map/ppermute | solution.py:474
  34.3 4.7 %collective-permute-done.4.refs_5_.refs_7_.refs_9_ = bf16[512,512]{1,0:T(8,128)(2,1)} collective-permute-done((bf16[512,512]{1,0:T(8,128)(2,1)S(1)}, bf16[512,512]{1,0:T(8,128)(2,1)}, u32[]{:S(2)}, u32[]{:S(2)}) %collective-permute-start.4) | collective-permute-done | bytes 524320 | tf_op jit(solution)/shard_map/ppermute | solution.py:474
  39.0 1.4 %collective-permute-start.2 = (bf16[512,512]{1,0:T(8,128)(2,1)}, bf16[512,512]{1,0:T(8,128)(2,1)}, u32[]{:S(2)}, u32[]{:S(2)}) collective-permute-start(bf16[512,512]{1,0:T(8,128)(2,1)} %collective-permute-done.1.refs_4_.refs_6_.refs_8_), channel_id=1, source_target_pairs={{2,4},{4,6},{3,5},{5,7},{10,12},{12,14},{11,13},{13,15},{18,20},{2... | collective-permute-start | bytes 1572872 | tf_op jit(solution)/shard_map/ppermute | solution.py:473
  40.5 1.3 %collective-permute-start.5 = (bf16[512,512]{1,0:T(8,128)(2,1)}, bf16[512,512]{1,0:T(8,128)(2,1)}, u32[]{:S(2)}, u32[]{:S(2)}) collective-permute-start(bf16[512,512]{1,0:T(8,128)(2,1)} %collective-permute-done.4.refs_5_.refs_7_.refs_9_), channel_id=1, source_target_pairs={{2,0},{4,2},{3,1},{5,3},{10,8},{12,10},{11,9},{13,11},{18,16},{20,... | collective-permute-start | bytes 1572872 | tf_op jit(solution)/shard_map/ppermute | solution.py:474
  41.8 2.6 %shard_map.70 = bf16[1024,512]{1,0:T(8,128)(2,1)} custom-call(s32[2,8]{1,0:T(2,128)S(1)} %bitcast.7, bf16[1,1024,2048]{2,1,0:T(8,128)(2,1)} %g_local.9), custom_call_target="tpu_custom_call" | custom-call | tf_op jit(solution)/shard_map/pallas_call | solution.py:147
  44.5 0.6 collective-permute-start.9
  45.0 8.1 %collective-permute-done.13.refs_5_ = bf16[512,512]{1,0:T(8,128)(2,1)} collective-permute-done((bf16[512,512]{1,0:T(8,128)(2,1)S(1)}, bf16[512,512]{1,0:T(8,128)(2,1)}, u32[]{:S(2)}, u32[]{:S(2)}) %collective-permute-start.13) | collective-permute-done | bytes 524320 | tf_op jit(solution)/shard_map/ppermute | solution.py:474
  53.1 1.5 %collective-permute-start.14 = (bf16[512,512]{1,0:T(8,128)(2,1)}, bf16[512,512]{1,0:T(8,128)(2,1)}, u32[]{:S(2)}, u32[]{:S(2)}) collective-permute-start(bf16[512,512]{1,0:T(8,128)(2,1)} %collective-permute-done.12.refs_4_), channel_id=1, source_target_pairs={{4,6},{5,7},{12,14},{13,15},{20,22},{21,23},{28,30},{29,31}} | collective-permute-start | bytes 1572872 | tf_op jit(solution)/shard_map/ppermute | solution.py:473
  54.6 0.7 compare_reduce_fusion
  56.5 5.8 %shard_map.71.refs_12_ = f32[1024,512]{1,0:T(8,128)S(1)} custom-call(s32[2,8]{1,0:T(2,128)S(1)} %bitcast.9, bf16[1,1024,2048]{2,1,0:T(8,128)(2,1)} %g_local.9, bf16[512,512]{1,0:T(8,128)(2,1)} %copy-done.3, bf16[512,512]{1,0:T(8,128)(2,1)} %copy-done.4, bf16[512,512]{1,0:T(8,128)(2,1)} %copy-done.5, bf16[512,512]{1,0:T(8,128)(2,1)} %copy-done.6, ...), custom_call_target="tpu_custom_call" | custom-call | tf_op jit(solution)/shard_map/pallas_call | solution.py:261
  62.3 2.8 %shard_map.72.refs_14_ = f32[1024,512]{1,0:T(8,128)S(1)} custom-call(s32[2,8]{1,0:T(2,128)S(1)} %bitcast.10, bf16[1,1024,2048]{2,1,0:T(8,128)(2,1)} %g_local.9, bf16[512,512]{1,0:T(8,128)(2,1)} %copy-done.3, bf16[512,512]{1,0:T(8,128)(2,1)} %copy-done.4, bf16[512,512]{1,0:T(8,128)(2,1)} %copy-done.5, ...), custom_call_target="tpu_custom_call", output_to_operand_aliasing={{}: (14, {})} | custom-call | tf_op jit(solution)/shard_map/pallas_call | solution.py:261
  65.2 1.3 %collective-permute-start.15 = (bf16[512,512]{1,0:T(8,128)(2,1)}, bf16[512,512]{1,0:T(8,128)(2,1)}, u32[]{:S(2)}, u32[]{:S(2)}) collective-permute-start(bf16[512,512]{1,0:T(8,128)(2,1)} %collective-permute-done.13.refs_5_), channel_id=1, source_target_pairs={{2,0},{3,1},{10,8},{11,9},{18,16},{19,17},{26,24},{27,25}} | collective-permute-start | bytes 1572872 | tf_op jit(solution)/shard_map/ppermute | solution.py:474
  66.5 3.3 %inner.1 = bf16[512,512]{1,0:T(8,128)(2,1)} custom-call(s32[2,8]{1,0:T(2,128)S(1)} %bitcast.11, bf16[1,1024,2048]{2,1,0:T(8,128)(2,1)} %g_local.9, bf16[1024,512]{1,0:T(8,128)(2,1)} %copy-done.2, bf16[1,1024,512]{2,1,0:T(8,128)(2,1)S(1)} %copy-done), custom_call_target="tpu_custom_call" | custom-call | tf_op jit(solution)/shard_map/inner/pallas_call | solution.py:301
  69.8 6.2 %collective-permute-start.16 = (bf16[512,512]{1,0:T(8,128)(2,1)}, bf16[512,512]{1,0:T(8,128)(2,1)}, u32[]{:S(2)}, u32[]{:S(2)}) collective-permute-start(bf16[512,512]{1,0:T(8,128)(2,1)} %inner.1), channel_id=1, source_target_pairs={{0,2},{6,4},{1,3},{7,5},{8,10},{14,12},{9,11},{15,13},{16,18},{22,... | collective-permute-start | bytes 1572872 | tf_op jit(solution)/shard_map/ppermute | solution.py:482
  76.0 1.1 conditional.1
  76.0 1.1 broadcast.7
  77.0 0.7 collective-permute-start.3
  77.7 1.3 %collective-permute-start.6 = (bf16[512,512]{1,0:T(8,128)(2,1)}, bf16[512,512]{1,0:T(8,128)(2,1)S(1)}, u32[]{:S(2)}, u32[]{:S(2)}) collective-permute-start(bf16[512,512]{1,0:T(8,128)(2,1)} %collective-permute-done.5.refs_9_.refs_11_), channel_id=1, source_target_pairs={{2,0},{3,1},{10,8},{11,9},{18,16},{19,17},{26,24},{27,25}} | collective-permute-start | bytes 1572872 | tf_op jit(solution)/shard_map/ppermute | solution.py:474
  79.7 1.0 shard_map.73.refs_16_
  80.7 3.6 %collective-permute-done.16.refs_19_ = bf16[512,512]{1,0:T(8,128)(2,1)} collective-permute-done((bf16[512,512]{1,0:T(8,128)(2,1)}, bf16[512,512]{1,0:T(8,128)(2,1)}, u32[]{:S(2)}, u32[]{:S(2)}) %collective-permute-start.16) | collective-permute-done | bytes 524320 | tf_op jit(solution)/shard_map/ppermute | solution.py:482
  84.3 2.7 %late_diag.1 = (f32[256,512]{1,0:T(8,128)S(1)}, bf16[256,512]{1,0:T(8,128)(2,1)S(1)}, f32[1024,512]{1,0:T(8,128)S(1)}) custom-call(s32[2,8]{1,0:T(2,128)S(1)} %bitcast.14, f32[1]{0:T(128)S(6)} %copy.13.weight, bf16[1,1024,2048]{2,1,0:T(8,128)(2,1)} %g_local.9, bf16[512,512]{1,0:T(8,128)(2,1)} %copy-done.3, bf16[512,512]{1,0:T(8,128)(2,1)} %copy-done.4, ...), custom_call_target="tpu_custom_call" | custom-call | tf_op jit(solution)/shard_map/late_diag/pallas_call | solution.py:367
  87.0 3.8 %collective-permute-done.6.refs_1_ = bf16[512,512]{1,0:T(8,128)(2,1)S(1)} collective-permute-done((bf16[512,512]{1,0:T(8,128)(2,1)}, bf16[512,512]{1,0:T(8,128)(2,1)S(1)}, u32[]{:S(2)}, u32[]{:S(2)}) %collective-permute-start.6) | collective-permute-done | bytes 524320 | tf_op jit(solution)/shard_map/ppermute | solution.py:474
  90.8 0.8 copy-done.8
  91.6 2.9 %late_off.1 = (f32[512,512]{1,0:T(8,128)S(1)}, bf16[512,512]{1,0:T(8,128)(2,1)S(1)}) custom-call(s32[2,8]{1,0:T(2,128)S(1)} %bitcast.15, f32[1]{0:T(128)S(6)} %copy.13.weight, bf16[1,1024,2048]{2,1,0:T(8,128)(2,1)} %g_local.9, bf16[512,512]{1,0:T(8,128)(2,1)} %copy-done.7, bf16[512,512]{1,0:T(8,128)(2,1)} %copy-done.8, bf16[1024,512]{1,0:T(8,128)(2,1)} %copy-done.2, ...), custom_call_target="tpu_custom_call" | custom-call | tf_op jit(solution)/shard_map/late_off/pallas_call | solution.py:405
  94.6 0.5 collective-permute-start.19
  95.1 1.8 %collective-permute-done.19.refs_0_ = bf16[256,512]{1,0:T(8,128)(2,1)S(1)} collective-permute-done((bf16[256,512]{1,0:T(8,128)(2,1)S(1)}, bf16[256,512]{1,0:T(8,128)(2,1)S(1)}, u32[]{:S(2)}, u32[]{:S(2)}) %collective-permute-start.19) | collective-permute-done | bytes 262176 | tf_op jit(solution)/shard_map/ppermute | solution.py:515
  96.9 1.6 %collective-permute-start.20 = (bf16[128,512]{1,0:T(8,128)(2,1)S(1)}, bf16[128,512]{1,0:T(8,128)(2,1)S(1)}, u32[]{:S(2)}, u32[]{:S(2)}) collective-permute-start(bf16[128,512]{1,0:T(8,128)(2,1)S(1)} %get-tuple-element.40), channel_id=1, source_target_pairs={{0,16},{8,24},{16,0},{24,8},{1,17},{9,25},{17,1},{25,9},{2,18},{10... | collective-permute-start | bytes 393224 | tf_op jit(solution)/shard_map/ppermute | solution.py:515
  98.5 4.1 %collective-permute-done.20.refs_0_ = bf16[128,512]{1,0:T(8,128)(2,1)S(1)} collective-permute-done((bf16[128,512]{1,0:T(8,128)(2,1)S(1)}, bf16[128,512]{1,0:T(8,128)(2,1)S(1)}, u32[]{:S(2)}, u32[]{:S(2)}) %collective-permute-start.20) | collective-permute-done | bytes 131104 | tf_op jit(solution)/shard_map/ppermute | solution.py:515
  102.6 1.0 collective-permute-start.22
  103.7 2.8 %collective-permute-start.23 = (bf16[32,512]{1,0:T(8,128)(2,1)S(1)}, bf16[32,512]{1,0:T(8,128)(2,1)S(1)}, u32[]{:S(2)}, u32[]{:S(2)}) collective-permute-start(bf16[32,512]{1,0:T(8,128)(2,1)S(1)} %get-tuple-element.44), channel_id=1, source_target_pairs={{0,6},{2,0},{4,2},{6,4},{1,7},{3,1},{5,3},{7,5},{8,14},{10,8},{12,... | collective-permute-start | bytes 98312 | tf_op jit(solution)/shard_map/ppermute | solution.py:515
  106.5 0.1 shard_map.74
  106.5 1.6 %collective-permute-start.18 = (bf16[256,512]{1,0:T(8,128)(2,1)S(1)}, bf16[256,512]{1,0:T(8,128)(2,1)S(1)}, u32[]{:S(2)}, u32[]{:S(2)}) collective-permute-start(bf16[256,512]{1,0:T(8,128)(2,1)S(1)} %get-tuple-element.36), channel_id=1, source_target_pairs={{0,16},{8,24},{16,0},{24,8},{1,17},{9,25},{17,1},{25,9},{2,18},{10... | collective-permute-start | bytes 786440 | tf_op jit(solution)/shard_map/ppermute | solution.py:515
  108.1 0.3 collective-permute-done.21
  108.4 0.5 collective-permute-done.23
  108.9 0.6 convert_add_fusion.1
  109.5 4.0 %collective-permute-done.18 = bf16[256,512]{1,0:T(8,128)(2,1)S(1)} collective-permute-done((bf16[256,512]{1,0:T(8,128)(2,1)S(1)}, bf16[256,512]{1,0:T(8,128)(2,1)S(1)}, u32[]{:S(2)}, u32[]{:S(2)}) %collective-permute-start.18) | collective-permute-done | bytes 262176 | tf_op jit(solution)/shard_map/ppermute | solution.py:515
  113.5 0.9 convert_add_fusion
  (36 shorter events, 0.3 us)
Async XLA Ops:
  0.6 5.3 %copy-start = (bf16[1,1024,512]{2,1,0:T(8,128)(2,1)S(1)}, bf16[1,1024,512]{2,1,0:T(8,128)(2,1)}, u32[]{:S(2)}) copy-start(bf16[1,1024,512]{2,1,0:T(8,128)(2,1)} %refs_17_.1) | copy-start | bytes 3145732
  2.8 12.8 %copy-start.9 = (s32[8,2]{0,1:T(2,128)S(1)}, s32[8,2]{0,1:T(2,128)}, u32[]{:S(2)}) copy-start(s32[8,2]{0,1:T(2,128)} %param.11) | copy-start | bytes 196
  2.8 37.7 %collective-permute-start.7 = (bf16[1024,512]{1,0:T(8,128)(2,1)S(1)}, bf16[1024,512]{1,0:T(8,128)(2,1)S(1)}, u32[]{:S(2)}, u32[]{:S(2)}) collective-permute-start(bf16[1024,512]{1,0:T(8,128)(2,1)S(1)} %shard_map.68), channel_id=1, source_target_pairs={{0,1},{1,0},{2,3},{3,2},{4,5},{5,4},{6,7},{7,6},{8,9},{9,8},{10,11... | collective-permute-start | bytes 3145736 | tf_op jit(solution)/shard_map/ppermute | solution.py:467
  6.0 12.3 %copy-start.3 = (bf16[512,512]{1,0:T(8,128)(2,1)}, bf16[512,512]{1,0:T(8,128)(2,1)S(1)}, u32[]{:S(2)}) copy-start(bf16[512,512]{1,0:T(8,128)(2,1)S(1)} %get-tuple-element.47.refs_0_) | copy-start | bytes 1572868
  6.0 12.3 %copy-start.4 = (bf16[512,512]{1,0:T(8,128)(2,1)}, bf16[512,512]{1,0:T(8,128)(2,1)S(1)}, u32[]{:S(2)}) copy-start(bf16[512,512]{1,0:T(8,128)(2,1)S(1)} %get-tuple-element.48.refs_1_) | copy-start | bytes 1572868
  6.0 15.8 %collective-permute-start.1 = (bf16[512,512]{1,0:T(8,128)(2,1)S(1)}, bf16[512,512]{1,0:T(8,128)(2,1)}, u32[]{:S(2)}, u32[]{:S(2)}) collective-permute-start(bf16[512,512]{1,0:T(8,128)(2,1)S(1)} %get-tuple-element.48.refs_1_), channel_id=1, source_target_pairs={{0,2},{2,4},{4,6},{1,3},{3,5},{5,7},{8,10},{10,12},{12,14},{9,11},... | collective-permute-start | bytes 1572872 | tf_op jit(solution)/shard_map/ppermute | solution.py:473
  10.3 21.3 %collective-permute-start.10 = (bf16[512,512]{1,0:T(8,128)(2,1)S(1)}, bf16[512,512]{1,0:T(8,128)(2,1)S(1)}, u32[]{:S(2)}, u32[]{:S(2)}) collective-permute-start(bf16[512,512]{1,0:T(8,128)(2,1)S(1)} %get-tuple-element.47.refs_0_), channel_id=1, source_target_pairs={{0,2},{2,4},{4,6},{1,3},{3,5},{5,7},{8,10},{10,12},{12,14},{9,11},... | collective-permute-start | bytes 1572872 | tf_op jit(solution)/shard_map/ppermute | solution.py:473
  13.0 20.0 %collective-permute-start.11 = (bf16[512,512]{1,0:T(8,128)(2,1)S(1)}, bf16[512,512]{1,0:T(8,128)(2,1)S(1)}, u32[]{:S(2)}, u32[]{:S(2)}) collective-permute-start(bf16[512,512]{1,0:T(8,128)(2,1)S(1)} %get-tuple-element.47.refs_0_), channel_id=1, source_target_pairs={{2,0},{4,2},{6,4},{3,1},{5,3},{7,5},{10,8},{12,10},{14,12},{11,9},... | collective-permute-start | bytes 1572872 | tf_op jit(solution)/shard_map/ppermute | solution.py:474
  14.3 24.8 %collective-permute-start.4 = (bf16[512,512]{1,0:T(8,128)(2,1)S(1)}, bf16[512,512]{1,0:T(8,128)(2,1)}, u32[]{:S(2)}, u32[]{:S(2)}) collective-permute-start(bf16[512,512]{1,0:T(8,128)(2,1)S(1)} %get-tuple-element.48.refs_1_), channel_id=1, source_target_pairs={{2,0},{4,2},{6,4},{3,1},{5,3},{7,5},{10,8},{12,10},{14,12},{11,9},... | collective-permute-start | bytes 1572872 | tf_op jit(solution)/shard_map/ppermute | solution.py:474
  21.8 40.6 %collective-permute-start.8 = (bf16[1024,512]{1,0:T(8,128)(2,1)}, bf16[1024,512]{1,0:T(8,128)(2,1)}, u32[]{:S(2)}, u32[]{:S(2)}) collective-permute-start(bf16[1024,512]{1,0:T(8,128)(2,1)} %shard_map.69), channel_id=1, source_target_pairs={{0,1},{1,0},{2,3},{3,2},{4,5},{5,4},{6,7},{7,6},{8,9},{9,8},{10,11... | collective-permute-start | bytes 3145736 | tf_op jit(solution)/shard_map/ppermute | solution.py:467
  31.6 12.9 %copy-start.5 = (bf16[512,512]{1,0:T(8,128)(2,1)}, bf16[512,512]{1,0:T(8,128)(2,1)S(1)}, u32[]{:S(2)}) copy-start(bf16[512,512]{1,0:T(8,128)(2,1)S(1)} %collective-permute-done.10.refs_2_) | copy-start | bytes 1572868
  31.6 12.9 %collective-permute-start.12 = (bf16[512,512]{1,0:T(8,128)(2,1)S(1)}, bf16[512,512]{1,0:T(8,128)(2,1)}, u32[]{:S(2)}, u32[]{:S(2)}) collective-permute-start(bf16[512,512]{1,0:T(8,128)(2,1)S(1)} %collective-permute-done.10.refs_2_), channel_id=1, source_target_pairs={{2,4},{4,6},{3,5},{5,7},{10,12},{12,14},{11,13},{13,15},{18,20},{2... | collective-permute-start | bytes 1572872 | tf_op jit(solution)/shard_map/ppermute | solution.py:473
  33.0 11.4 %copy-start.6 = (bf16[512,512]{1,0:T(8,128)(2,1)}, bf16[512,512]{1,0:T(8,128)(2,1)S(1)}, u32[]{:S(2)}) copy-start(bf16[512,512]{1,0:T(8,128)(2,1)S(1)} %collective-permute-done.11.refs_3_) | copy-start | bytes 1572868
  33.0 20.1 %collective-permute-start.13 = (bf16[512,512]{1,0:T(8,128)(2,1)S(1)}, bf16[512,512]{1,0:T(8,128)(2,1)}, u32[]{:S(2)}, u32[]{:S(2)}) collective-permute-start(bf16[512,512]{1,0:T(8,128)(2,1)S(1)} %collective-permute-done.11.refs_3_), channel_id=1, source_target_pairs={{2,0},{4,2},{3,1},{5,3},{10,8},{12,10},{11,9},{13,11},{18,16},{20,... | collective-permute-start | bytes 1572872 | tf_op jit(solution)/shard_map/ppermute | solution.py:474
  39.0 23.3 %collective-permute-start.2 = (bf16[512,512]{1,0:T(8,128)(2,1)}, bf16[512,512]{1,0:T(8,128)(2,1)}, u32[]{:S(2)}, u32[]{:S(2)}) collective-permute-start(bf16[512,512]{1,0:T(8,128)(2,1)} %collective-permute-done.1.refs_4_.refs_6_.refs_8_), channel_id=1, source_target_pairs={{2,4},{4,6},{3,5},{5,7},{10,12},{12,14},{11,13},{13,15},{18,20},{2... | collective-permute-start | bytes 1572872 | tf_op jit(solution)/shard_map/ppermute | solution.py:473
  40.5 4.0 %copy-start.2 = (bf16[1024,512]{1,0:T(8,128)(2,1)}, bf16[1024,512]{1,0:T(8,128)(2,1)S(1)}, u32[]{:S(2)}) copy-start(bf16[1024,512]{1,0:T(8,128)(2,1)S(1)} %collective-permute-done.7.refs_6_.refs_10_.refs_12_.slot.refs_2_) | copy-start | bytes 3145732
  40.5 21.8 %collective-permute-start.5 = (bf16[512,512]{1,0:T(8,128)(2,1)}, bf16[512,512]{1,0:T(8,128)(2,1)}, u32[]{:S(2)}, u32[]{:S(2)}) collective-permute-start(bf16[512,512]{1,0:T(8,128)(2,1)} %collective-permute-done.4.refs_5_.refs_7_.refs_9_), channel_id=1, source_target_pairs={{2,0},{4,2},{3,1},{5,3},{10,8},{12,10},{11,9},{13,11},{18,16},{20,... | collective-permute-start | bytes 1572872 | tf_op jit(solution)/shard_map/ppermute | solution.py:474
  44.5 36.2 %collective-permute-start.9 = (bf16[1024,512]{1,0:T(8,128)(2,1)}, bf16[1024,512]{1,0:T(8,128)(2,1)}, u32[]{:S(2)}, u32[]{:S(2)}) collective-permute-start(bf16[1024,512]{1,0:T(8,128)(2,1)} %shard_map.70), channel_id=1, source_target_pairs={{0,1},{1,0},{2,3},{3,2},{4,5},{5,4},{6,7},{7,6},{8,9},{9,8},{10,11... | collective-permute-start | bytes 3145736 | tf_op jit(solution)/shard_map/ppermute | solution.py:467
  53.1 24.6 %collective-permute-start.14 = (bf16[512,512]{1,0:T(8,128)(2,1)}, bf16[512,512]{1,0:T(8,128)(2,1)}, u32[]{:S(2)}, u32[]{:S(2)}) collective-permute-start(bf16[512,512]{1,0:T(8,128)(2,1)} %collective-permute-done.12.refs_4_), channel_id=1, source_target_pairs={{4,6},{5,7},{12,14},{13,15},{20,22},{21,23},{28,30},{29,31}} | collective-permute-start | bytes 1572872 | tf_op jit(solution)/shard_map/ppermute | solution.py:473
  65.2 14.6 %collective-permute-start.15 = (bf16[512,512]{1,0:T(8,128)(2,1)}, bf16[512,512]{1,0:T(8,128)(2,1)}, u32[]{:S(2)}, u32[]{:S(2)}) collective-permute-start(bf16[512,512]{1,0:T(8,128)(2,1)} %collective-permute-done.13.refs_5_), channel_id=1, source_target_pairs={{2,0},{3,1},{10,8},{11,9},{18,16},{19,17},{26,24},{27,25}} | collective-permute-start | bytes 1572872 | tf_op jit(solution)/shard_map/ppermute | solution.py:474
  69.8 14.5 %collective-permute-start.16 = (bf16[512,512]{1,0:T(8,128)(2,1)}, bf16[512,512]{1,0:T(8,128)(2,1)}, u32[]{:S(2)}, u32[]{:S(2)}) collective-permute-start(bf16[512,512]{1,0:T(8,128)(2,1)} %inner.1), channel_id=1, source_target_pairs={{0,2},{6,4},{1,3},{7,5},{8,10},{14,12},{9,11},{15,13},{16,18},{22,... | collective-permute-start | bytes 1572872 | tf_op jit(solution)/shard_map/ppermute | solution.py:482
  77.0 9.9 %collective-permute-start.3 = (bf16[512,512]{1,0:T(8,128)(2,1)}, bf16[512,512]{1,0:T(8,128)(2,1)S(1)}, u32[]{:S(2)}, u32[]{:S(2)}) collective-permute-start(bf16[512,512]{1,0:T(8,128)(2,1)} %collective-permute-done.2.refs_8_.refs_10_), channel_id=1, source_target_pairs={{4,6},{5,7},{12,14},{13,15},{20,22},{21,23},{28,30},{29,31}} | collective-permute-start | bytes 1572872 | tf_op jit(solution)/shard_map/ppermute | solution.py:473
  77.7 13.1 %collective-permute-start.6 = (bf16[512,512]{1,0:T(8,128)(2,1)}, bf16[512,512]{1,0:T(8,128)(2,1)S(1)}, u32[]{:S(2)}, u32[]{:S(2)}) collective-permute-start(bf16[512,512]{1,0:T(8,128)(2,1)} %collective-permute-done.5.refs_9_.refs_11_), channel_id=1, source_target_pairs={{2,0},{3,1},{10,8},{11,9},{18,16},{19,17},{26,24},{27,25}} | collective-permute-start | bytes 1572872 | tf_op jit(solution)/shard_map/ppermute | solution.py:474
  79.7 4.6 %copy-start.1 = (bf16[1,128,512]{2,1,0:T(8,128)(2,1)S(1)}, bf16[1,128,512]{2,1,0:T(8,128)(2,1)}, u32[]{:S(2)}) copy-start(bf16[1,128,512]{2,1,0:T(8,128)(2,1)} %refs_18_.1) | copy-start | bytes 393220
  87.0 3.8 %copy-start.7 = (bf16[512,512]{1,0:T(8,128)(2,1)}, bf16[512,512]{1,0:T(8,128)(2,1)S(1)}, u32[]{:S(2)}) copy-start(bf16[512,512]{1,0:T(8,128)(2,1)S(1)} %collective-permute-done.3.refs_0_) | copy-start | bytes 1572868
  90.8 0.8 copy-start.8
  94.5 11.9 %collective-permute-start.17 = (bf16[512,512]{1,0:T(8,128)(2,1)S(1)}, bf16[512,512]{1,0:T(8,128)(2,1)S(1)}, u32[]{:S(2)}, u32[]{:S(2)}) collective-permute-start(bf16[512,512]{1,0:T(8,128)(2,1)S(1)} %get-tuple-element.34), channel_id=1, source_target_pairs={{0,8},{8,0},{16,24},{24,16},{1,9},{9,1},{17,25},{25,17},{2,10},{10... | collective-permute-start | bytes 1572872 | tf_op jit(solution)/shard_map/ppermute | solution.py:515
  94.6 2.3 %collective-permute-start.19 = (bf16[256,512]{1,0:T(8,128)(2,1)S(1)}, bf16[256,512]{1,0:T(8,128)(2,1)S(1)}, u32[]{:S(2)}, u32[]{:S(2)}) collective-permute-start(bf16[256,512]{1,0:T(8,128)(2,1)S(1)} %get-tuple-element.38), channel_id=1, source_target_pairs={{0,8},{8,0},{16,24},{24,16},{1,9},{9,1},{17,25},{25,17},{2,10},{10... | collective-permute-start | bytes 786440 | tf_op jit(solution)/shard_map/ppermute | solution.py:515
  96.9 5.6 %collective-permute-start.20 = (bf16[128,512]{1,0:T(8,128)(2,1)S(1)}, bf16[128,512]{1,0:T(8,128)(2,1)S(1)}, u32[]{:S(2)}, u32[]{:S(2)}) collective-permute-start(bf16[128,512]{1,0:T(8,128)(2,1)S(1)} %get-tuple-element.40), channel_id=1, source_target_pairs={{0,16},{8,24},{16,0},{24,8},{1,17},{9,25},{17,1},{25,9},{2,18},{10... | collective-permute-start | bytes 393224 | tf_op jit(solution)/shard_map/ppermute | solution.py:515
  102.6 5.9 %collective-permute-start.21 = (bf16[32,512]{1,0:T(8,128)(2,1)S(1)}, bf16[32,512]{1,0:T(8,128)(2,1)S(1)}, u32[]{:S(2)}, u32[]{:S(2)}) collective-permute-start(bf16[32,512]{1,0:T(8,128)(2,1)S(1)} %get-tuple-element.42), channel_id=1, source_target_pairs={{0,2},{2,4},{4,6},{6,0},{1,3},{3,5},{5,7},{7,1},{8,10},{10,12},{12... | collective-permute-start | bytes 98312 | tf_op jit(solution)/shard_map/ppermute | solution.py:515
  102.6 5.8 %collective-permute-start.22 = (bf16[32,512]{1,0:T(8,128)(2,1)S(1)}, bf16[32,512]{1,0:T(8,128)(2,1)S(1)}, u32[]{:S(2)}, u32[]{:S(2)}) collective-permute-start(bf16[32,512]{1,0:T(8,128)(2,1)S(1)} %get-tuple-element.43), channel_id=1, source_target_pairs={{0,4},{2,6},{4,0},{6,2},{1,5},{3,7},{5,1},{7,3},{8,12},{10,14},{12... | collective-permute-start | bytes 98312 | tf_op jit(solution)/shard_map/ppermute | solution.py:515
  103.7 5.3 %collective-permute-start.23 = (bf16[32,512]{1,0:T(8,128)(2,1)S(1)}, bf16[32,512]{1,0:T(8,128)(2,1)S(1)}, u32[]{:S(2)}, u32[]{:S(2)}) collective-permute-start(bf16[32,512]{1,0:T(8,128)(2,1)S(1)} %get-tuple-element.44), channel_id=1, source_target_pairs={{0,6},{2,0},{4,2},{6,4},{1,7},{3,1},{5,3},{7,5},{8,14},{10,8},{12,... | collective-permute-start | bytes 98312 | tf_op jit(solution)/shard_map/ppermute | solution.py:515
  106.5 7.0 %collective-permute-start.18 = (bf16[256,512]{1,0:T(8,128)(2,1)S(1)}, bf16[256,512]{1,0:T(8,128)(2,1)S(1)}, u32[]{:S(2)}, u32[]{:S(2)}) collective-permute-start(bf16[256,512]{1,0:T(8,128)(2,1)S(1)} %get-tuple-element.36), channel_id=1, source_target_pairs={{0,16},{8,24},{16,0},{24,8},{1,17},{9,25},{17,1},{25,9},{2,18},{10... | collective-permute-start | bytes 786440 | tf_op jit(solution)/shard_map/ppermute | solution.py:515

commit v5 on v4

--- a/solution.py
+++ b/solution.py
@@ -427,7 +427,8 @@
         return v
 
     for s, send in enumerate(sends):
-        send[...] = part(lax.rem(me + s + 1, group)).astype(BF16)
+        to = me ^ (s + 1) if group & (group - 1) == 0 else lax.rem(me + s + 1, group)
+        send[...] = part(to).astype(BF16)
     own[...] = part(me)
 
 
@@ -449,7 +450,8 @@
         perm = []
         for i in range(size):
             d = (i // stride) % group
-            perm.append((i, i + ((d + step) % group - d) * stride))
+            to = d ^ step if group & (group - 1) == 0 else (d + step) % group
+            perm.append((i, i + (to - d) * stride))
         perms.append(perm)
     return perms
 

time: 115 us -> 115 us (level)
  transfers between devices with their start and end apart: 23 -> 23, of which waited for: 11 -> 10; matrix products, arithmetic and copies ran while one was open for 2% -> 2% of each run, Pallas kernels for 18% -> 18%
where the time goes in v5:
time: 115 us
  waiting for transfers between devices  43.4 us (38%)
  starting transfers between devices  38.2 us (33%)
  Pallas kernels  26.1 us (23%)
  between operations  2.83 us (2%)
  other arithmetic  2.22 us (2%)
  local copies, waits for them, and re-layouts  1.97 us (2%)
    ppermute x6, waiting for transfers between devices, blocked(): lax.ppermute(b, 'row', [(i + 1, i) for i in range(sz.rows - step)])  16.6 us
    ppermute x6, waiting for transfers between devices, blocked(): lax.ppermute(a, 'row', [(i, i + 1) for i in range(step - 1, sz.rows - 1)])  12.9 us
    ppermute x6, starting transfers between devices, blocked(): lax.ppermute(a, 'row', [(i, i + 1) for i in range(step - 1, sz.rows - 1)])  12 us
    ppermute x7, waiting for transfers between devices, swapped(): ins.append(lax.ppermute(v, axis, perm))  10.3 us
    pallas_call x3, Pallas kernels, early_call(): pl.pallas_call(functools.partial(early_kernel, sz, ready, before, keys, l...  9.57 us
    ppermute x7, starting transfers between devices, swapped(): ins.append(lax.ppermute(v, axis, perm))  8.12 us
    ppermute x6, starting transfers between devices, blocked(): lax.ppermute(b, 'row', [(i + 1, i) for i in range(sz.rows - step)])  7.73 us
    pallas_call x3, Pallas kernels, pick(): pl.pallas_call(functools.partial(pick_kernel, sz, slot, parts), out_shape...  7.41 us
  transfers between devices with their start and end apart: 23, of which 10 were waited for; matrix products, arithmetic and copies ran while one was open for 2% of the time, Pallas kernels for 18%

profile of v5, /device:TPU:0, one launch (start us, length us, event | category | flops | bytes accessed | tf_op | source)
XLA Modules:
  0.0 114.7 jit_solution(14255124937163444663)
XLA Ops:
  0.6 2.2 %shard_map.68 = bf16[1024,512]{1,0:T(8,128)(2,1)S(1)} custom-call(s32[2,8]{1,0:T(2,128)} %bitcast.5, bf16[1,1024,2048]{2,1,0:T(8,128)(2,1)} %g_local.9), custom_call_target="tpu_custom_call" | custom-call | tf_op jit(solution)/shard_map/pallas_call | solution.py:147
  2.8 3.1 %collective-permute-start.7 = (bf16[1024,512]{1,0:T(8,128)(2,1)S(1)}, bf16[1024,512]{1,0:T(8,128)(2,1)S(1)}, u32[]{:S(2)}, u32[]{:S(2)}) collective-permute-start(bf16[1024,512]{1,0:T(8,128)(2,1)S(1)} %shard_map.68), channel_id=1, source_target_pairs={{0,1},{1,0},{2,3},{3,2},{4,5},{5,4},{6,7},{7,6},{8,9},{9,8},{10,11... | collective-permute-start | bytes 3145736 | tf_op jit(solution)/shard_map/ppermute | solution.py:469
  6.0 4.3 %collective-permute-start.1 = (bf16[512,512]{1,0:T(8,128)(2,1)S(1)}, bf16[512,512]{1,0:T(8,128)(2,1)}, u32[]{:S(2)}, u32[]{:S(2)}) collective-permute-start(bf16[512,512]{1,0:T(8,128)(2,1)S(1)} %get-tuple-element.48.refs_1_), channel_id=1, source_target_pairs={{0,2},{2,4},{4,6},{1,3},{3,5},{5,7},{8,10},{10,12},{12,14},{9,11},... | collective-permute-start | bytes 1572872 | tf_op jit(solution)/shard_map/ppermute | solution.py:475
  10.3 2.7 %collective-permute-start.10 = (bf16[512,512]{1,0:T(8,128)(2,1)S(1)}, bf16[512,512]{1,0:T(8,128)(2,1)S(1)}, u32[]{:S(2)}, u32[]{:S(2)}) collective-permute-start(bf16[512,512]{1,0:T(8,128)(2,1)S(1)} %get-tuple-element.47.refs_0_), channel_id=1, source_target_pairs={{0,2},{2,4},{4,6},{1,3},{3,5},{5,7},{8,10},{10,12},{12,14},{9,11},... | collective-permute-start | bytes 1572872 | tf_op jit(solution)/shard_map/ppermute | solution.py:475
  13.0 1.3 %collective-permute-start.11 = (bf16[512,512]{1,0:T(8,128)(2,1)S(1)}, bf16[512,512]{1,0:T(8,128)(2,1)S(1)}, u32[]{:S(2)}, u32[]{:S(2)}) collective-permute-start(bf16[512,512]{1,0:T(8,128)(2,1)S(1)} %get-tuple-element.47.refs_0_), channel_id=1, source_target_pairs={{2,0},{4,2},{6,4},{3,1},{5,3},{7,5},{10,8},{12,10},{14,12},{11,9},... | collective-permute-start | bytes 1572872 | tf_op jit(solution)/shard_map/ppermute | solution.py:476
  14.3 1.3 %collective-permute-start.4 = (bf16[512,512]{1,0:T(8,128)(2,1)S(1)}, bf16[512,512]{1,0:T(8,128)(2,1)}, u32[]{:S(2)}, u32[]{:S(2)}) collective-permute-start(bf16[512,512]{1,0:T(8,128)(2,1)S(1)} %get-tuple-element.48.refs_1_), channel_id=1, source_target_pairs={{2,0},{4,2},{6,4},{3,1},{5,3},{7,5},{10,8},{12,10},{14,12},{11,9},... | collective-permute-start | bytes 1572872 | tf_op jit(solution)/shard_map/ppermute | solution.py:476
  15.6 2.6 %shard_map.69 = bf16[1024,512]{1,0:T(8,128)(2,1)} custom-call(s32[2,8]{1,0:T(2,128)S(1)} %bitcast.6, bf16[1,1024,2048]{2,1,0:T(8,128)(2,1)} %g_local.9), custom_call_target="tpu_custom_call" | custom-call | tf_op jit(solution)/shard_map/pallas_call | solution.py:147
  18.2 3.5 %collective-permute-done.1.refs_4_.refs_6_.refs_8_ = bf16[512,512]{1,0:T(8,128)(2,1)} collective-permute-done((bf16[512,512]{1,0:T(8,128)(2,1)S(1)}, bf16[512,512]{1,0:T(8,128)(2,1)}, u32[]{:S(2)}, u32[]{:S(2)}) %collective-permute-start.1) | collective-permute-done | bytes 524320 | tf_op jit(solution)/shard_map/ppermute | solution.py:475
  21.8 0.5 collective-permute-start.8
  22.3 9.3 %collective-permute-done.10.refs_2_ = bf16[512,512]{1,0:T(8,128)(2,1)S(1)} collective-permute-done((bf16[512,512]{1,0:T(8,128)(2,1)S(1)}, bf16[512,512]{1,0:T(8,128)(2,1)S(1)}, u32[]{:S(2)}, u32[]{:S(2)}) %collective-permute-start.10) | collective-permute-done | bytes 524320 | tf_op jit(solution)/shard_map/ppermute | solution.py:475
  31.6 1.4 %collective-permute-start.12 = (bf16[512,512]{1,0:T(8,128)(2,1)S(1)}, bf16[512,512]{1,0:T(8,128)(2,1)}, u32[]{:S(2)}, u32[]{:S(2)}) collective-permute-start(bf16[512,512]{1,0:T(8,128)(2,1)S(1)} %collective-permute-done.10.refs_2_), channel_id=1, source_target_pairs={{2,4},{4,6},{3,5},{5,7},{10,12},{12,14},{11,13},{13,15},{18,20},{2... | collective-permute-start | bytes 1572872 | tf_op jit(solution)/shard_map/ppermute | solution.py:475
  33.0 1.3 %collective-permute-start.13 = (bf16[512,512]{1,0:T(8,128)(2,1)S(1)}, bf16[512,512]{1,0:T(8,128)(2,1)}, u32[]{:S(2)}, u32[]{:S(2)}) collective-permute-start(bf16[512,512]{1,0:T(8,128)(2,1)S(1)} %collective-permute-done.11.refs_3_), channel_id=1, source_target_pairs={{2,0},{4,2},{3,1},{5,3},{10,8},{12,10},{11,9},{13,11},{18,16},{20,... | collective-permute-start | bytes 1572872 | tf_op jit(solution)/shard_map/ppermute | solution.py:476
  34.3 4.7 %collective-permute-done.4.refs_5_.refs_7_.refs_9_ = bf16[512,512]{1,0:T(8,128)(2,1)} collective-permute-done((bf16[512,512]{1,0:T(8,128)(2,1)S(1)}, bf16[512,512]{1,0:T(8,128)(2,1)}, u32[]{:S(2)}, u32[]{:S(2)}) %collective-permute-start.4) | collective-permute-done | bytes 524320 | tf_op jit(solution)/shard_map/ppermute | solution.py:476
  39.0 1.4 %collective-permute-start.2 = (bf16[512,512]{1,0:T(8,128)(2,1)}, bf16[512,512]{1,0:T(8,128)(2,1)}, u32[]{:S(2)}, u32[]{:S(2)}) collective-permute-start(bf16[512,512]{1,0:T(8,128)(2,1)} %collective-permute-done.1.refs_4_.refs_6_.refs_8_), channel_id=1, source_target_pairs={{2,4},{4,6},{3,5},{5,7},{10,12},{12,14},{11,13},{13,15},{18,20},{2... | collective-permute-start | bytes 1572872 | tf_op jit(solution)/shard_map/ppermute | solution.py:475
  40.5 1.3 %collective-permute-start.5 = (bf16[512,512]{1,0:T(8,128)(2,1)}, bf16[512,512]{1,0:T(8,128)(2,1)}, u32[]{:S(2)}, u32[]{:S(2)}) collective-permute-start(bf16[512,512]{1,0:T(8,128)(2,1)} %collective-permute-done.4.refs_5_.refs_7_.refs_9_), channel_id=1, source_target_pairs={{2,0},{4,2},{3,1},{5,3},{10,8},{12,10},{11,9},{13,11},{18,16},{20,... | collective-permute-start | bytes 1572872 | tf_op jit(solution)/shard_map/ppermute | solution.py:476
  41.8 2.6 %shard_map.70 = bf16[1024,512]{1,0:T(8,128)(2,1)} custom-call(s32[2,8]{1,0:T(2,128)S(1)} %bitcast.7, bf16[1,1024,2048]{2,1,0:T(8,128)(2,1)} %g_local.9), custom_call_target="tpu_custom_call" | custom-call | tf_op jit(solution)/shard_map/pallas_call | solution.py:147
  44.5 0.6 collective-permute-start.9
  45.0 8.1 %collective-permute-done.13.refs_5_ = bf16[512,512]{1,0:T(8,128)(2,1)} collective-permute-done((bf16[512,512]{1,0:T(8,128)(2,1)S(1)}, bf16[512,512]{1,0:T(8,128)(2,1)}, u32[]{:S(2)}, u32[]{:S(2)}) %collective-permute-start.13) | collective-permute-done | bytes 524320 | tf_op jit(solution)/shard_map/ppermute | solution.py:476
  53.1 1.5 %collective-permute-start.14 = (bf16[512,512]{1,0:T(8,128)(2,1)}, bf16[512,512]{1,0:T(8,128)(2,1)}, u32[]{:S(2)}, u32[]{:S(2)}) collective-permute-start(bf16[512,512]{1,0:T(8,128)(2,1)} %collective-permute-done.12.refs_4_), channel_id=1, source_target_pairs={{4,6},{5,7},{12,14},{13,15},{20,22},{21,23},{28,30},{29,31}} | collective-permute-start | bytes 1572872 | tf_op jit(solution)/shard_map/ppermute | solution.py:475
  54.6 0.7 compare_reduce_fusion
  56.5 5.8 %shard_map.71.refs_12_ = f32[1024,512]{1,0:T(8,128)S(1)} custom-call(s32[2,8]{1,0:T(2,128)S(1)} %bitcast.9, bf16[1,1024,2048]{2,1,0:T(8,128)(2,1)} %g_local.9, bf16[512,512]{1,0:T(8,128)(2,1)} %copy-done.3, bf16[512,512]{1,0:T(8,128)(2,1)} %copy-done.4, bf16[512,512]{1,0:T(8,128)(2,1)} %copy-done.5, bf16[512,512]{1,0:T(8,128)(2,1)} %copy-done.6, ...), custom_call_target="tpu_custom_call" | custom-call | tf_op jit(solution)/shard_map/pallas_call | solution.py:261
  62.3 2.8 %shard_map.72.refs_14_ = f32[1024,512]{1,0:T(8,128)S(1)} custom-call(s32[2,8]{1,0:T(2,128)S(1)} %bitcast.10, bf16[1,1024,2048]{2,1,0:T(8,128)(2,1)} %g_local.9, bf16[512,512]{1,0:T(8,128)(2,1)} %copy-done.3, bf16[512,512]{1,0:T(8,128)(2,1)} %copy-done.4, bf16[512,512]{1,0:T(8,128)(2,1)} %copy-done.5, ...), custom_call_target="tpu_custom_call", output_to_operand_aliasing={{}: (14, {})} | custom-call | tf_op jit(solution)/shard_map/pallas_call | solution.py:261
  65.2 1.3 %collective-permute-start.15 = (bf16[512,512]{1,0:T(8,128)(2,1)}, bf16[512,512]{1,0:T(8,128)(2,1)}, u32[]{:S(2)}, u32[]{:S(2)}) collective-permute-start(bf16[512,512]{1,0:T(8,128)(2,1)} %collective-permute-done.13.refs_5_), channel_id=1, source_target_pairs={{2,0},{3,1},{10,8},{11,9},{18,16},{19,17},{26,24},{27,25}} | collective-permute-start | bytes 1572872 | tf_op jit(solution)/shard_map/ppermute | solution.py:476
  66.5 3.3 %inner.1 = bf16[512,512]{1,0:T(8,128)(2,1)} custom-call(s32[2,8]{1,0:T(2,128)S(1)} %bitcast.11, bf16[1,1024,2048]{2,1,0:T(8,128)(2,1)} %g_local.9, bf16[1024,512]{1,0:T(8,128)(2,1)} %copy-done.2, bf16[1,1024,512]{2,1,0:T(8,128)(2,1)S(1)} %copy-done), custom_call_target="tpu_custom_call" | custom-call | tf_op jit(solution)/shard_map/inner/pallas_call | solution.py:301
  69.8 6.2 %collective-permute-start.16 = (bf16[512,512]{1,0:T(8,128)(2,1)}, bf16[512,512]{1,0:T(8,128)(2,1)}, u32[]{:S(2)}, u32[]{:S(2)}) collective-permute-start(bf16[512,512]{1,0:T(8,128)(2,1)} %inner.1), channel_id=1, source_target_pairs={{0,2},{6,4},{1,3},{7,5},{8,10},{14,12},{9,11},{15,13},{16,18},{22,... | collective-permute-start | bytes 1572872 | tf_op jit(solution)/shard_map/ppermute | solution.py:484
  76.0 1.1 conditional.1
  76.0 1.1 broadcast.7
  77.0 0.7 collective-permute-start.3
  77.7 1.3 %collective-permute-start.6 = (bf16[512,512]{1,0:T(8,128)(2,1)}, bf16[512,512]{1,0:T(8,128)(2,1)S(1)}, u32[]{:S(2)}, u32[]{:S(2)}) collective-permute-start(bf16[512,512]{1,0:T(8,128)(2,1)} %collective-permute-done.5.refs_9_.refs_11_), channel_id=1, source_target_pairs={{2,0},{3,1},{10,8},{11,9},{18,16},{19,17},{26,24},{27,25}} | collective-permute-start | bytes 1572872 | tf_op jit(solution)/shard_map/ppermute | solution.py:476
  79.7 1.0 shard_map.73.refs_16_
  80.7 3.6 %collective-permute-done.16.refs_19_ = bf16[512,512]{1,0:T(8,128)(2,1)} collective-permute-done((bf16[512,512]{1,0:T(8,128)(2,1)}, bf16[512,512]{1,0:T(8,128)(2,1)}, u32[]{:S(2)}, u32[]{:S(2)}) %collective-permute-start.16) | collective-permute-done | bytes 524320 | tf_op jit(solution)/shard_map/ppermute | solution.py:484
  84.3 2.7 %late_diag.1 = (f32[256,512]{1,0:T(8,128)S(1)}, bf16[256,512]{1,0:T(8,128)(2,1)S(1)}, f32[1024,512]{1,0:T(8,128)S(1)}) custom-call(s32[2,8]{1,0:T(2,128)S(1)} %bitcast.14, f32[1]{0:T(128)S(6)} %copy.13.weight, bf16[1,1024,2048]{2,1,0:T(8,128)(2,1)} %g_local.9, bf16[512,512]{1,0:T(8,128)(2,1)} %copy-done.3, bf16[512,512]{1,0:T(8,128)(2,1)} %copy-done.4, ...), custom_call_target="tpu_custom_call" | custom-call | tf_op jit(solution)/shard_map/late_diag/pallas_call | solution.py:367
  87.0 3.8 %collective-permute-done.6.refs_1_ = bf16[512,512]{1,0:T(8,128)(2,1)S(1)} collective-permute-done((bf16[512,512]{1,0:T(8,128)(2,1)}, bf16[512,512]{1,0:T(8,128)(2,1)S(1)}, u32[]{:S(2)}, u32[]{:S(2)}) %collective-permute-start.6) | collective-permute-done | bytes 524320 | tf_op jit(solution)/shard_map/ppermute | solution.py:476
  90.8 0.8 copy-done.8
  91.6 2.9 %late_off.1 = (f32[512,512]{1,0:T(8,128)S(1)}, bf16[512,512]{1,0:T(8,128)(2,1)S(1)}) custom-call(s32[2,8]{1,0:T(2,128)S(1)} %bitcast.15, f32[1]{0:T(128)S(6)} %copy.13.weight, bf16[1,1024,2048]{2,1,0:T(8,128)(2,1)} %g_local.9, bf16[512,512]{1,0:T(8,128)(2,1)} %copy-done.7, bf16[512,512]{1,0:T(8,128)(2,1)} %copy-done.8, bf16[1024,512]{1,0:T(8,128)(2,1)} %copy-done.2, ...), custom_call_target="tpu_custom_call" | custom-call | tf_op jit(solution)/shard_map/late_off/pallas_call | solution.py:405
  94.5 0.1 collective-permute-start.17
  94.6 0.5 collective-permute-start.19
  95.1 1.8 %collective-permute-done.19.refs_0_ = bf16[256,512]{1,0:T(8,128)(2,1)S(1)} collective-permute-done((bf16[256,512]{1,0:T(8,128)(2,1)S(1)}, bf16[256,512]{1,0:T(8,128)(2,1)S(1)}, u32[]{:S(2)}, u32[]{:S(2)}) %collective-permute-start.19) | collective-permute-done | bytes 262176 | tf_op jit(solution)/shard_map/ppermute | solution.py:517
  96.9 1.6 %collective-permute-start.20 = (bf16[128,512]{1,0:T(8,128)(2,1)S(1)}, bf16[128,512]{1,0:T(8,128)(2,1)S(1)}, u32[]{:S(2)}, u32[]{:S(2)}) collective-permute-start(bf16[128,512]{1,0:T(8,128)(2,1)S(1)} %get-tuple-element.40), channel_id=1, source_target_pairs={{0,16},{8,24},{16,0},{24,8},{1,17},{9,25},{17,1},{25,9},{2,18},{10... | collective-permute-start | bytes 393224 | tf_op jit(solution)/shard_map/ppermute | solution.py:517
  98.5 4.1 %collective-permute-done.20.refs_0_ = bf16[128,512]{1,0:T(8,128)(2,1)S(1)} collective-permute-done((bf16[128,512]{1,0:T(8,128)(2,1)S(1)}, bf16[128,512]{1,0:T(8,128)(2,1)S(1)}, u32[]{:S(2)}, u32[]{:S(2)}) %collective-permute-start.20) | collective-permute-done | bytes 131104 | tf_op jit(solution)/shard_map/ppermute | solution.py:517
  102.6 1.0 collective-permute-start.22
  103.7 3.4 %collective-permute-start.23 = (bf16[32,512]{1,0:T(8,128)(2,1)S(1)}, bf16[32,512]{1,0:T(8,128)(2,1)S(1)}, u32[]{:S(2)}, u32[]{:S(2)}) collective-permute-start(bf16[32,512]{1,0:T(8,128)(2,1)S(1)} %get-tuple-element.44), channel_id=1, source_target_pairs={{0,6},{2,4},{4,2},{6,0},{1,7},{3,5},{5,3},{7,1},{8,14},{10,12},{12... | collective-permute-start | bytes 98312 | tf_op jit(solution)/shard_map/ppermute | solution.py:517
  107.0 0.1 shard_map.74
  107.1 1.6 %collective-permute-start.18 = (bf16[256,512]{1,0:T(8,128)(2,1)S(1)}, bf16[256,512]{1,0:T(8,128)(2,1)S(1)}, u32[]{:S(2)}, u32[]{:S(2)}) collective-permute-start(bf16[256,512]{1,0:T(8,128)(2,1)S(1)} %get-tuple-element.36), channel_id=1, source_target_pairs={{0,16},{8,24},{16,0},{24,8},{1,17},{9,25},{17,1},{25,9},{2,18},{10... | collective-permute-start | bytes 786440 | tf_op jit(solution)/shard_map/ppermute | solution.py:517
  108.7 0.7 collective-permute-done.23
  109.4 0.6 convert_add_fusion.1
  110.0 3.8 %collective-permute-done.18 = bf16[256,512]{1,0:T(8,128)(2,1)S(1)} collective-permute-done((bf16[256,512]{1,0:T(8,128)(2,1)S(1)}, bf16[256,512]{1,0:T(8,128)(2,1)S(1)}, u32[]{:S(2)}, u32[]{:S(2)}) %collective-permute-start.18) | collective-permute-done | bytes 262176 | tf_op jit(solution)/shard_map/ppermute | solution.py:517
  113.8 0.9 convert_add_fusion
  (36 shorter events, 0.3 us)
Async XLA Ops:
  0.6 5.3 %copy-start = (bf16[1,1024,512]{2,1,0:T(8,128)(2,1)S(1)}, bf16[1,1024,512]{2,1,0:T(8,128)(2,1)}, u32[]{:S(2)}) copy-start(bf16[1,1024,512]{2,1,0:T(8,128)(2,1)} %refs_17_.1) | copy-start | bytes 3145732
  2.8 12.8 %copy-start.9 = (s32[8,2]{0,1:T(2,128)S(1)}, s32[8,2]{0,1:T(2,128)}, u32[]{:S(2)}) copy-start(s32[8,2]{0,1:T(2,128)} %param.11) | copy-start | bytes 196
  2.8 37.7 %collective-permute-start.7 = (bf16[1024,512]{1,0:T(8,128)(2,1)S(1)}, bf16[1024,512]{1,0:T(8,128)(2,1)S(1)}, u32[]{:S(2)}, u32[]{:S(2)}) collective-permute-start(bf16[1024,512]{1,0:T(8,128)(2,1)S(1)} %shard_map.68), channel_id=1, source_target_pairs={{0,1},{1,0},{2,3},{3,2},{4,5},{5,4},{6,7},{7,6},{8,9},{9,8},{10,11... | collective-permute-start | bytes 3145736 | tf_op jit(solution)/shard_map/ppermute | solution.py:469
  6.0 12.3 %copy-start.3 = (bf16[512,512]{1,0:T(8,128)(2,1)}, bf16[512,512]{1,0:T(8,128)(2,1)S(1)}, u32[]{:S(2)}) copy-start(bf16[512,512]{1,0:T(8,128)(2,1)S(1)} %get-tuple-element.47.refs_0_) | copy-start | bytes 1572868
  6.0 12.3 %copy-start.4 = (bf16[512,512]{1,0:T(8,128)(2,1)}, bf16[512,512]{1,0:T(8,128)(2,1)S(1)}, u32[]{:S(2)}) copy-start(bf16[512,512]{1,0:T(8,128)(2,1)S(1)} %get-tuple-element.48.refs_1_) | copy-start | bytes 1572868
  6.0 15.8 %collective-permute-start.1 = (bf16[512,512]{1,0:T(8,128)(2,1)S(1)}, bf16[512,512]{1,0:T(8,128)(2,1)}, u32[]{:S(2)}, u32[]{:S(2)}) collective-permute-start(bf16[512,512]{1,0:T(8,128)(2,1)S(1)} %get-tuple-element.48.refs_1_), channel_id=1, source_target_pairs={{0,2},{2,4},{4,6},{1,3},{3,5},{5,7},{8,10},{10,12},{12,14},{9,11},... | collective-permute-start | bytes 1572872 | tf_op jit(solution)/shard_map/ppermute | solution.py:475
  10.3 21.3 %collective-permute-start.10 = (bf16[512,512]{1,0:T(8,128)(2,1)S(1)}, bf16[512,512]{1,0:T(8,128)(2,1)S(1)}, u32[]{:S(2)}, u32[]{:S(2)}) collective-permute-start(bf16[512,512]{1,0:T(8,128)(2,1)S(1)} %get-tuple-element.47.refs_0_), channel_id=1, source_target_pairs={{0,2},{2,4},{4,6},{1,3},{3,5},{5,7},{8,10},{10,12},{12,14},{9,11},... | collective-permute-start | bytes 1572872 | tf_op jit(solution)/shard_map/ppermute | solution.py:475
  13.0 20.0 %collective-permute-start.11 = (bf16[512,512]{1,0:T(8,128)(2,1)S(1)}, bf16[512,512]{1,0:T(8,128)(2,1)S(1)}, u32[]{:S(2)}, u32[]{:S(2)}) collective-permute-start(bf16[512,512]{1,0:T(8,128)(2,1)S(1)} %get-tuple-element.47.refs_0_), channel_id=1, source_target_pairs={{2,0},{4,2},{6,4},{3,1},{5,3},{7,5},{10,8},{12,10},{14,12},{11,9},... | collective-permute-start | bytes 1572872 | tf_op jit(solution)/shard_map/ppermute | solution.py:476
  14.3 24.8 %collective-permute-start.4 = (bf16[512,512]{1,0:T(8,128)(2,1)S(1)}, bf16[512,512]{1,0:T(8,128)(2,1)}, u32[]{:S(2)}, u32[]{:S(2)}) collective-permute-start(bf16[512,512]{1,0:T(8,128)(2,1)S(1)} %get-tuple-element.48.refs_1_), channel_id=1, source_target_pairs={{2,0},{4,2},{6,4},{3,1},{5,3},{7,5},{10,8},{12,10},{14,12},{11,9},... | collective-permute-start | bytes 1572872 | tf_op jit(solution)/shard_map/ppermute | solution.py:476
  21.8 40.6 %collective-permute-start.8 = (bf16[1024,512]{1,0:T(8,128)(2,1)}, bf16[1024,512]{1,0:T(8,128)(2,1)}, u32[]{:S(2)}, u32[]{:S(2)}) collective-permute-start(bf16[1024,512]{1,0:T(8,128)(2,1)} %shard_map.69), channel_id=1, source_target_pairs={{0,1},{1,0},{2,3},{3,2},{4,5},{5,4},{6,7},{7,6},{8,9},{9,8},{10,11... | collective-permute-start | bytes 3145736 | tf_op jit(solution)/shard_map/ppermute | solution.py:469
  31.6 12.9 %copy-start.5 = (bf16[512,512]{1,0:T(8,128)(2,1)}, bf16[512,512]{1,0:T(8,128)(2,1)S(1)}, u32[]{:S(2)}) copy-start(bf16[512,512]{1,0:T(8,128)(2,1)S(1)} %collective-permute-done.10.refs_2_) | copy-start | bytes 1572868
  31.6 12.9 %collective-permute-start.12 = (bf16[512,512]{1,0:T(8,128)(2,1)S(1)}, bf16[512,512]{1,0:T(8,128)(2,1)}, u32[]{:S(2)}, u32[]{:S(2)}) collective-permute-start(bf16[512,512]{1,0:T(8,128)(2,1)S(1)} %collective-permute-done.10.refs_2_), channel_id=1, source_target_pairs={{2,4},{4,6},{3,5},{5,7},{10,12},{12,14},{11,13},{13,15},{18,20},{2... | collective-permute-start | bytes 1572872 | tf_op jit(solution)/shard_map/ppermute | solution.py:475
  33.0 11.4 %copy-start.6 = (bf16[512,512]{1,0:T(8,128)(2,1)}, bf16[512,512]{1,0:T(8,128)(2,1)S(1)}, u32[]{:S(2)}) copy-start(bf16[512,512]{1,0:T(8,128)(2,1)S(1)} %collective-permute-done.11.refs_3_) | copy-start | bytes 1572868
  33.0 20.1 %collective-permute-start.13 = (bf16[512,512]{1,0:T(8,128)(2,1)S(1)}, bf16[512,512]{1,0:T(8,128)(2,1)}, u32[]{:S(2)}, u32[]{:S(2)}) collective-permute-start(bf16[512,512]{1,0:T(8,128)(2,1)S(1)} %collective-permute-done.11.refs_3_), channel_id=1, source_target_pairs={{2,0},{4,2},{3,1},{5,3},{10,8},{12,10},{11,9},{13,11},{18,16},{20,... | collective-permute-start | bytes 1572872 | tf_op jit(solution)/shard_map/ppermute | solution.py:476
  39.0 23.3 %collective-permute-start.2 = (bf16[512,512]{1,0:T(8,128)(2,1)}, bf16[512,512]{1,0:T(8,128)(2,1)}, u32[]{:S(2)}, u32[]{:S(2)}) collective-permute-start(bf16[512,512]{1,0:T(8,128)(2,1)} %collective-permute-done.1.refs_4_.refs_6_.refs_8_), channel_id=1, source_target_pairs={{2,4},{4,6},{3,5},{5,7},{10,12},{12,14},{11,13},{13,15},{18,20},{2... | collective-permute-start | bytes 1572872 | tf_op jit(solution)/shard_map/ppermute | solution.py:475
  40.5 4.0 %copy-start.2 = (bf16[1024,512]{1,0:T(8,128)(2,1)}, bf16[1024,512]{1,0:T(8,128)(2,1)S(1)}, u32[]{:S(2)}) copy-start(bf16[1024,512]{1,0:T(8,128)(2,1)S(1)} %collective-permute-done.7.refs_6_.refs_10_.refs_12_.slot.refs_2_) | copy-start | bytes 3145732
  40.5 21.8 %collective-permute-start.5 = (bf16[512,512]{1,0:T(8,128)(2,1)}, bf16[512,512]{1,0:T(8,128)(2,1)}, u32[]{:S(2)}, u32[]{:S(2)}) collective-permute-start(bf16[512,512]{1,0:T(8,128)(2,1)} %collective-permute-done.4.refs_5_.refs_7_.refs_9_), channel_id=1, source_target_pairs={{2,0},{4,2},{3,1},{5,3},{10,8},{12,10},{11,9},{13,11},{18,16},{20,... | collective-permute-start | bytes 1572872 | tf_op jit(solution)/shard_map/ppermute | solution.py:476
  44.5 36.2 %collective-permute-start.9 = (bf16[1024,512]{1,0:T(8,128)(2,1)}, bf16[1024,512]{1,0:T(8,128)(2,1)}, u32[]{:S(2)}, u32[]{:S(2)}) collective-permute-start(bf16[1024,512]{1,0:T(8,128)(2,1)} %shard_map.70), channel_id=1, source_target_pairs={{0,1},{1,0},{2,3},{3,2},{4,5},{5,4},{6,7},{7,6},{8,9},{9,8},{10,11... | collective-permute-start | bytes 3145736 | tf_op jit(solution)/shard_map/ppermute | solution.py:469
  53.1 24.6 %collective-permute-start.14 = (bf16[512,512]{1,0:T(8,128)(2,1)}, bf16[512,512]{1,0:T(8,128)(2,1)}, u32[]{:S(2)}, u32[]{:S(2)}) collective-permute-start(bf16[512,512]{1,0:T(8,128)(2,1)} %collective-permute-done.12.refs_4_), channel_id=1, source_target_pairs={{4,6},{5,7},{12,14},{13,15},{20,22},{21,23},{28,30},{29,31}} | collective-permute-start | bytes 1572872 | tf_op jit(solution)/shard_map/ppermute | solution.py:475
  65.2 14.6 %collective-permute-start.15 = (bf16[512,512]{1,0:T(8,128)(2,1)}, bf16[512,512]{1,0:T(8,128)(2,1)}, u32[]{:S(2)}, u32[]{:S(2)}) collective-permute-start(bf16[512,512]{1,0:T(8,128)(2,1)} %collective-permute-done.13.refs_5_), channel_id=1, source_target_pairs={{2,0},{3,1},{10,8},{11,9},{18,16},{19,17},{26,24},{27,25}} | collective-permute-start | bytes 1572872 | tf_op jit(solution)/shard_map/ppermute | solution.py:476
  69.8 14.5 %collective-permute-start.16 = (bf16[512,512]{1,0:T(8,128)(2,1)}, bf16[512,512]{1,0:T(8,128)(2,1)}, u32[]{:S(2)}, u32[]{:S(2)}) collective-permute-start(bf16[512,512]{1,0:T(8,128)(2,1)} %inner.1), channel_id=1, source_target_pairs={{0,2},{6,4},{1,3},{7,5},{8,10},{14,12},{9,11},{15,13},{16,18},{22,... | collective-permute-start | bytes 1572872 | tf_op jit(solution)/shard_map/ppermute | solution.py:484
  77.0 9.9 %collective-permute-start.3 = (bf16[512,512]{1,0:T(8,128)(2,1)}, bf16[512,512]{1,0:T(8,128)(2,1)S(1)}, u32[]{:S(2)}, u32[]{:S(2)}) collective-permute-start(bf16[512,512]{1,0:T(8,128)(2,1)} %collective-permute-done.2.refs_8_.refs_10_), channel_id=1, source_target_pairs={{4,6},{5,7},{12,14},{13,15},{20,22},{21,23},{28,30},{29,31}} | collective-permute-start | bytes 1572872 | tf_op jit(solution)/shard_map/ppermute | solution.py:475
  77.7 13.1 %collective-permute-start.6 = (bf16[512,512]{1,0:T(8,128)(2,1)}, bf16[512,512]{1,0:T(8,128)(2,1)S(1)}, u32[]{:S(2)}, u32[]{:S(2)}) collective-permute-start(bf16[512,512]{1,0:T(8,128)(2,1)} %collective-permute-done.5.refs_9_.refs_11_), channel_id=1, source_target_pairs={{2,0},{3,1},{10,8},{11,9},{18,16},{19,17},{26,24},{27,25}} | collective-permute-start | bytes 1572872 | tf_op jit(solution)/shard_map/ppermute | solution.py:476
  79.7 4.6 %copy-start.1 = (bf16[1,128,512]{2,1,0:T(8,128)(2,1)S(1)}, bf16[1,128,512]{2,1,0:T(8,128)(2,1)}, u32[]{:S(2)}) copy-start(bf16[1,128,512]{2,1,0:T(8,128)(2,1)} %refs_18_.1) | copy-start | bytes 393220
  87.0 3.8 %copy-start.7 = (bf16[512,512]{1,0:T(8,128)(2,1)}, bf16[512,512]{1,0:T(8,128)(2,1)S(1)}, u32[]{:S(2)}) copy-start(bf16[512,512]{1,0:T(8,128)(2,1)S(1)} %collective-permute-done.3.refs_0_) | copy-start | bytes 1572868
  90.8 0.8 copy-start.8
  94.5 12.5 %collective-permute-start.17 = (bf16[512,512]{1,0:T(8,128)(2,1)S(1)}, bf16[512,512]{1,0:T(8,128)(2,1)S(1)}, u32[]{:S(2)}, u32[]{:S(2)}) collective-permute-start(bf16[512,512]{1,0:T(8,128)(2,1)S(1)} %get-tuple-element.34), channel_id=1, source_target_pairs={{0,8},{8,0},{16,24},{24,16},{1,9},{9,1},{17,25},{25,17},{2,10},{10... | collective-permute-start | bytes 1572872 | tf_op jit(solution)/shard_map/ppermute | solution.py:517
  94.6 2.3 %collective-permute-start.19 = (bf16[256,512]{1,0:T(8,128)(2,1)S(1)}, bf16[256,512]{1,0:T(8,128)(2,1)S(1)}, u32[]{:S(2)}, u32[]{:S(2)}) collective-permute-start(bf16[256,512]{1,0:T(8,128)(2,1)S(1)} %get-tuple-element.38), channel_id=1, source_target_pairs={{0,8},{8,0},{16,24},{24,16},{1,9},{9,1},{17,25},{25,17},{2,10},{10... | collective-permute-start | bytes 786440 | tf_op jit(solution)/shard_map/ppermute | solution.py:517
  96.9 5.6 %collective-permute-start.20 = (bf16[128,512]{1,0:T(8,128)(2,1)S(1)}, bf16[128,512]{1,0:T(8,128)(2,1)S(1)}, u32[]{:S(2)}, u32[]{:S(2)}) collective-permute-start(bf16[128,512]{1,0:T(8,128)(2,1)S(1)} %get-tuple-element.40), channel_id=1, source_target_pairs={{0,16},{8,24},{16,0},{24,8},{1,17},{9,25},{17,1},{25,9},{2,18},{10... | collective-permute-start | bytes 393224 | tf_op jit(solution)/shard_map/ppermute | solution.py:517
  102.6 6.1 %collective-permute-start.21 = (bf16[32,512]{1,0:T(8,128)(2,1)S(1)}, bf16[32,512]{1,0:T(8,128)(2,1)S(1)}, u32[]{:S(2)}, u32[]{:S(2)}) collective-permute-start(bf16[32,512]{1,0:T(8,128)(2,1)S(1)} %get-tuple-element.42), channel_id=1, source_target_pairs={{0,2},{2,0},{4,6},{6,4},{1,3},{3,1},{5,7},{7,5},{8,10},{10,8},{12,... | collective-permute-start | bytes 98312 | tf_op jit(solution)/shard_map/ppermute | solution.py:517
  102.6 6.0 %collective-permute-start.22 = (bf16[32,512]{1,0:T(8,128)(2,1)S(1)}, bf16[32,512]{1,0:T(8,128)(2,1)S(1)}, u32[]{:S(2)}, u32[]{:S(2)}) collective-permute-start(bf16[32,512]{1,0:T(8,128)(2,1)S(1)} %get-tuple-element.43), channel_id=1, source_target_pairs={{0,4},{2,6},{4,0},{6,2},{1,5},{3,7},{5,1},{7,3},{8,12},{10,14},{12... | collective-permute-start | bytes 98312 | tf_op jit(solution)/shard_map/ppermute | solution.py:517
  103.7 5.7 %collective-permute-start.23 = (bf16[32,512]{1,0:T(8,128)(2,1)S(1)}, bf16[32,512]{1,0:T(8,128)(2,1)S(1)}, u32[]{:S(2)}, u32[]{:S(2)}) collective-permute-start(bf16[32,512]{1,0:T(8,128)(2,1)S(1)} %get-tuple-element.44), channel_id=1, source_target_pairs={{0,6},{2,4},{4,2},{6,0},{1,7},{3,5},{5,3},{7,1},{8,14},{10,12},{12... | collective-permute-start | bytes 98312 | tf_op jit(solution)/shard_map/ppermute | solution.py:517
  107.1 6.7 %collective-permute-start.18 = (bf16[256,512]{1,0:T(8,128)(2,1)S(1)}, bf16[256,512]{1,0:T(8,128)(2,1)S(1)}, u32[]{:S(2)}, u32[]{:S(2)}) collective-permute-start(bf16[256,512]{1,0:T(8,128)(2,1)S(1)} %get-tuple-element.36), channel_id=1, source_target_pairs={{0,16},{8,24},{16,0},{24,8},{1,17},{9,25},{17,1},{25,9},{2,18},{10... | collective-permute-start | bytes 786440 | tf_op jit(solution)/shard_map/ppermute | solution.py:517

commit v6 on v5

--- a/solution.py
+++ b/solution.py
@@ -527,11 +527,28 @@
     off_in = swapped("pole", sends, shifts(sz.poles, sz.outer, sz.cores))
     diag, *sends = fold(sz.rows, "row", 1, diag, diag_in)
     diag_in = swapped("row", sends, shifts(sz.rows, sz.rows, 1))
-    for v in off_in:
-        off = off + v.astype(F32)
-    for v in diag_in:
-        diag = diag + v.astype(F32)
-    return off, diag
+    return last_sums(off, off_in, diag, diag_in)
+
+
+def last_kernel(n_off, n_diag, *refs):
+    off, *off_in = refs[:n_off]
+    diag, *diag_in = refs[n_off:n_off + n_diag]
+    for own, ins, out in ((off, off_in, refs[-2]), (diag, diag_in, refs[-1])):
+        v = own[...]
+        for r in ins:
+            v = v + r[...].astype(F32)
+        out[...] = v
+
+
+def last_sums(off, off_in, diag, diag_in):
+    return pl.pallas_call(
+        functools.partial(last_kernel, 1 + len(off_in), 1 + len(diag_in)),
+        out_shape=[jax.ShapeDtypeStruct(v.shape, F32) for v in (off, diag)],
+        in_specs=[VMEM] * (2 + len(off_in) + len(diag_in)),
+        out_specs=[VMEM] * 2,
+        compiler_params=SMALL,
+        name="last_sums",
+    )(off, *off_in, diag, *diag_in)
 
 
 def make_body(mesh):

time: 115 us -> 116 us (level)
  waiting for transfers between devices: 43.4 us -> 45.8 us
  other arithmetic: 2.22 us -> 0.71 us
    ppermute x7, waiting for transfers between devices: 10.3 us -> 12.8 us  [swapped(): ins.append(lax.ppermute(v, axis, perm))]
    add x2 -> x0, other arithmetic: 1.52 us -> none  [the longest x1 0.87 us: blocked(): off = off + v.astype(F32)]
where the time goes in v6:
time: 116 us
  waiting for transfers between devices  45.8 us (39%)
  starting transfers between devices  37.3 us (32%)
  Pallas kernels  26.9 us (23%)
  between operations  2.83 us (2%)
  local copies, waits for them, and re-layouts  1.97 us (2%)
    ppermute x6, waiting for transfers between devices, blocked(): lax.ppermute(b, 'row', [(i + 1, i) for i in range(sz.rows - step)])  16.6 us
    ppermute x6, waiting for transfers between devices, blocked(): lax.ppermute(a, 'row', [(i, i + 1) for i in range(step - 1, sz.rows - 1)])  12.9 us
    ppermute x7, waiting for transfers between devices, swapped(): ins.append(lax.ppermute(v, axis, perm))  12.8 us
    ppermute x6, starting transfers between devices, blocked(): lax.ppermute(a, 'row', [(i, i + 1) for i in range(step - 1, sz.rows - 1)])  12 us
    pallas_call x3, Pallas kernels, early_call(): pl.pallas_call(functools.partial(early_kernel, sz, ready, before, keys, l...  9.57 us
    ppermute x6, starting transfers between devices, blocked(): lax.ppermute(b, 'row', [(i + 1, i) for i in range(sz.rows - step)])  7.73 us
    pallas_call x3, Pallas kernels, pick(): pl.pallas_call(functools.partial(pick_kernel, sz, slot, parts), out_shape...  7.41 us
    ppermute x7, starting transfers between devices, swapped(): ins.append(lax.ppermute(v, axis, perm))  7.17 us
  transfers between devices with their start and end apart: 23, of which 10 were waited for; matrix products, arithmetic and copies ran while one was open for 2% of the time, Pallas kernels for 18%

profile of v6, /device:TPU:0, one launch (start us, length us, event | category | flops | bytes accessed | tf_op | source)
XLA Modules:
  0.0 115.5 jit_solution(1215380314481061344)
XLA Ops:
  0.6 2.2 %shard_map.68 = bf16[1024,512]{1,0:T(8,128)(2,1)S(1)} custom-call(s32[2,8]{1,0:T(2,128)} %bitcast.5, bf16[1,1024,2048]{2,1,0:T(8,128)(2,1)} %g_local.9), custom_call_target="tpu_custom_call" | custom-call | tf_op jit(solution)/shard_map/pallas_call | solution.py:147
  2.8 3.1 %collective-permute-start.7 = (bf16[1024,512]{1,0:T(8,128)(2,1)S(1)}, bf16[1024,512]{1,0:T(8,128)(2,1)S(1)}, u32[]{:S(2)}, u32[]{:S(2)}) collective-permute-start(bf16[1024,512]{1,0:T(8,128)(2,1)S(1)} %shard_map.68), channel_id=1, source_target_pairs={{0,1},{1,0},{2,3},{3,2},{4,5},{5,4},{6,7},{7,6},{8,9},{9,8},{10,11... | collective-permute-start | bytes 3145736 | tf_op jit(solution)/shard_map/ppermute | solution.py:469
  6.0 4.3 %collective-permute-start.1 = (bf16[512,512]{1,0:T(8,128)(2,1)S(1)}, bf16[512,512]{1,0:T(8,128)(2,1)}, u32[]{:S(2)}, u32[]{:S(2)}) collective-permute-start(bf16[512,512]{1,0:T(8,128)(2,1)S(1)} %get-tuple-element.48.refs_1_), channel_id=1, source_target_pairs={{0,2},{2,4},{4,6},{1,3},{3,5},{5,7},{8,10},{10,12},{12,14},{9,11},... | collective-permute-start | bytes 1572872 | tf_op jit(solution)/shard_map/ppermute | solution.py:475
  10.3 2.7 %collective-permute-start.10 = (bf16[512,512]{1,0:T(8,128)(2,1)S(1)}, bf16[512,512]{1,0:T(8,128)(2,1)S(1)}, u32[]{:S(2)}, u32[]{:S(2)}) collective-permute-start(bf16[512,512]{1,0:T(8,128)(2,1)S(1)} %get-tuple-element.47.refs_0_), channel_id=1, source_target_pairs={{0,2},{2,4},{4,6},{1,3},{3,5},{5,7},{8,10},{10,12},{12,14},{9,11},... | collective-permute-start | bytes 1572872 | tf_op jit(solution)/shard_map/ppermute | solution.py:475
  13.0 1.3 %collective-permute-start.11 = (bf16[512,512]{1,0:T(8,128)(2,1)S(1)}, bf16[512,512]{1,0:T(8,128)(2,1)S(1)}, u32[]{:S(2)}, u32[]{:S(2)}) collective-permute-start(bf16[512,512]{1,0:T(8,128)(2,1)S(1)} %get-tuple-element.47.refs_0_), channel_id=1, source_target_pairs={{2,0},{4,2},{6,4},{3,1},{5,3},{7,5},{10,8},{12,10},{14,12},{11,9},... | collective-permute-start | bytes 1572872 | tf_op jit(solution)/shard_map/ppermute | solution.py:476
  14.3 1.3 %collective-permute-start.4 = (bf16[512,512]{1,0:T(8,128)(2,1)S(1)}, bf16[512,512]{1,0:T(8,128)(2,1)}, u32[]{:S(2)}, u32[]{:S(2)}) collective-permute-start(bf16[512,512]{1,0:T(8,128)(2,1)S(1)} %get-tuple-element.48.refs_1_), channel_id=1, source_target_pairs={{2,0},{4,2},{6,4},{3,1},{5,3},{7,5},{10,8},{12,10},{14,12},{11,9},... | collective-permute-start | bytes 1572872 | tf_op jit(solution)/shard_map/ppermute | solution.py:476
  15.6 2.6 %shard_map.69 = bf16[1024,512]{1,0:T(8,128)(2,1)} custom-call(s32[2,8]{1,0:T(2,128)S(1)} %bitcast.6, bf16[1,1024,2048]{2,1,0:T(8,128)(2,1)} %g_local.9), custom_call_target="tpu_custom_call" | custom-call | tf_op jit(solution)/shard_map/pallas_call | solution.py:147
  18.2 3.5 %collective-permute-done.1.refs_4_.refs_6_.refs_8_ = bf16[512,512]{1,0:T(8,128)(2,1)} collective-permute-done((bf16[512,512]{1,0:T(8,128)(2,1)S(1)}, bf16[512,512]{1,0:T(8,128)(2,1)}, u32[]{:S(2)}, u32[]{:S(2)}) %collective-permute-start.1) | collective-permute-done | bytes 524320 | tf_op jit(solution)/shard_map/ppermute | solution.py:475
  21.8 0.5 collective-permute-start.8
  22.3 9.3 %collective-permute-done.10.refs_2_ = bf16[512,512]{1,0:T(8,128)(2,1)S(1)} collective-permute-done((bf16[512,512]{1,0:T(8,128)(2,1)S(1)}, bf16[512,512]{1,0:T(8,128)(2,1)S(1)}, u32[]{:S(2)}, u32[]{:S(2)}) %collective-permute-start.10) | collective-permute-done | bytes 524320 | tf_op jit(solution)/shard_map/ppermute | solution.py:475
  31.6 1.4 %collective-permute-start.12 = (bf16[512,512]{1,0:T(8,128)(2,1)S(1)}, bf16[512,512]{1,0:T(8,128)(2,1)}, u32[]{:S(2)}, u32[]{:S(2)}) collective-permute-start(bf16[512,512]{1,0:T(8,128)(2,1)S(1)} %collective-permute-done.10.refs_2_), channel_id=1, source_target_pairs={{2,4},{4,6},{3,5},{5,7},{10,12},{12,14},{11,13},{13,15},{18,20},{2... | collective-permute-start | bytes 1572872 | tf_op jit(solution)/shard_map/ppermute | solution.py:475
  33.0 1.3 %collective-permute-start.13 = (bf16[512,512]{1,0:T(8,128)(2,1)S(1)}, bf16[512,512]{1,0:T(8,128)(2,1)}, u32[]{:S(2)}, u32[]{:S(2)}) collective-permute-start(bf16[512,512]{1,0:T(8,128)(2,1)S(1)} %collective-permute-done.11.refs_3_), channel_id=1, source_target_pairs={{2,0},{4,2},{3,1},{5,3},{10,8},{12,10},{11,9},{13,11},{18,16},{20,... | collective-permute-start | bytes 1572872 | tf_op jit(solution)/shard_map/ppermute | solution.py:476
  34.3 4.7 %collective-permute-done.4.refs_5_.refs_7_.refs_9_ = bf16[512,512]{1,0:T(8,128)(2,1)} collective-permute-done((bf16[512,512]{1,0:T(8,128)(2,1)S(1)}, bf16[512,512]{1,0:T(8,128)(2,1)}, u32[]{:S(2)}, u32[]{:S(2)}) %collective-permute-start.4) | collective-permute-done | bytes 524320 | tf_op jit(solution)/shard_map/ppermute | solution.py:476
  39.0 1.4 %collective-permute-start.2 = (bf16[512,512]{1,0:T(8,128)(2,1)}, bf16[512,512]{1,0:T(8,128)(2,1)}, u32[]{:S(2)}, u32[]{:S(2)}) collective-permute-start(bf16[512,512]{1,0:T(8,128)(2,1)} %collective-permute-done.1.refs_4_.refs_6_.refs_8_), channel_id=1, source_target_pairs={{2,4},{4,6},{3,5},{5,7},{10,12},{12,14},{11,13},{13,15},{18,20},{2... | collective-permute-start | bytes 1572872 | tf_op jit(solution)/shard_map/ppermute | solution.py:475
  40.5 1.3 %collective-permute-start.5 = (bf16[512,512]{1,0:T(8,128)(2,1)}, bf16[512,512]{1,0:T(8,128)(2,1)}, u32[]{:S(2)}, u32[]{:S(2)}) collective-permute-start(bf16[512,512]{1,0:T(8,128)(2,1)} %collective-permute-done.4.refs_5_.refs_7_.refs_9_), channel_id=1, source_target_pairs={{2,0},{4,2},{3,1},{5,3},{10,8},{12,10},{11,9},{13,11},{18,16},{20,... | collective-permute-start | bytes 1572872 | tf_op jit(solution)/shard_map/ppermute | solution.py:476
  41.8 2.6 %shard_map.70 = bf16[1024,512]{1,0:T(8,128)(2,1)} custom-call(s32[2,8]{1,0:T(2,128)S(1)} %bitcast.7, bf16[1,1024,2048]{2,1,0:T(8,128)(2,1)} %g_local.9), custom_call_target="tpu_custom_call" | custom-call | tf_op jit(solution)/shard_map/pallas_call | solution.py:147
  44.5 0.6 collective-permute-start.9
  45.0 8.1 %collective-permute-done.13.refs_5_ = bf16[512,512]{1,0:T(8,128)(2,1)} collective-permute-done((bf16[512,512]{1,0:T(8,128)(2,1)S(1)}, bf16[512,512]{1,0:T(8,128)(2,1)}, u32[]{:S(2)}, u32[]{:S(2)}) %collective-permute-start.13) | collective-permute-done | bytes 524320 | tf_op jit(solution)/shard_map/ppermute | solution.py:476
  53.1 1.5 %collective-permute-start.14 = (bf16[512,512]{1,0:T(8,128)(2,1)}, bf16[512,512]{1,0:T(8,128)(2,1)}, u32[]{:S(2)}, u32[]{:S(2)}) collective-permute-start(bf16[512,512]{1,0:T(8,128)(2,1)} %collective-permute-done.12.refs_4_), channel_id=1, source_target_pairs={{4,6},{5,7},{12,14},{13,15},{20,22},{21,23},{28,30},{29,31}} | collective-permute-start | bytes 1572872 | tf_op jit(solution)/shard_map/ppermute | solution.py:475
  54.6 0.7 compare_reduce_fusion
  56.5 5.8 %shard_map.71.refs_12_ = f32[1024,512]{1,0:T(8,128)S(1)} custom-call(s32[2,8]{1,0:T(2,128)S(1)} %bitcast.9, bf16[1,1024,2048]{2,1,0:T(8,128)(2,1)} %g_local.9, bf16[512,512]{1,0:T(8,128)(2,1)} %copy-done.3, bf16[512,512]{1,0:T(8,128)(2,1)} %copy-done.4, bf16[512,512]{1,0:T(8,128)(2,1)} %copy-done.5, bf16[512,512]{1,0:T(8,128)(2,1)} %copy-done.6, ...), custom_call_target="tpu_custom_call" | custom-call | tf_op jit(solution)/shard_map/pallas_call | solution.py:261
  62.3 2.8 %shard_map.72.refs_14_ = f32[1024,512]{1,0:T(8,128)S(1)} custom-call(s32[2,8]{1,0:T(2,128)S(1)} %bitcast.10, bf16[1,1024,2048]{2,1,0:T(8,128)(2,1)} %g_local.9, bf16[512,512]{1,0:T(8,128)(2,1)} %copy-done.3, bf16[512,512]{1,0:T(8,128)(2,1)} %copy-done.4, bf16[512,512]{1,0:T(8,128)(2,1)} %copy-done.5, ...), custom_call_target="tpu_custom_call", output_to_operand_aliasing={{}: (14, {})} | custom-call | tf_op jit(solution)/shard_map/pallas_call | solution.py:261
  65.2 1.3 %collective-permute-start.15 = (bf16[512,512]{1,0:T(8,128)(2,1)}, bf16[512,512]{1,0:T(8,128)(2,1)}, u32[]{:S(2)}, u32[]{:S(2)}) collective-permute-start(bf16[512,512]{1,0:T(8,128)(2,1)} %collective-permute-done.13.refs_5_), channel_id=1, source_target_pairs={{2,0},{3,1},{10,8},{11,9},{18,16},{19,17},{26,24},{27,25}} | collective-permute-start | bytes 1572872 | tf_op jit(solution)/shard_map/ppermute | solution.py:476
  66.5 3.3 %inner.1 = bf16[512,512]{1,0:T(8,128)(2,1)} custom-call(s32[2,8]{1,0:T(2,128)S(1)} %bitcast.11, bf16[1,1024,2048]{2,1,0:T(8,128)(2,1)} %g_local.9, bf16[1024,512]{1,0:T(8,128)(2,1)} %copy-done.2, bf16[1,1024,512]{2,1,0:T(8,128)(2,1)S(1)} %copy-done), custom_call_target="tpu_custom_call" | custom-call | tf_op jit(solution)/shard_map/inner/pallas_call | solution.py:301
  69.8 6.2 %collective-permute-start.16 = (bf16[512,512]{1,0:T(8,128)(2,1)}, bf16[512,512]{1,0:T(8,128)(2,1)}, u32[]{:S(2)}, u32[]{:S(2)}) collective-permute-start(bf16[512,512]{1,0:T(8,128)(2,1)} %inner.1), channel_id=1, source_target_pairs={{0,2},{6,4},{1,3},{7,5},{8,10},{14,12},{9,11},{15,13},{16,18},{22,... | collective-permute-start | bytes 1572872 | tf_op jit(solution)/shard_map/ppermute | solution.py:484
  76.0 1.1 conditional.1
  76.0 1.1 broadcast.7
  77.0 0.7 collective-permute-start.3
  77.7 1.3 %collective-permute-start.6 = (bf16[512,512]{1,0:T(8,128)(2,1)}, bf16[512,512]{1,0:T(8,128)(2,1)S(1)}, u32[]{:S(2)}, u32[]{:S(2)}) collective-permute-start(bf16[512,512]{1,0:T(8,128)(2,1)} %collective-permute-done.5.refs_9_.refs_11_), channel_id=1, source_target_pairs={{2,0},{3,1},{10,8},{11,9},{18,16},{19,17},{26,24},{27,25}} | collective-permute-start | bytes 1572872 | tf_op jit(solution)/shard_map/ppermute | solution.py:476
  79.7 1.0 shard_map.73.refs_16_
  80.7 3.6 %collective-permute-done.16.refs_19_ = bf16[512,512]{1,0:T(8,128)(2,1)} collective-permute-done((bf16[512,512]{1,0:T(8,128)(2,1)}, bf16[512,512]{1,0:T(8,128)(2,1)}, u32[]{:S(2)}, u32[]{:S(2)}) %collective-permute-start.16) | collective-permute-done | bytes 524320 | tf_op jit(solution)/shard_map/ppermute | solution.py:484
  84.3 2.7 %late_diag.1 = (f32[256,512]{1,0:T(8,128)S(1)}, bf16[256,512]{1,0:T(8,128)(2,1)S(1)}, f32[1024,512]{1,0:T(8,128)S(1)}) custom-call(s32[2,8]{1,0:T(2,128)S(1)} %bitcast.14, f32[1]{0:T(128)S(6)} %copy.13.weight, bf16[1,1024,2048]{2,1,0:T(8,128)(2,1)} %g_local.9, bf16[512,512]{1,0:T(8,128)(2,1)} %copy-done.3, bf16[512,512]{1,0:T(8,128)(2,1)} %copy-done.4, ...), custom_call_target="tpu_custom_call" | custom-call | tf_op jit(solution)/shard_map/late_diag/pallas_call | solution.py:367
  87.0 3.8 %collective-permute-done.6.refs_1_ = bf16[512,512]{1,0:T(8,128)(2,1)S(1)} collective-permute-done((bf16[512,512]{1,0:T(8,128)(2,1)}, bf16[512,512]{1,0:T(8,128)(2,1)S(1)}, u32[]{:S(2)}, u32[]{:S(2)}) %collective-permute-start.6) | collective-permute-done | bytes 524320 | tf_op jit(solution)/shard_map/ppermute | solution.py:476
  90.8 0.8 copy-done.8
  91.6 2.9 %late_off.1 = (f32[512,512]{1,0:T(8,128)S(1)}, bf16[512,512]{1,0:T(8,128)(2,1)S(1)}) custom-call(s32[2,8]{1,0:T(2,128)S(1)} %bitcast.15, f32[1]{0:T(128)S(6)} %copy.13.weight, bf16[1,1024,2048]{2,1,0:T(8,128)(2,1)} %g_local.9, bf16[512,512]{1,0:T(8,128)(2,1)} %copy-done.7, bf16[512,512]{1,0:T(8,128)(2,1)} %copy-done.8, bf16[1024,512]{1,0:T(8,128)(2,1)} %copy-done.2, ...), custom_call_target="tpu_custom_call" | custom-call | tf_op jit(solution)/shard_map/late_off/pallas_call | solution.py:405
  94.5 0.1 collective-permute-start.17
  94.6 0.5 collective-permute-start.19
  95.1 1.4 %collective-permute-done.17.refs_0_ = bf16[512,512]{1,0:T(8,128)(2,1)S(1)} collective-permute-done((bf16[512,512]{1,0:T(8,128)(2,1)S(1)}, bf16[512,512]{1,0:T(8,128)(2,1)S(1)}, u32[]{:S(2)}, u32[]{:S(2)}) %collective-permute-start.17) | collective-permute-done | bytes 524320 | tf_op jit(solution)/shard_map/ppermute | solution.py:517
  96.5 0.1 shard_map.74
  96.6 1.6 %collective-permute-start.18 = (bf16[256,512]{1,0:T(8,128)(2,1)S(1)}, bf16[256,512]{1,0:T(8,128)(2,1)S(1)}, u32[]{:S(2)}, u32[]{:S(2)}) collective-permute-start(bf16[256,512]{1,0:T(8,128)(2,1)S(1)} %get-tuple-element.36), channel_id=1, source_target_pairs={{0,16},{8,24},{16,0},{24,8},{1,17},{9,25},{17,1},{25,9},{2,18},{10... | collective-permute-start | bytes 786440 | tf_op jit(solution)/shard_map/ppermute | solution.py:517
  98.2 0.6 collective-permute-start.20
  98.8 9.0 %collective-permute-done.20.refs_0_ = bf16[128,512]{1,0:T(8,128)(2,1)S(1)} collective-permute-done((bf16[128,512]{1,0:T(8,128)(2,1)S(1)}, bf16[128,512]{1,0:T(8,128)(2,1)S(1)}, u32[]{:S(2)}, u32[]{:S(2)}) %collective-permute-start.20) | collective-permute-done | bytes 131104 | tf_op jit(solution)/shard_map/ppermute | solution.py:517
  107.9 0.1 collective-permute-start.21
  107.9 1.0 collective-permute-start.22
  108.9 3.4 %collective-permute-start.23 = (bf16[32,512]{1,0:T(8,128)(2,1)S(1)}, bf16[32,512]{1,0:T(8,128)(2,1)S(1)}, u32[]{:S(2)}, u32[]{:S(2)}) collective-permute-start(bf16[32,512]{1,0:T(8,128)(2,1)S(1)} %get-tuple-element.44), channel_id=1, source_target_pairs={{0,6},{2,4},{4,2},{6,0},{1,7},{3,5},{5,3},{7,1},{8,14},{10,12},{12... | collective-permute-start | bytes 98312 | tf_op jit(solution)/shard_map/ppermute | solution.py:517
  112.3 0.6 collective-permute-done.22.refs_4_
  112.9 1.7 %collective-permute-done.23.refs_5_ = bf16[32,512]{1,0:T(8,128)(2,1)S(1)} collective-permute-done((bf16[32,512]{1,0:T(8,128)(2,1)S(1)}, bf16[32,512]{1,0:T(8,128)(2,1)S(1)}, u32[]{:S(2)}, u32[]{:S(2)}) %collective-permute-start.23) | collective-permute-done | bytes 32800 | tf_op jit(solution)/shard_map/ppermute | solution.py:517
  114.7 0.9 last_sums.1
  (35 shorter events, 0.2 us)
Async XLA Ops:
  0.6 5.3 %copy-start = (bf16[1,1024,512]{2,1,0:T(8,128)(2,1)S(1)}, bf16[1,1024,512]{2,1,0:T(8,128)(2,1)}, u32[]{:S(2)}) copy-start(bf16[1,1024,512]{2,1,0:T(8,128)(2,1)} %refs_17_.1) | copy-start | bytes 3145732
  2.8 12.8 %copy-start.9 = (s32[8,2]{0,1:T(2,128)S(1)}, s32[8,2]{0,1:T(2,128)}, u32[]{:S(2)}) copy-start(s32[8,2]{0,1:T(2,128)} %param.11) | copy-start | bytes 196
  2.8 37.7 %collective-permute-start.7 = (bf16[1024,512]{1,0:T(8,128)(2,1)S(1)}, bf16[1024,512]{1,0:T(8,128)(2,1)S(1)}, u32[]{:S(2)}, u32[]{:S(2)}) collective-permute-start(bf16[1024,512]{1,0:T(8,128)(2,1)S(1)} %shard_map.68), channel_id=1, source_target_pairs={{0,1},{1,0},{2,3},{3,2},{4,5},{5,4},{6,7},{7,6},{8,9},{9,8},{10,11... | collective-permute-start | bytes 3145736 | tf_op jit(solution)/shard_map/ppermute | solution.py:469
  6.0 12.3 %copy-start.3 = (bf16[512,512]{1,0:T(8,128)(2,1)}, bf16[512,512]{1,0:T(8,128)(2,1)S(1)}, u32[]{:S(2)}) copy-start(bf16[512,512]{1,0:T(8,128)(2,1)S(1)} %get-tuple-element.47.refs_0_) | copy-start | bytes 1572868
  6.0 12.3 %copy-start.4 = (bf16[512,512]{1,0:T(8,128)(2,1)}, bf16[512,512]{1,0:T(8,128)(2,1)S(1)}, u32[]{:S(2)}) copy-start(bf16[512,512]{1,0:T(8,128)(2,1)S(1)} %get-tuple-element.48.refs_1_) | copy-start | bytes 1572868
  6.0 15.8 %collective-permute-start.1 = (bf16[512,512]{1,0:T(8,128)(2,1)S(1)}, bf16[512,512]{1,0:T(8,128)(2,1)}, u32[]{:S(2)}, u32[]{:S(2)}) collective-permute-start(bf16[512,512]{1,0:T(8,128)(2,1)S(1)} %get-tuple-element.48.refs_1_), channel_id=1, source_target_pairs={{0,2},{2,4},{4,6},{1,3},{3,5},{5,7},{8,10},{10,12},{12,14},{9,11},... | collective-permute-start | bytes 1572872 | tf_op jit(solution)/shard_map/ppermute | solution.py:475
  10.3 21.3 %collective-permute-start.10 = (bf16[512,512]{1,0:T(8,128)(2,1)S(1)}, bf16[512,512]{1,0:T(8,128)(2,1)S(1)}, u32[]{:S(2)}, u32[]{:S(2)}) collective-permute-start(bf16[512,512]{1,0:T(8,128)(2,1)S(1)} %get-tuple-element.47.refs_0_), channel_id=1, source_target_pairs={{0,2},{2,4},{4,6},{1,3},{3,5},{5,7},{8,10},{10,12},{12,14},{9,11},... | collective-permute-start | bytes 1572872 | tf_op jit(solution)/shard_map/ppermute | solution.py:475
  13.0 20.0 %collective-permute-start.11 = (bf16[512,512]{1,0:T(8,128)(2,1)S(1)}, bf16[512,512]{1,0:T(8,128)(2,1)S(1)}, u32[]{:S(2)}, u32[]{:S(2)}) collective-permute-start(bf16[512,512]{1,0:T(8,128)(2,1)S(1)} %get-tuple-element.47.refs_0_), channel_id=1, source_target_pairs={{2,0},{4,2},{6,4},{3,1},{5,3},{7,5},{10,8},{12,10},{14,12},{11,9},... | collective-permute-start | bytes 1572872 | tf_op jit(solution)/shard_map/ppermute | solution.py:476
  14.3 24.8 %collective-permute-start.4 = (bf16[512,512]{1,0:T(8,128)(2,1)S(1)}, bf16[512,512]{1,0:T(8,128)(2,1)}, u32[]{:S(2)}, u32[]{:S(2)}) collective-permute-start(bf16[512,512]{1,0:T(8,128)(2,1)S(1)} %get-tuple-element.48.refs_1_), channel_id=1, source_target_pairs={{2,0},{4,2},{6,4},{3,1},{5,3},{7,5},{10,8},{12,10},{14,12},{11,9},... | collective-permute-start | bytes 1572872 | tf_op jit(solution)/shard_map/ppermute | solution.py:476
  21.8 40.6 %collective-permute-start.8 = (bf16[1024,512]{1,0:T(8,128)(2,1)}, bf16[1024,512]{1,0:T(8,128)(2,1)}, u32[]{:S(2)}, u32[]{:S(2)}) collective-permute-start(bf16[1024,512]{1,0:T(8,128)(2,1)} %shard_map.69), channel_id=1, source_target_pairs={{0,1},{1,0},{2,3},{3,2},{4,5},{5,4},{6,7},{7,6},{8,9},{9,8},{10,11... | collective-permute-start | bytes 3145736 | tf_op jit(solution)/shard_map/ppermute | solution.py:469
  31.6 12.9 %copy-start.5 = (bf16[512,512]{1,0:T(8,128)(2,1)}, bf16[512,512]{1,0:T(8,128)(2,1)S(1)}, u32[]{:S(2)}) copy-start(bf16[512,512]{1,0:T(8,128)(2,1)S(1)} %collective-permute-done.10.refs_2_) | copy-start | bytes 1572868
  31.6 12.9 %collective-permute-start.12 = (bf16[512,512]{1,0:T(8,128)(2,1)S(1)}, bf16[512,512]{1,0:T(8,128)(2,1)}, u32[]{:S(2)}, u32[]{:S(2)}) collective-permute-start(bf16[512,512]{1,0:T(8,128)(2,1)S(1)} %collective-permute-done.10.refs_2_), channel_id=1, source_target_pairs={{2,4},{4,6},{3,5},{5,7},{10,12},{12,14},{11,13},{13,15},{18,20},{2... | collective-permute-start | bytes 1572872 | tf_op jit(solution)/shard_map/ppermute | solution.py:475
  33.0 11.4 %copy-start.6 = (bf16[512,512]{1,0:T(8,128)(2,1)}, bf16[512,512]{1,0:T(8,128)(2,1)S(1)}, u32[]{:S(2)}) copy-start(bf16[512,512]{1,0:T(8,128)(2,1)S(1)} %collective-permute-done.11.refs_3_) | copy-start | bytes 1572868
  33.0 20.1 %collective-permute-start.13 = (bf16[512,512]{1,0:T(8,128)(2,1)S(1)}, bf16[512,512]{1,0:T(8,128)(2,1)}, u32[]{:S(2)}, u32[]{:S(2)}) collective-permute-start(bf16[512,512]{1,0:T(8,128)(2,1)S(1)} %collective-permute-done.11.refs_3_), channel_id=1, source_target_pairs={{2,0},{4,2},{3,1},{5,3},{10,8},{12,10},{11,9},{13,11},{18,16},{20,... | collective-permute-start | bytes 1572872 | tf_op jit(solution)/shard_map/ppermute | solution.py:476
  39.0 23.3 %collective-permute-start.2 = (bf16[512,512]{1,0:T(8,128)(2,1)}, bf16[512,512]{1,0:T(8,128)(2,1)}, u32[]{:S(2)}, u32[]{:S(2)}) collective-permute-start(bf16[512,512]{1,0:T(8,128)(2,1)} %collective-permute-done.1.refs_4_.refs_6_.refs_8_), channel_id=1, source_target_pairs={{2,4},{4,6},{3,5},{5,7},{10,12},{12,14},{11,13},{13,15},{18,20},{2... | collective-permute-start | bytes 1572872 | tf_op jit(solution)/shard_map/ppermute | solution.py:475
  40.5 4.0 %copy-start.2 = (bf16[1024,512]{1,0:T(8,128)(2,1)}, bf16[1024,512]{1,0:T(8,128)(2,1)S(1)}, u32[]{:S(2)}) copy-start(bf16[1024,512]{1,0:T(8,128)(2,1)S(1)} %collective-permute-done.7.refs_6_.refs_10_.refs_12_.slot.refs_2_) | copy-start | bytes 3145732
  40.5 21.8 %collective-permute-start.5 = (bf16[512,512]{1,0:T(8,128)(2,1)}, bf16[512,512]{1,0:T(8,128)(2,1)}, u32[]{:S(2)}, u32[]{:S(2)}) collective-permute-start(bf16[512,512]{1,0:T(8,128)(2,1)} %collective-permute-done.4.refs_5_.refs_7_.refs_9_), channel_id=1, source_target_pairs={{2,0},{4,2},{3,1},{5,3},{10,8},{12,10},{11,9},{13,11},{18,16},{20,... | collective-permute-start | bytes 1572872 | tf_op jit(solution)/shard_map/ppermute | solution.py:476
  44.5 36.2 %collective-permute-start.9 = (bf16[1024,512]{1,0:T(8,128)(2,1)}, bf16[1024,512]{1,0:T(8,128)(2,1)}, u32[]{:S(2)}, u32[]{:S(2)}) collective-permute-start(bf16[1024,512]{1,0:T(8,128)(2,1)} %shard_map.70), channel_id=1, source_target_pairs={{0,1},{1,0},{2,3},{3,2},{4,5},{5,4},{6,7},{7,6},{8,9},{9,8},{10,11... | collective-permute-start | bytes 3145736 | tf_op jit(solution)/shard_map/ppermute | solution.py:469
  53.1 24.6 %collective-permute-start.14 = (bf16[512,512]{1,0:T(8,128)(2,1)}, bf16[512,512]{1,0:T(8,128)(2,1)}, u32[]{:S(2)}, u32[]{:S(2)}) collective-permute-start(bf16[512,512]{1,0:T(8,128)(2,1)} %collective-permute-done.12.refs_4_), channel_id=1, source_target_pairs={{4,6},{5,7},{12,14},{13,15},{20,22},{21,23},{28,30},{29,31}} | collective-permute-start | bytes 1572872 | tf_op jit(solution)/shard_map/ppermute | solution.py:475
  65.2 14.6 %collective-permute-start.15 = (bf16[512,512]{1,0:T(8,128)(2,1)}, bf16[512,512]{1,0:T(8,128)(2,1)}, u32[]{:S(2)}, u32[]{:S(2)}) collective-permute-start(bf16[512,512]{1,0:T(8,128)(2,1)} %collective-permute-done.13.refs_5_), channel_id=1, source_target_pairs={{2,0},{3,1},{10,8},{11,9},{18,16},{19,17},{26,24},{27,25}} | collective-permute-start | bytes 1572872 | tf_op jit(solution)/shard_map/ppermute | solution.py:476
  69.8 14.5 %collective-permute-start.16 = (bf16[512,512]{1,0:T(8,128)(2,1)}, bf16[512,512]{1,0:T(8,128)(2,1)}, u32[]{:S(2)}, u32[]{:S(2)}) collective-permute-start(bf16[512,512]{1,0:T(8,128)(2,1)} %inner.1), channel_id=1, source_target_pairs={{0,2},{6,4},{1,3},{7,5},{8,10},{14,12},{9,11},{15,13},{16,18},{22,... | collective-permute-start | bytes 1572872 | tf_op jit(solution)/shard_map/ppermute | solution.py:484
  77.0 9.9 %collective-permute-start.3 = (bf16[512,512]{1,0:T(8,128)(2,1)}, bf16[512,512]{1,0:T(8,128)(2,1)S(1)}, u32[]{:S(2)}, u32[]{:S(2)}) collective-permute-start(bf16[512,512]{1,0:T(8,128)(2,1)} %collective-permute-done.2.refs_8_.refs_10_), channel_id=1, source_target_pairs={{4,6},{5,7},{12,14},{13,15},{20,22},{21,23},{28,30},{29,31}} | collective-permute-start | bytes 1572872 | tf_op jit(solution)/shard_map/ppermute | solution.py:475
  77.7 13.1 %collective-permute-start.6 = (bf16[512,512]{1,0:T(8,128)(2,1)}, bf16[512,512]{1,0:T(8,128)(2,1)S(1)}, u32[]{:S(2)}, u32[]{:S(2)}) collective-permute-start(bf16[512,512]{1,0:T(8,128)(2,1)} %collective-permute-done.5.refs_9_.refs_11_), channel_id=1, source_target_pairs={{2,0},{3,1},{10,8},{11,9},{18,16},{19,17},{26,24},{27,25}} | collective-permute-start | bytes 1572872 | tf_op jit(solution)/shard_map/ppermute | solution.py:476
  79.7 4.6 %copy-start.1 = (bf16[1,128,512]{2,1,0:T(8,128)(2,1)S(1)}, bf16[1,128,512]{2,1,0:T(8,128)(2,1)}, u32[]{:S(2)}) copy-start(bf16[1,128,512]{2,1,0:T(8,128)(2,1)} %refs_18_.1) | copy-start | bytes 393220
  87.0 3.8 %copy-start.7 = (bf16[512,512]{1,0:T(8,128)(2,1)}, bf16[512,512]{1,0:T(8,128)(2,1)S(1)}, u32[]{:S(2)}) copy-start(bf16[512,512]{1,0:T(8,128)(2,1)S(1)} %collective-permute-done.3.refs_0_) | copy-start | bytes 1572868
  90.8 0.8 copy-start.8
  94.5 2.0 %collective-permute-start.17 = (bf16[512,512]{1,0:T(8,128)(2,1)S(1)}, bf16[512,512]{1,0:T(8,128)(2,1)S(1)}, u32[]{:S(2)}, u32[]{:S(2)}) collective-permute-start(bf16[512,512]{1,0:T(8,128)(2,1)S(1)} %get-tuple-element.34), channel_id=1, source_target_pairs={{0,8},{8,0},{16,24},{24,16},{1,9},{9,1},{17,25},{25,17},{2,10},{10... | collective-permute-start | bytes 1572872 | tf_op jit(solution)/shard_map/ppermute | solution.py:517
  94.6 3.5 %collective-permute-start.19 = (bf16[256,512]{1,0:T(8,128)(2,1)S(1)}, bf16[256,512]{1,0:T(8,128)(2,1)S(1)}, u32[]{:S(2)}, u32[]{:S(2)}) collective-permute-start(bf16[256,512]{1,0:T(8,128)(2,1)S(1)} %get-tuple-element.38), channel_id=1, source_target_pairs={{0,8},{8,0},{16,24},{24,16},{1,9},{9,1},{17,25},{25,17},{2,10},{10... | collective-permute-start | bytes 786440 | tf_op jit(solution)/shard_map/ppermute | solution.py:517
  96.6 18.1 %collective-permute-start.18 = (bf16[256,512]{1,0:T(8,128)(2,1)S(1)}, bf16[256,512]{1,0:T(8,128)(2,1)S(1)}, u32[]{:S(2)}, u32[]{:S(2)}) collective-permute-start(bf16[256,512]{1,0:T(8,128)(2,1)S(1)} %get-tuple-element.36), channel_id=1, source_target_pairs={{0,16},{8,24},{16,0},{24,8},{1,17},{9,25},{17,1},{25,9},{2,18},{10... | collective-permute-start | bytes 786440 | tf_op jit(solution)/shard_map/ppermute | solution.py:517
  98.2 9.6 %collective-permute-start.20 = (bf16[128,512]{1,0:T(8,128)(2,1)S(1)}, bf16[128,512]{1,0:T(8,128)(2,1)S(1)}, u32[]{:S(2)}, u32[]{:S(2)}) collective-permute-start(bf16[128,512]{1,0:T(8,128)(2,1)S(1)} %get-tuple-element.40), channel_id=1, source_target_pairs={{0,16},{8,24},{16,0},{24,8},{1,17},{9,25},{17,1},{25,9},{2,18},{10... | collective-permute-start | bytes 393224 | tf_op jit(solution)/shard_map/ppermute | solution.py:517
  107.9 4.5 %collective-permute-start.21 = (bf16[32,512]{1,0:T(8,128)(2,1)S(1)}, bf16[32,512]{1,0:T(8,128)(2,1)S(1)}, u32[]{:S(2)}, u32[]{:S(2)}) collective-permute-start(bf16[32,512]{1,0:T(8,128)(2,1)S(1)} %get-tuple-element.42), channel_id=1, source_target_pairs={{0,2},{2,0},{4,6},{6,4},{1,3},{3,1},{5,7},{7,5},{8,10},{10,8},{12,... | collective-permute-start | bytes 98312 | tf_op jit(solution)/shard_map/ppermute | solution.py:517
  107.9 5.0 %collective-permute-start.22 = (bf16[32,512]{1,0:T(8,128)(2,1)S(1)}, bf16[32,512]{1,0:T(8,128)(2,1)S(1)}, u32[]{:S(2)}, u32[]{:S(2)}) collective-permute-start(bf16[32,512]{1,0:T(8,128)(2,1)S(1)} %get-tuple-element.43), channel_id=1, source_target_pairs={{0,4},{2,6},{4,0},{6,2},{1,5},{3,7},{5,1},{7,3},{8,12},{10,14},{12... | collective-permute-start | bytes 98312 | tf_op jit(solution)/shard_map/ppermute | solution.py:517
  108.9 5.7 %collective-permute-start.23 = (bf16[32,512]{1,0:T(8,128)(2,1)S(1)}, bf16[32,512]{1,0:T(8,128)(2,1)S(1)}, u32[]{:S(2)}, u32[]{:S(2)}) collective-permute-start(bf16[32,512]{1,0:T(8,128)(2,1)S(1)} %get-tuple-element.44), channel_id=1, source_target_pairs={{0,6},{2,4},{4,2},{6,0},{1,7},{3,5},{5,3},{7,1},{8,14},{10,12},{12... | collective-permute-start | bytes 98312 | tf_op jit(solution)/shard_map/ppermute | solution.py:517
